TPU v7x, 256 devices: a whole 4x4x8 slice. The times are simulated.
256 devices in a mesh: seq: 32 (over x, z), ch: 8 (over y, core).
Axes of the slice: x: 4, y: 4, z: 8, core: 2. Of those that a mesh axis runs over, the one named last changes fastest.
Arguments:
- queries_in: bfloat16 [8192, 8192], P('seq', 'ch'), may hold values from -160 to 160
- keys_in: bfloat16 [8192, 8192], P('seq', 'ch'), may hold values from -8 to 8
- values_in: bfloat16 [8192, 8192], P('seq', 'ch'), may hold values from -6 to 6
- gate_branch: bfloat16 [8192, 8192], P('seq', 'ch'), may hold values from -6 to 6
- key_branch: bfloat16 [8192, 8192], P('seq', 'ch'), may hold values from -6 to 6
- mr_filter: bfloat16 [128, 8192], P(None, 'ch'), may hold values from -3 to 3
- out_grad: bfloat16 [8192, 8192], P('seq', 'ch'), may hold values from -40 to 40
- doc_ids: int32 [8192], replicated, may hold values from 0 to 63, never falling along the last dimension, each value on 1 to 1024 neighbouring positions
Outputs:
- query_grad: bfloat16 [8192, 8192], P('seq', 'ch')
- key_grad: bfloat16 [8192, 8192], P('seq', 'ch')
- value_grad: bfloat16 [8192, 8192], P('seq', 'ch')
- gate_grad: bfloat16 [8192, 8192], P('seq', 'ch')
- branch_grad: bfloat16 [8192, 8192], P('seq', 'ch')
- filter_step: float32 [128, 8192], P('seq', 'ch')
Inputs may be any that keep to these rules, and one draw needn't show every extreme that they name: `doc_ids`: document numbers never fall along the sequence; each document has 1 to 1024 tokens and one has exactly 1024.
All inputs are finite; a program needn't handle non-finite values.
Results may differ from a plain program's by a relative error of at most 0.009.
Values may be sent and summed in bfloat16 or wider, within the bound.
No kernel may reach another device: no remote copies, remote signals or barrier semaphores. Data moves between devices by JAX's collectives and lax.ppermute only.
A program may use at most 128 MiB of HBM per device.

v0:
```python
import jax
import jax.numpy as jnp
from jax import lax
from jax.sharding import PartitionSpec as P

HD = 128
TAPS = 128
SPAN = 4


def from_behind(array, axis, by):
    size = lax.axis_size(axis)
    pairs = [(i, i + by) for i in range(size) if 0 <= i + by < size]
    return lax.ppermute(array, axis, pairs)


def causal_conv(extended, weights_in):
    channels = extended.shape[1]
    kernel = jnp.flip(weights_in, 0)[:, None, :]
    result = lax.conv_general_dilated(
        extended[None],
        kernel,
        (1,),
        "VALID",
        dimension_numbers=("NWC", "WIO", "NWC"),
        feature_group_count=channels,
        preferred_element_type=jnp.float32,
    )
    return result[0]


def anti_conv(extended, weights_in):
    channels = extended.shape[1]
    kernel = weights_in[:, None, :]
    result = lax.conv_general_dilated(
        extended[None],
        kernel,
        (1,),
        "VALID",
        dimension_numbers=("NWC", "WIO", "NWC"),
        feature_group_count=channels,
        preferred_element_type=jnp.float32,
    )
    return result[0]


def filter_corr(extended, gradient):
    channels = extended.shape[1]
    kernel = gradient[:, None, :]
    result = lax.conv_general_dilated(
        extended[None],
        kernel,
        (1,),
        "VALID",
        dimension_numbers=("NWC", "WIO", "NWC"),
        feature_group_count=channels,
        preferred_element_type=jnp.float32,
    )
    return jnp.flip(result[0], 0)


def per_device(
    queries_in, keys_in, values_in, gate_branch, key_branch, mr_filter, out_grad, doc_ids
):
    shard_len = queries_in.shape[0]
    width = queries_in.shape[1]
    heads_dev = width // HD
    window = (SPAN + 1) * shard_len
    score_scale = HD ** (-0.5)
    position = lax.axis_index("seq")
    earlier = []
    current = (keys_in, values_in)
    for offset in range(SPAN):
        current = from_behind((current[0], current[1]), "seq", 1)
        earlier.append(current)
    key_win = jnp.concatenate(
        [earlier[SPAN - 1 - index][0] for index in range(SPAN)] + [keys_in], 0
    ).reshape(window, heads_dev, HD)
    value_win = jnp.concatenate(
        [earlier[SPAN - 1 - index][1] for index in range(SPAN)] + [values_in], 0
    ).reshape(window, heads_dev, HD)
    doc_front = jnp.concatenate([jnp.full((SPAN * shard_len,), -1, jnp.int32), doc_ids], 0)
    key_doc = lax.dynamic_slice_in_dim(doc_front, position * shard_len, window, 0)
    query_doc = lax.dynamic_slice_in_dim(doc_ids, position * shard_len, shard_len, 0)
    query_pos = position * shard_len + jnp.arange(shard_len, dtype=jnp.int32)
    key_pos = (position - SPAN) * shard_len + jnp.arange(window, dtype=jnp.int32)
    allowed = (query_doc[:, None] == key_doc[None, :]) & (key_pos[None, :] <= query_pos[:, None])
    queries = queries_in.reshape(shard_len, heads_dev, HD)
    scores = (
        jnp.einsum("qhd,khd->hqk", queries, key_win, preferred_element_type=jnp.float32)
        * score_scale
    )
    scores = jnp.where(allowed[None], scores, -jnp.inf)
    row_max = jnp.max(scores, -1)
    log_total = row_max + jnp.log(jnp.sum(jnp.exp(scores - row_max[..., None]), -1))
    weights = jnp.where(allowed[None], jnp.exp(scores - log_total[..., None]), 0.0)
    probs = weights.astype(jnp.bfloat16)
    attn_out = (
        jnp.einsum("hqk,khd->qhd", probs, value_win, preferred_element_type=jnp.float32)
        .astype(jnp.bfloat16)
        .reshape(shard_len, width)
    )
    mixed = (key_branch.astype(jnp.float32) * attn_out.astype(jnp.float32)).astype(jnp.bfloat16)
    mixed_edge = from_behind(mixed[shard_len - (TAPS - 1) :], "seq", 1)
    mixed_ext = jnp.concatenate([mixed_edge, mixed], 0)
    conv_out = causal_conv(mixed_ext, mr_filter)
    gate_grad = (out_grad.astype(jnp.float32) * conv_out).astype(jnp.bfloat16)
    conv_grad = (out_grad.astype(jnp.float32) * gate_branch.astype(jnp.float32)).astype(
        jnp.bfloat16
    )
    grad_edge = from_behind(conv_grad[: TAPS - 1], "seq", -1)
    mixed_grad = anti_conv(jnp.concatenate([conv_grad, grad_edge], 0), mr_filter)
    filter_part = filter_corr(mixed_ext, conv_grad)
    branch_grad = (mixed_grad * attn_out.astype(jnp.float32)).astype(jnp.bfloat16)
    attn_grad = (mixed_grad * key_branch.astype(jnp.float32)).astype(jnp.bfloat16)
    out_grads = attn_grad.reshape(shard_len, heads_dev, HD)
    out_rows = attn_out.reshape(shard_len, heads_dev, HD)
    row_dot = jnp.einsum("qhd,qhd->hq", out_grads, out_rows, preferred_element_type=jnp.float32)
    prob_grad = jnp.einsum("qhd,khd->hqk", out_grads, value_win, preferred_element_type=jnp.float32)
    score_grad = (weights * (prob_grad - row_dot[..., None])).astype(jnp.bfloat16)
    query_grad = (
        (
            jnp.einsum("hqk,khd->qhd", score_grad, key_win, preferred_element_type=jnp.float32)
            * score_scale
        )
        .astype(jnp.bfloat16)
        .reshape(shard_len, width)
    )
    key_terms = (
        jnp.einsum("hqk,qhd->khd", score_grad, queries, preferred_element_type=jnp.float32)
        * score_scale
    ).reshape(window, width)
    value_terms = jnp.einsum(
        "hqk,qhd->khd", probs, out_grads, preferred_element_type=jnp.float32
    ).reshape(window, width)
    key_sum = key_terms[SPAN * shard_len :]
    value_sum = value_terms[SPAN * shard_len :]
    for offset in range(SPAN):
        first_row = (SPAN - 1 - offset) * shard_len
        back_key, back_value = from_behind(
            (
                key_terms[first_row : first_row + shard_len],
                value_terms[first_row : first_row + shard_len],
            ),
            "seq",
            -(offset + 1),
        )
        key_sum = key_sum + back_key
        value_sum = value_sum + back_value
    tap_rows = TAPS // lax.axis_size("seq")
    filter_grad = lax.psum(filter_part, "seq")
    filter_sq = jnp.sum(jnp.square(mr_filter.astype(jnp.float32)))
    norms = lax.psum((filter_sq, jnp.sum(filter_grad * filter_grad)), "ch")
    own_grad = lax.dynamic_slice_in_dim(filter_grad, position * tap_rows, tap_rows, 0)
    trust = jnp.sqrt(norms[0]) / jnp.sqrt(norms[1] + 1e-06)
    filter_step = trust * own_grad
    return (
        query_grad,
        key_sum.astype(jnp.bfloat16),
        value_sum.astype(jnp.bfloat16),
        gate_grad,
        branch_grad,
        filter_step,
    )


def solution(mesh):
    return jax.shard_map(
        per_device,
        mesh=mesh,
        in_specs=(
            P("seq", "ch"),
            P("seq", "ch"),
            P("seq", "ch"),
            P("seq", "ch"),
            P("seq", "ch"),
            P(None, "ch"),
            P("seq", "ch"),
            P(),
        ),
        out_specs=(
            P("seq", "ch"),
            P("seq", "ch"),
            P("seq", "ch"),
            P("seq", "ch"),
            P("seq", "ch"),
            P("seq", "ch"),
        ),
        check_vma=False,
    )
```

profile of v0, /device:TPU:1, one launch (start us, length us, event | category | flops | bytes accessed | tf_op | source)
XLA Modules:
  0.0 591.8 jit_solution(14305902823616144180)
XLA Ops:
  8.6 4.4 collective-permute-start
  14.2 3.5 collective-permute-start.5
  17.8 5.7 collective-permute-done
  23.5 4.9 collective-permute-start.1
  34.8 4.9 collective-permute-start.6
  39.7 6.3 %collective-permute-done.1 = bf16[256,1024]{0,1:T(8,128)(2,1)} collective-permute-done((bf16[256,1024]{0,1:T(8,128)(2,1)S(1)}, bf16[256,1024]{0,1:T(8,128)(2,1)}, u32[]{:S(2)}, u32[]{:S(2)}) %collective-permute-start.1) | collective-permute-done | bytes 524320 | tf_op jit(solution)/shard_map/ppermute | solution.py:14
  46.0 5.0 collective-permute-start.2
  57.2 4.2 collective-permute-start.7
  61.5 7.1 %collective-permute-done.2 = bf16[256,1024]{0,1:T(8,128)(2,1)} collective-permute-done((bf16[256,1024]{0,1:T(8,128)(2,1)}, bf16[256,1024]{0,1:T(8,128)(2,1)}, u32[]{:S(2)}, u32[]{:S(2)}) %collective-permute-start.2) | collective-permute-done | bytes 524320 | tf_op jit(solution)/shard_map/ppermute | solution.py:14
  68.6 4.1 collective-permute-start.3
  72.7 14.8 %fusion.1 = f32[1,256,1024]{2,0,1:T(1,128)} fusion(bf16[1,383,1024]{2,1,0:T(8,128)(2,1)S(1)} %maximum_bitcast_fusion, bf16[128,1,1024]{2,0,1:T(8,128)(2,1)S(1)} %bitcast.87), kind=kOutput, calls=%fused_computation.7 | convolution fusion | flops 67108864 | bytes 2095104 | tf_op jit(solution)/shard_map/conv_general_dilated | solution.py:35
  87.5 3.7 collective-permute-start.8
  93.6 6.7 %collective-permute-done.8 = bf16[256,1024]{0,1:T(8,128)(2,1)S(1)} collective-permute-done((bf16[256,1024]{0,1:T(8,128)(2,1)S(1)}, bf16[256,1024]{0,1:T(8,128)(2,1)S(1)}, u32[]{:S(2)}, u32[]{:S(2)}) %collective-permute-start.8) | collective-permute-done | bytes 524320 | tf_op jit(solution)/shard_map/ppermute | solution.py:14
  123.6 7.4 %multiply_convert_fusion = bf16[8,256,1280]{1,2,0:T(8,128)(2,1)S(1)} fusion(f32[8,256,1280]{1,2,0:T(8,128)} %copy-done, bf16[256,8,128]{0,2,1:T(8,128)(2,1)S(1)} %copy.62, bf16[1280,8,128]{0,2,1:T(8,128)(2,1)} %bitcast.84, f32[8,256]{1,0:T(8,128)S(1)} %multiply_reduce_fusion, f32[8,256]{1,0:T(8,128)S(1)} %log_add_fusion, ...), kind=kOutput, calls=%fused_computation.1 | convolution fusion | flops 684195840 | bytes 19218432 | tf_op jit(solution)/shard_map/qhd,khd->hqk/dot_general | solution.py:119
  132.7 4.2 multiply_bitcast_fusion
  136.9 4.3 convolution_bitcast_fusion
  142.2 4.3 fusion.22
  161.0 5.4 collective-permute-start.17
  166.4 4.3 fusion.21
  181.4 13.9 %fusion.4 = f32[1,128,1024]{2,0,1:T(1,128)S(1)} fusion(bf16[1,383,1024]{2,1,0:T(8,128)(2,1)S(1)} %maximum_bitcast_fusion.1, bf16[256,1,1024]{2,0,1:T(8,128)(2,1)S(1)} %bitcast.85), kind=kOutput, calls=%fused_computation.17 | convolution fusion | flops 67108864 | bytes 1832960 | tf_op jit(solution)/shard_map/conv_general_dilated | solution.py:50
  200.7 74.0 %collective-permute-done.10 = f32[256,1024]{1,0:T(8,128)} collective-permute-done((f32[256,1024]{1,0:T(8,128)}, f32[256,1024]{1,0:T(8,128)}, u32[]{:S(2)}, u32[]{:S(2)}) %collective-permute-start.10) | collective-permute-done | bytes 1048608 | tf_op jit(solution)/shard_map/ppermute | solution.py:14
  276.2 15.8 %fusion.6 = f32[1,256,1024]{2,0,1:T(1,128)} fusion(bf16[1,383,1024]{2,1,0:T(8,128)(2,1)} %copy-done.17, bf16[128,1,1024]{2,0,1:T(8,128)(2,1)S(1)} %bitcast.88), kind=kOutput, calls=%fused_computation.19 | convolution fusion | flops 67108864 | bytes 2095104 | tf_op jit(solution)/shard_map/conv_general_dilated | solution.py:20
  292.0 261.7 %all-reduce.4.cloned.1.call-done = f32[128,1024]{1,0:T(8,128)} async-done(((f32[128,1024]{1,0:T(8,128)}), f32[128,1024]{1,0:T(8,128)}) %all-reduce.4.cloned.1.call-update) | async-done | bytes 524304 | tf_op jit(solution)/shard_map/psum | solution.py:151
  557.8 17.6 %all-reduce.1 = (f32[]{:T(128)}, f32[]{:T(128)}) all-reduce(f32[]{:T(128)} %multiply_reduce_fusion.2, f32[]{:T(128)} %multiply_reduce_fusion.1), channel_id=1, replica_groups=mesh['seq'=32,'ch'=8] {'ch'}, use_global_device_ids=true, to_apply=%region_3.4 | all-reduce | flops 2 | bytes 16 | tf_op jit(solution)/shard_map/psum | solution.py:153
  (138 shorter events, 87.3 us)
Async XLA Ops:
  7.2 546.5 %all-reduce.4.cloned.1.call-start = ((), (), s32[]{:S(2)}) async-start(), calls=%async_computation | async-start | bytes 1048576 | tf_op jit(solution)/shard_map/psum | solution.py:151
  8.6 15.0 %collective-permute-start = (bf16[256,1024]{0,1:T(8,128)(2,1)S(1)}, bf16[256,1024]{0,1:T(8,128)(2,1)S(1)}, u32[]{:S(2)}, u32[]{:S(2)}) collective-permute-start(bf16[256,1024]{0,1:T(8,128)(2,1)S(1)} %copy.42), channel_id=1, source_target_pairs={{0,8},{8,16},{16,24},{24,32},{32,40},{40,48},{48,56},{56,64},{64,7... | collective-permute-start | bytes 1572872 | tf_op jit(solution)/shard_map/ppermute | solution.py:14
  14.2 20.5 %collective-permute-start.5 = (bf16[256,1024]{0,1:T(8,128)(2,1)S(1)}, bf16[256,1024]{0,1:T(8,128)(2,1)S(1)}, u32[]{:S(2)}, u32[]{:S(2)}) collective-permute-start(bf16[256,1024]{0,1:T(8,128)(2,1)S(1)} %copy.48), channel_id=1, source_target_pairs={{0,8},{8,16},{16,24},{24,32},{32,40},{40,48},{48,56},{56,64},{64,7... | collective-permute-start | bytes 1572872 | tf_op jit(solution)/shard_map/ppermute | solution.py:14
  23.5 22.5 %collective-permute-start.1 = (bf16[256,1024]{0,1:T(8,128)(2,1)S(1)}, bf16[256,1024]{0,1:T(8,128)(2,1)}, u32[]{:S(2)}, u32[]{:S(2)}) collective-permute-start(bf16[256,1024]{0,1:T(8,128)(2,1)S(1)} %collective-permute-done), channel_id=1, source_target_pairs={{0,8},{8,16},{16,24},{24,32},{32,40},{40,48},{48,56},{56,64},{64,7... | collective-permute-start | bytes 1572872 | tf_op jit(solution)/shard_map/ppermute | solution.py:14
  29.8 57.7 %copy-start.7 = (bf16[256,1024]{1,0:T(8,128)(2,1)}, bf16[256,1024]{1,0:T(8,128)(2,1)S(1)}, u32[]{:S(2)}) copy-start(bf16[256,1024]{1,0:T(8,128)(2,1)S(1)} %fusion.8) | copy-start | bytes 1572868
  29.9 25.7 %collective-permute-start.4 = (bf16[127,1024]{1,0:T(8,128)(2,1)S(1)}, bf16[127,1024]{1,0:T(8,128)(2,1)}, u32[]{:S(2)}, u32[]{:S(2)}) collective-permute-start(bf16[127,1024]{1,0:T(8,128)(2,1)S(1)} %slice.88), channel_id=1, source_target_pairs={{8,0},{16,8},{24,16},{32,24},{40,32},{48,40},{56,48},{64,56},{72,6... | collective-permute-start | bytes 780296 | tf_op jit(solution)/shard_map/ppermute | solution.py:14
  34.8 52.8 %copy-start.19 = (bf16[256,1024]{0,1:T(8,128)(2,1)}, bf16[256,1024]{0,1:T(8,128)(2,1)S(1)}, u32[]{:S(2)}) copy-start(bf16[256,1024]{0,1:T(8,128)(2,1)S(1)} %collective-permute-done.5) | copy-start | bytes 1572868
  34.8 22.5 %collective-permute-start.6 = (bf16[256,1024]{0,1:T(8,128)(2,1)S(1)}, bf16[256,1024]{0,1:T(8,128)(2,1)}, u32[]{:S(2)}, u32[]{:S(2)}) collective-permute-start(bf16[256,1024]{0,1:T(8,128)(2,1)S(1)} %collective-permute-done.5), channel_id=1, source_target_pairs={{0,8},{8,16},{16,24},{24,32},{32,40},{40,48},{48,56},{56,64},{64,7... | collective-permute-start | bytes 1572872 | tf_op jit(solution)/shard_map/ppermute | solution.py:14
  46.0 22.6 %collective-permute-start.2 = (bf16[256,1024]{0,1:T(8,128)(2,1)}, bf16[256,1024]{0,1:T(8,128)(2,1)}, u32[]{:S(2)}, u32[]{:S(2)}) collective-permute-start(bf16[256,1024]{0,1:T(8,128)(2,1)} %collective-permute-done.1), channel_id=1, source_target_pairs={{0,8},{8,16},{16,24},{24,32},{32,40},{40,48},{48,56},{56,64},{64,7... | collective-permute-start | bytes 1572872 | tf_op jit(solution)/shard_map/ppermute | solution.py:14
  57.2 30.3 %collective-permute-start.7 = (bf16[256,1024]{0,1:T(8,128)(2,1)}, bf16[256,1024]{0,1:T(8,128)(2,1)S(1)}, u32[]{:S(2)}, u32[]{:S(2)}) collective-permute-start(bf16[256,1024]{0,1:T(8,128)(2,1)} %collective-permute-done.6), channel_id=1, source_target_pairs={{0,8},{8,16},{16,24},{24,32},{32,40},{40,48},{48,56},{56,64},{64,7... | collective-permute-start | bytes 1572872 | tf_op jit(solution)/shard_map/ppermute | solution.py:14
  68.6 22.7 %collective-permute-start.3 = (bf16[256,1024]{0,1:T(8,128)(2,1)}, bf16[256,1024]{0,1:T(8,128)(2,1)S(1)}, u32[]{:S(2)}, u32[]{:S(2)}) collective-permute-start(bf16[256,1024]{0,1:T(8,128)(2,1)} %collective-permute-done.2), channel_id=1, source_target_pairs={{0,8},{8,16},{16,24},{24,32},{32,40},{40,48},{48,56},{56,64},{64,7... | collective-permute-start | bytes 1572872 | tf_op jit(solution)/shard_map/ppermute | solution.py:14
  87.5 12.8 %collective-permute-start.8 = (bf16[256,1024]{0,1:T(8,128)(2,1)S(1)}, bf16[256,1024]{0,1:T(8,128)(2,1)S(1)}, u32[]{:S(2)}, u32[]{:S(2)}) collective-permute-start(bf16[256,1024]{0,1:T(8,128)(2,1)S(1)} %collective-permute-done.7), channel_id=1, source_target_pairs={{0,8},{8,16},{16,24},{24,32},{32,40},{40,48},{48,56},{56,64},{64,7... | collective-permute-start | bytes 1572872 | tf_op jit(solution)/shard_map/ppermute | solution.py:14
  149.1 49.0 %collective-permute-start.12 = (f32[256,1024]{1,0:T(8,128)}, f32[256,1024]{1,0:T(8,128)}, u32[]{:S(2)}, u32[]{:S(2)}) collective-permute-start(f32[256,1024]{1,0:T(8,128)} %copy.61), channel_id=1, source_target_pairs={{32,0},{40,8},{48,16},{56,24},{64,32},{72,40},{80,48},{88,56},{96,... | collective-permute-start | bytes 3145736 | tf_op jit(solution)/shard_map/ppermute | solution.py:14
  152.9 46.5 %collective-permute-start.11 = (f32[256,1024]{1,0:T(8,128)}, f32[256,1024]{1,0:T(8,128)}, u32[]{:S(2)}, u32[]{:S(2)}) collective-permute-start(f32[256,1024]{1,0:T(8,128)} %copy.60), channel_id=1, source_target_pairs={{24,0},{32,8},{40,16},{48,24},{56,32},{64,40},{72,48},{80,56},{88,... | collective-permute-start | bytes 3145736 | tf_op jit(solution)/shard_map/ppermute | solution.py:14
  155.5 119.1 %collective-permute-start.10 = (f32[256,1024]{1,0:T(8,128)}, f32[256,1024]{1,0:T(8,128)}, u32[]{:S(2)}, u32[]{:S(2)}) collective-permute-start(f32[256,1024]{1,0:T(8,128)} %copy.59), channel_id=1, source_target_pairs={{16,0},{24,8},{32,16},{40,24},{48,32},{56,40},{64,48},{72,56},{80,... | collective-permute-start | bytes 3145736 | tf_op jit(solution)/shard_map/ppermute | solution.py:14
  159.6 418.5 %collective-permute-start.9 = (f32[256,1024]{1,0:T(8,128)}, f32[256,1024]{1,0:T(8,128)}, u32[]{:S(2)}, u32[]{:S(2)}) collective-permute-start(f32[256,1024]{1,0:T(8,128)} %copy.57), channel_id=1, source_target_pairs={{8,0},{16,8},{24,16},{32,24},{40,32},{48,40},{56,48},{64,56},{72,6... | collective-permute-start | bytes 3145736 | tf_op jit(solution)/shard_map/ppermute | solution.py:14
  161.0 17.9 %collective-permute-start.17 = (bf16[127,1024]{1,0:T(8,128)(2,1)S(1)}, bf16[127,1024]{1,0:T(8,128)(2,1)}, u32[]{:S(2)}, u32[]{:S(2)}) collective-permute-start(bf16[127,1024]{1,0:T(8,128)(2,1)S(1)} %slice.99), channel_id=1, source_target_pairs={{0,8},{8,16},{16,24},{24,32},{32,40},{40,48},{48,56},{56,64},{64,7... | collective-permute-start | bytes 780296 | tf_op jit(solution)/shard_map/ppermute | solution.py:14
  178.8 402.7 %collective-permute-start.16 = (f32[256,1024]{1,0:T(8,128)}, f32[256,1024]{1,0:T(8,128)}, u32[]{:S(2)}, u32[]{:S(2)}) collective-permute-start(f32[256,1024]{1,0:T(8,128)} %copy.68), channel_id=1, source_target_pairs={{32,0},{40,8},{48,16},{56,24},{64,32},{72,40},{80,48},{88,56},{96,... | collective-permute-start | bytes 3145736 | tf_op jit(solution)/shard_map/ppermute | solution.py:14
  195.3 80.9 %copy-start.24 = (bf16[128,1024]{1,0:T(8,128)(2,1)S(1)}, bf16[128,1024]{1,0:T(8,128)(2,1)}, u32[]{:S(2)}) copy-start(bf16[128,1024]{1,0:T(8,128)(2,1)} %rev.8) | copy-start | bytes 786436
  198.1 383.4 %collective-permute-start.15 = (f32[256,1024]{1,0:T(8,128)}, f32[256,1024]{1,0:T(8,128)}, u32[]{:S(2)}, u32[]{:S(2)}) collective-permute-start(f32[256,1024]{1,0:T(8,128)} %copy.67), channel_id=1, source_target_pairs={{24,0},{32,8},{40,16},{48,24},{56,32},{64,40},{72,48},{80,56},{88,... | collective-permute-start | bytes 3145736 | tf_op jit(solution)/shard_map/ppermute | solution.py:14
  199.4 382.1 %collective-permute-start.14 = (f32[256,1024]{1,0:T(8,128)}, f32[256,1024]{1,0:T(8,128)}, u32[]{:S(2)}, u32[]{:S(2)}) collective-permute-start(f32[256,1024]{1,0:T(8,128)} %copy.66), channel_id=1, source_target_pairs={{16,0},{24,8},{32,16},{40,24},{48,32},{56,40},{64,48},{72,56},{80,... | collective-permute-start | bytes 3145736 | tf_op jit(solution)/shard_map/ppermute | solution.py:14
  274.7 306.8 %collective-permute-start.13 = (f32[256,1024]{1,0:T(8,128)}, f32[256,1024]{1,0:T(8,128)}, u32[]{:S(2)}, u32[]{:S(2)}) collective-permute-start(f32[256,1024]{1,0:T(8,128)} %copy.64), channel_id=1, source_target_pairs={{8,0},{16,8},{24,16},{32,24},{40,32},{48,40},{56,48},{64,56},{72,6... | collective-permute-start | bytes 3145736 | tf_op jit(solution)/shard_map/ppermute | solution.py:14
  276.2 279.3 %copy-start.11 = (bf16[256,1024]{1,0:T(8,128)(2,1)S(1)}, bf16[256,1024]{1,0:T(8,128)(2,1)}, u32[]{:S(2)}) copy-start(bf16[256,1024]{1,0:T(8,128)(2,1)} %param.14) | copy-start | bytes 1572868
  292.0 286.1 %copy-start.4 = (f32[256,1024]{1,0:T(8,128)S(1)}, f32[256,1024]{1,0:T(8,128)}, u32[]{:S(2)}) copy-start(f32[256,1024]{1,0:T(8,128)} %copy.58) | copy-start | bytes 3145732
  (24 other events, 334.0 us)
Sparse Core Ops, SparseCore 0:
  198.2 355.4 all-reduce.3
where the time goes:
time: 593 us; the launch traced here: 592 us
  waiting for transfers between devices  366 us (62%)
  matrix products  66 us (11%)
  starting transfers between devices  52.2 us (9%)
  local copies, waits for them, and re-layouts  48.7 us (8%)
  other arithmetic  25.7 us (4%)
  blocking collectives  17.6 us (3%)
  between operations  16.1 us (3%)
    psum x1, waiting for transfers between devices, per_device(): filter_grad = lax.psum(filter_part, 'seq')  262 us
    ppermute x18, waiting for transfers between devices, from_behind(): return lax.ppermute(array, axis, pairs)  104 us
    ppermute x18, starting transfers between devices, from_behind(): return lax.ppermute(array, axis, pairs)  52.2 us
    psum x1, blocking collectives, per_device(): norms = lax.psum((filter_sq, jnp.sum(filter_grad * filter_grad)), 'ch')  17.6 us
    conv_general_dilated x1, matrix products, causal_conv(): lax.conv_general_dilated(extended[None], kernel, (1,), 'VALID', dimension...  15.8 us
    conv_general_dilated x1, matrix products, anti_conv(): lax.conv_general_dilated(extended[None], kernel, (1,), 'VALID', dimension...  14.8 us
    conv_general_dilated x1, matrix products, filter_corr(): lax.conv_general_dilated(extended[None], kernel, (1,), 'VALID', dimension...  13.9 us
    unnamed x72, local copies, waits for them, and re-layouts  13.3 us
  transfers between devices with their start and end apart: 19, of which 8 were waited for; matrix products, arithmetic and copies ran while one was open for 15% of the time, Pallas kernels for 0%

commit v1 on v0

v1 whole, which is shorter than its diff:
```python
import jax
import jax.numpy as jnp
from jax import lax
from jax.experimental import pallas as pl
from jax.experimental.pallas import tpu as pltpu
from jax.sharding import PartitionSpec as P


HD = 128
TAPS = 128
SPAN = 4
ROW = 8
TOK = 256
NEG = -1e30
STEP = 4
SCALE = HD ** (-0.5)


def causal_conv(extended, weights_in):
    kernel = jnp.flip(weights_in, 0)[:, None, :]
    return lax.conv_general_dilated(
        extended[None],
        kernel,
        (1,),
        "VALID",
        dimension_numbers=("NWC", "WIO", "NWC"),
        feature_group_count=extended.shape[1],
        preferred_element_type=jnp.float32,
    )[0]


def anti_conv(extended, weights_in):
    return lax.conv_general_dilated(
        extended[None],
        weights_in[:, None, :],
        (1,),
        "VALID",
        dimension_numbers=("NWC", "WIO", "NWC"),
        feature_group_count=extended.shape[1],
        preferred_element_type=jnp.float32,
    )[0]


def pack_kernel(*refs):
    *in_refs, out_ref = refs
    for head in range(out_ref.shape[0]):
        for n, in_ref in enumerate(in_refs):
            out_ref[head, n * TOK : (n + 1) * TOK] = in_ref[:, head * HD : (head + 1) * HD]


def pack(*arrays):
    heads = arrays[0].shape[1] // HD
    n = len(arrays)
    return pl.pallas_call(
        pack_kernel,
        grid=(heads // STEP,),
        in_specs=[pl.BlockSpec((TOK, STEP * HD), lambda h: (0, h))] * n,
        out_specs=pl.BlockSpec((STEP, n * TOK, HD), lambda h: (h, 0, 0)),
        out_shape=jax.ShapeDtypeStruct((heads, n * TOK, HD), arrays[0].dtype),
        name="pack",
    )(*arrays)


def pack_grad_kernel(q_ref, mixed_grad_ref, key_ref, out_ref):
    attn_grad = mixed_grad_ref[...] * key_ref[...].astype(jnp.float32)
    attn_grad = attn_grad.astype(jnp.bfloat16)
    for head in range(out_ref.shape[0]):
        lanes = slice(head * HD, (head + 1) * HD)
        out_ref[head, :TOK] = q_ref[:, lanes]
        out_ref[head, TOK:] = attn_grad[:, lanes]


def pack_grad(q, mixed_grad, key):
    heads = key.shape[1] // HD
    return pl.pallas_call(
        pack_grad_kernel,
        grid=(heads // STEP,),
        in_specs=[pl.BlockSpec((TOK, STEP * HD), lambda h: (0, h))] * 3,
        out_specs=pl.BlockSpec((STEP, 2 * TOK, HD), lambda h: (h, 0, 0)),
        out_shape=jax.ShapeDtypeStruct((heads, 2 * TOK, HD), key.dtype),
        name="pack_grad",
    )(q, mixed_grad, key)


def unpack_kernel(x_ref, *out_refs):
    for head in range(x_ref.shape[0]):
        for n, out_ref in enumerate(out_refs):
            out_ref[:, head * HD : (head + 1) * HD] = x_ref[head, n * TOK : (n + 1) * TOK]


def unpack(x):
    heads, rows, _ = x.shape
    n = rows // TOK
    return pl.pallas_call(
        unpack_kernel,
        grid=(heads // STEP,),
        in_specs=[pl.BlockSpec((STEP, rows, HD), lambda h: (h, 0, 0))],
        out_specs=[pl.BlockSpec((TOK, STEP * HD), lambda h: (0, h))] * n,
        out_shape=[jax.ShapeDtypeStruct((TOK, heads * HD), x.dtype)] * n,
        name="unpack",
    )(x)


def dot_nn(a, b):
    return jnp.dot(a, b, preferred_element_type=jnp.float32)


def window_of(block, width):
    first = block + (SPAN + 1 - width)
    return first, pl.ds(pl.multiple_of(first * TOK, TOK), width * TOK)


def key_blocks(kv_ref, kvh_ref):
    for b in range(SPAN + ROW):
        src = kvh_ref if b < SPAN else kv_ref
        at = b if b < SPAN else b - SPAN
        yield b, slice(b * TOK, (b + 1) * TOK), src[at, :TOK], src[at, TOK:]


def masked_scores(k, q, kdoc, qdoc, width):
    scores = dot_nn(k, q.T)
    same = jnp.concatenate([kdoc, kdoc], 1) == qdoc
    key_at = lax.broadcasted_iota(jnp.int32, scores.shape, 0)
    query_at = lax.broadcasted_iota(jnp.int32, scores.shape, 1) + (width - 1) * TOK
    return jnp.where(same & (key_at <= query_at), scores, NEG)


def by_width(width_ref, block, attend):
    for width in range(1, SPAN + 2):
        pl.when(width_ref[block] == width)(lambda width=width: attend(width))


def fwd_kernel(
    width_ref, kv_ref, kvh_ref, kdoc_ref, qdoc_ref, qg_ref, out_ref, top_ref, inv_ref, k_s, vt_s
):
    block = pl.program_id(0)

    @pl.when(block == 0)
    def _():
        for b, rows, k, v in key_blocks(kv_ref, kvh_ref):
            k_s[rows] = k
            vt_s[b] = v.T

    def attend(width):
        first, rows = window_of(block, width)
        q = qg_ref[0, :TOK]
        vt = jnp.concatenate([vt_s[first + n] for n in range(width)], 1)
        scores = masked_scores(k_s[rows], q, kdoc_ref[rows], qdoc_ref[0], width)
        top = jnp.max(scores, 0, keepdims=True)
        weights = jnp.exp((scores - top) * SCALE)
        inv = 1.0 / jnp.sum(weights, 0, keepdims=True)
        top_ref[0] = top
        inv_ref[0] = inv
        probs = (weights * inv).astype(jnp.bfloat16)
        out_ref[0] = dot_nn(vt, probs).astype(jnp.bfloat16).T

    by_width(width_ref, block, attend)


def bwd_kernel(
    width_ref, kv_ref, kvh_ref, kdoc_ref, qdoc_ref, qg_ref, out_ref, top_ref, inv_ref,
    dq_ref, dkv_lo_ref, dkv_hi_ref, dkvh_ref, k_s, v_s, kt_s, dk_s, dv_s,
):
    block = pl.program_id(0)

    @pl.when(block == 0)
    def _():
        for b, rows, k, v in key_blocks(kv_ref, kvh_ref):
            k_s[rows] = k
            v_s[rows] = v
            kt_s[b] = k.T
        dk_s[...] = jnp.zeros_like(dk_s)
        dv_s[...] = jnp.zeros_like(dv_s)

    def attend(width):
        first, rows = window_of(block, width)
        q = qg_ref[0, :TOK]
        grad = qg_ref[0, TOK:]
        grad_t = grad.T
        kt = jnp.concatenate([kt_s[first + n] for n in range(width)], 1)
        scores = masked_scores(k_s[rows], q, kdoc_ref[rows], qdoc_ref[0], width)
        weights = jnp.exp((scores - top_ref[0]) * SCALE) * inv_ref[0]
        probs = weights.astype(jnp.bfloat16)
        row_dot = jnp.sum(
            out_ref[0].T.astype(jnp.float32) * grad_t.astype(jnp.float32), 0, keepdims=True
        )
        prob_grad = dot_nn(v_s[rows], grad_t)
        score_grad = (weights * (prob_grad - row_dot)).astype(jnp.bfloat16)
        dq_ref[0] = (dot_nn(kt, score_grad) * SCALE).astype(jnp.bfloat16).T
        dk_s[rows] += dot_nn(score_grad, q)
        dv_s[rows] += dot_nn(probs, grad)

    by_width(width_ref, block, attend)

    @pl.when(block == ROW - 1)
    def _():
        outs = (dkvh_ref, dkv_lo_ref, dkv_hi_ref)
        for b in range(SPAN + ROW):
            rows = slice(b * TOK, (b + 1) * TOK)
            ref = outs[b // SPAN]
            ref[b % SPAN, :TOK] = (dk_s[rows] * SCALE).astype(ref.dtype)
            ref[b % SPAN, TOK:] = dv_s[rows].astype(ref.dtype)


KEYS = (SPAN + ROW) * TOK


def whole(*shape):
    return pl.BlockSpec(shape, lambda b, w: (0,) * len(shape))


def each(*shape):
    return pl.BlockSpec((1,) + shape, lambda b, w: (b, 0, 0))


SHARED_SPECS = [
    whole(ROW, 2 * TOK, HD),
    whole(SPAN, 2 * TOK, HD),
    whole(KEYS, HD),
    each(1, TOK),
    each(2 * TOK, HD),
]


def attention_fwd(widths, *operands):
    return pl.pallas_call(
        fwd_kernel,
        grid_spec=pltpu.PrefetchScalarGridSpec(
            num_scalar_prefetch=1,
            grid=(ROW,),
            in_specs=SHARED_SPECS,
            out_specs=[each(TOK, HD), each(1, TOK), each(1, TOK)],
            scratch_shapes=[
                pltpu.VMEM((KEYS, HD), jnp.bfloat16),
                pltpu.VMEM((SPAN + ROW, HD, TOK), jnp.bfloat16),
            ],
        ),
        out_shape=[
            jax.ShapeDtypeStruct((ROW, TOK, HD), jnp.bfloat16),
            jax.ShapeDtypeStruct((ROW, 1, TOK), jnp.float32),
            jax.ShapeDtypeStruct((ROW, 1, TOK), jnp.float32),
        ],
        compiler_params=pltpu.CompilerParams(vmem_limit_bytes=40 << 20),
        name="attn_fwd",
    )(widths, *operands)


def attention_bwd(widths, *operands):
    return pl.pallas_call(
        bwd_kernel,
        grid_spec=pltpu.PrefetchScalarGridSpec(
            num_scalar_prefetch=1,
            grid=(ROW,),
            in_specs=SHARED_SPECS + [each(TOK, HD), each(1, TOK), each(1, TOK)],
            out_specs=[each(TOK, HD)] + [whole(SPAN, 2 * TOK, HD)] * 3,
            scratch_shapes=[
                pltpu.VMEM((KEYS, HD), jnp.bfloat16),
                pltpu.VMEM((KEYS, HD), jnp.bfloat16),
                pltpu.VMEM((SPAN + ROW, HD, TOK), jnp.bfloat16),
                pltpu.VMEM((KEYS, HD), jnp.float32),
                pltpu.VMEM((KEYS, HD), jnp.float32),
            ],
        ),
        out_shape=[
            jax.ShapeDtypeStruct((ROW, TOK, HD), jnp.bfloat16),
            jax.ShapeDtypeStruct((SPAN, 2 * TOK, HD), jnp.bfloat16),
            jax.ShapeDtypeStruct((SPAN, 2 * TOK, HD), jnp.float32),
            jax.ShapeDtypeStruct((SPAN, 2 * TOK, HD), jnp.bfloat16),
        ],
        compiler_params=pltpu.CompilerParams(vmem_limit_bytes=40 << 20),
        name="attn_bwd",
    )(widths, *operands)


def per_device(
    queries_in, keys_in, values_in, gate_branch, key_branch, mr_filter, out_grad, doc_ids
):
    n_seq = lax.axis_size("seq")
    position = lax.axis_index("seq")
    rings = [list(range(g, g + ROW)) for g in range(0, n_seq, ROW)]

    def swap(x, groups=rings, axis="seq"):
        return lax.all_to_all(x, axis, 0, 0, axis_index_groups=groups, tiled=True)

    def shift(x, by):
        pairs = [(i, i + by) for i in range(n_seq) if 0 <= i + by < n_seq]
        return lax.ppermute(x, "seq", pairs)

    doc_front = jnp.concatenate([jnp.full((SPAN * TOK,), -1, jnp.int32), doc_ids], 0)
    docs = lax.dynamic_slice_in_dim(
        doc_front, (position // ROW) * (ROW * TOK), (SPAN + ROW) * TOK, 0
    ).reshape(SPAN + ROW, TOK)
    widths = jnp.ones((ROW,), jnp.int32)
    for back in range(1, SPAN + 1):
        widths = widths + (docs[SPAN - back : SPAN + ROW - back, -1] == docs[SPAN:, 0])
    kdoc = jnp.broadcast_to(docs.reshape(-1, 1), ((SPAN + ROW) * TOK, HD))
    qdoc = docs[SPAN:].reshape(ROW, 1, TOK)

    kv = swap(pack(keys_in, values_in))

    conv_grad = (out_grad.astype(jnp.float32) * gate_branch.astype(jnp.float32)).astype(
        jnp.bfloat16
    )
    grad_edge = shift(conv_grad[:TAPS], -1)
    mixed_grad = anti_conv(
        jnp.concatenate([conv_grad, grad_edge[: TAPS - 1]], 0), mr_filter
    )
    kvh = shift(kv[ROW - SPAN :], ROW)
    qg = swap(pack_grad(queries_in, mixed_grad, key_branch))

    shared = (widths, kv, kvh, kdoc, qdoc, qg)
    attn_head, top, inv = attention_fwd(*shared)
    attn_out = unpack(swap(attn_head))[0]
    dq_head, dkv_lo, dkv_hi, dkvh = attention_bwd(*shared, attn_head, top, inv)
    back = shift(dkvh, -ROW)
    dkv_hi = (dkv_hi + back.astype(jnp.float32)).astype(jnp.bfloat16)
    dqkv = jnp.concatenate([dq_head, jnp.concatenate([dkv_lo, dkv_hi], 0)], 1)
    query_grad, key_grad, value_grad = unpack(swap(dqkv))

    mixed = (key_branch.astype(jnp.float32) * attn_out.astype(jnp.float32)).astype(jnp.bfloat16)
    mixed_edge = shift(mixed[TOK - TAPS :], 1)
    mixed_ext = jnp.concatenate([mixed_edge[1:], mixed], 0)
    filter_part = anti_conv(mixed_ext, conv_grad)
    conv_out = causal_conv(mixed_ext, mr_filter)
    gate_grad = (out_grad.astype(jnp.float32) * conv_out).astype(jnp.bfloat16)
    branch_grad = (mixed_grad * attn_out.astype(jnp.float32)).astype(jnp.bfloat16)

    tap_rows = TAPS // n_seq
    parts = jnp.flip(filter_part, 0).astype(jnp.bfloat16)
    parts = swap(parts.reshape(n_seq, tap_rows, -1), None)
    own_grad = jnp.sum(parts.astype(jnp.float32), 0)
    own_filter = lax.dynamic_slice_in_dim(mr_filter, position * tap_rows, tap_rows, 0)
    norms = jnp.stack(
        [jnp.sum(jnp.square(own_filter.astype(jnp.float32))), jnp.sum(own_grad * own_grad)]
    )
    norms = jnp.broadcast_to(norms[:, None], (2, HD))
    hops = [("ch", 1), ("ch", 2), ("ch", 4)] + [("seq", h) for h in (8, 16, 1, 2, 4)]
    for axis, hop in hops:
        pairs = [(i, i ^ hop) for i in range(lax.axis_size(axis))]
        norms = norms + lax.ppermute(norms, axis, pairs)
    trust = jnp.sqrt(norms[0, 0]) / jnp.sqrt(norms[1, 0] + 1e-06)
    filter_step = trust * own_grad
    return (query_grad, key_grad, value_grad, gate_grad, branch_grad, filter_step)


def solution(mesh):
    rows = P("seq", "ch")
    return jax.shard_map(
        per_device,
        mesh=mesh,
        in_specs=(rows, rows, rows, rows, rows, P(None, "ch"), rows, P()),
        out_specs=(rows,) * 6,
        check_vma=False,
    )
```

time: 593 us -> 251 us (0.42)
  waiting for transfers between devices: 366 us -> 70.6 us
  local copies, waits for them, and re-layouts: 48.7 us -> 17.4 us
  matrix products: 66 us -> 42.9 us
  Pallas kernels: 0 us -> 22.6 us
  between operations: 16.1 us -> 2.34 us
  other arithmetic: 25.7 us -> 12.3 us
    psum x1 -> x0, waiting for transfers between devices: 262 us -> none  [per_device(): filter_grad = lax.psum(filter_part, 'seq')]
    ppermute x18 -> x12, waiting for transfers between devices: 104 us -> 36.3 us  [the longest x8 24.1 us: per_device(): norms = norms + lax.ppermute(norms, axis, pairs)]
    all_to_all x0 -> x4, waiting for transfers between devices: none -> 34.3 us  [swap(): return lax.all_to_all(x, axis, 0, 0, axis_index_groups=groups, tiled=True)]
    all_to_all x0 -> x4, starting transfers between devices: none -> 32 us  [swap(): return lax.all_to_all(x, axis, 0, 0, axis_index_groups=groups, tiled=True)]
    ppermute x18 -> x12, starting transfers between devices: 52.2 us -> 26.1 us  [the longest x8 18.3 us: per_device(): norms = norms + lax.ppermute(norms, axis, pairs)]
    slice x14 -> x7, local copies, waits for them, and re-layouts: 25.9 us -> 0.73 us  [the longest x1 0.52 us: per_device(): trust = jnp.sqrt(norms[0, 0]) / jnp.sqrt(norms[1, 0] + 1e-06)]
    pallas_call x0 -> x6, Pallas kernels: none -> 22.6 us  [the longest x1 7.43 us: attention_bwd(): pl.pallas_call(bwd_kernel, grid_spec=pltpu.PrefetchScalarGridSpec(num_sca...]
    dot_general x6 -> x0, matrix products: 21.5 us -> none  [the longest x1 7.36 us: per_device(): jnp.einsum('qhd,khd->hqk', out_grads, value_win, preferred_element_type=j...]
  transfers between devices with their start and end apart: 19 -> 16, of which waited for: 8 -> 9; matrix products, arithmetic and copies ran while one was open for 15% -> 17% of each run, Pallas kernels for 0% -> 5%
where the time goes in v1:
time: 251 us; the launch traced here: 247 us
  waiting for transfers between devices  70.6 us (28%)
  starting transfers between devices  58.1 us (23%)
  matrix products  42.9 us (17%)
  Pallas kernels  22.6 us (9%)
  blocking collectives  20.9 us (8%)
  local copies, waits for them, and re-layouts  17.4 us (7%)
  other arithmetic  12.3 us (5%)
    all_to_all x4, waiting for transfers between devices, swap(): return lax.all_to_all(x, axis, 0, 0, axis_index_groups=groups, tiled=True)  34.3 us
    all_to_all x4, starting transfers between devices, swap(): return lax.all_to_all(x, axis, 0, 0, axis_index_groups=groups, tiled=True)  32 us
    conv_general_dilated x2, matrix products, anti_conv(): lax.conv_general_dilated(extended[None], weights_in[:, None, :], (1,), 'V...  28.8 us
    ppermute x8, waiting for transfers between devices, per_device(): norms = norms + lax.ppermute(norms, axis, pairs)  24.1 us
    all_to_all x1, blocking collectives, swap(): return lax.all_to_all(x, axis, 0, 0, axis_index_groups=groups, tiled=True)  20.9 us
    ppermute x8, starting transfers between devices, per_device(): norms = norms + lax.ppermute(norms, axis, pairs)  18.3 us
    conv_general_dilated x1, matrix products, causal_conv(): lax.conv_general_dilated(extended[None], kernel, (1,), 'VALID', dimension...  14.1 us
    ppermute x4, waiting for transfers between devices, shift(): return lax.ppermute(x, 'seq', pairs)  12.2 us
  transfers between devices with their start and end apart: 16, of which 9 were waited for; matrix products, arithmetic and copies ran while one was open for 17% of the time, Pallas kernels for 5%

profile of v1, /device:TPU:1, one launch (start us, length us, event | category | flops | bytes accessed | tf_op | source)
XLA Modules:
  0.0 247.3 jit_solution(3984442836236860709)
XLA Ops:
  5.5 10.0 %all-to-all-start = ((bf16[8,512,128]{2,1,0:T(8,128)(2,1)}), bf16[8,512,128]{2,1,0:T(8,128)(2,1)S(1)}, u32[]{:S(2)}, u32[]{:S(2)}) async-start(bf16[8,512,128]{2,1,0:T(8,128)(2,1)} %pack.1), calls=%async_computation | async-start | bytes 2097152 | tf_op jit(solution)/shard_map/all_to_all | solution.py:283
  15.6 14.8 %fusion = f32[1,256,1024]{2,0,1:T(1,128)} fusion(bf16[1,383,1024]{2,1,0:T(8,128)(2,1)S(1)} %maximum_bitcast_fusion, bf16[128,1,1024]{2,0,1:T(8,128)(2,1)S(1)} %bitcast.29), kind=kOutput, calls=%fused_computation.1 | convolution fusion | flops 67108864 | bytes 2095104 | tf_op jit(solution)/shard_map/conv_general_dilated | solution.py:33
  30.4 2.4 copy.67
  35.2 9.5 %all-to-all-done.kv_ref = bf16[8,512,128]{2,1,0:T(8,128)(2,1)S(1)} async-done(((bf16[8,512,128]{2,1,0:T(8,128)(2,1)}), bf16[8,512,128]{2,1,0:T(8,128)(2,1)S(1)}, u32[]{:S(2)}, u32[]{:S(2)}) %all-to-all-start) | async-done | bytes 1048608 | tf_op jit(solution)/shard_map/all_to_all | solution.py:283
  44.7 3.6 %all-to-all-start.1 = ((bf16[8,512,128]{2,1,0:T(8,128)(2,1)}), bf16[8,512,128]{2,1,0:T(8,128)(2,1)S(1)}, u32[]{:S(2)}, u32[]{:S(2)}) async-start(bf16[8,512,128]{2,1,0:T(8,128)(2,1)} %pack_grad.1), calls=%async_computation.1 | async-start | bytes 2097152 | tf_op jit(solution)/shard_map/all_to_all | solution.py:283
  48.4 3.7 %collective-permute-start = (bf16[4,512,128]{2,1,0:T(8,128)(2,1)S(1)}, bf16[4,512,128]{2,1,0:T(8,128)(2,1)S(1)}, u32[]{:S(2)}, u32[]{:S(2)}) collective-permute-start(bf16[4,512,128]{2,1,0:T(8,128)(2,1)S(1)} %slice.72), channel_id=1, source_target_pairs={{0,64},{8,72},{16,80},{24,88},{32,96},{40,104},{48,112},{56,120},{... | collective-permute-start | bytes 1572872 | tf_op jit(solution)/shard_map/ppermute | solution.py:287
  52.6 24.8 %all-to-all-done.1.qg_ref = bf16[8,512,128]{2,1,0:T(8,128)(2,1)S(1)} async-done(((bf16[8,512,128]{2,1,0:T(8,128)(2,1)}), bf16[8,512,128]{2,1,0:T(8,128)(2,1)S(1)}, u32[]{:S(2)}, u32[]{:S(2)}) %all-to-all-start.1) | async-done | bytes 1048608 | tf_op jit(solution)/shard_map/all_to_all | solution.py:283
  79.6 6.5 %attn_fwd.1 = (bf16[8,256,128]{2,1,0:T(8,128)(2,1)S(1)}, f32[8,1,256]{2,1,0:T(1,128)S(1)}, f32[8,1,256]{2,1,0:T(1,128)S(1)}) custom-call(s32[8]{0:T(128)S(1)} %fusion.17.width_ref, bf16[8,512,128]{2,1,0:T(8,128)(2,1)S(1)} %all-to-all-done.kv_ref, bf16[4,512,128]{2,1,0:T(8,128)(2,1)S(1)} %collective-permute-done.kvh_ref, ...), custom_call_target="tpu_custom_call" | custom-call | tf_op jit(solution)/shard_map/attn_fwd/pallas_call | solution.py:226
  86.1 20.9 %all_to_all.25.x_ref = bf16[8,256,128]{2,1,0:T(8,128)(2,1)} all-to-all(bf16[8,256,128]{2,1,0:T(8,128)(2,1)S(1)} %get-tuple-element.16.out_ref), channel_id=1, replica_groups={{0,8,16,24,32,40,48,56},{64,72,80,88,96,104,112,120},{128,136,144,152,1..., dimensions={0} | all-to-all | bytes 1048576 | tf_op jit(solution)/shard_map/all_to_all | solution.py:283
  109.6 2.7 %fusion.9 = (bf16[256,1024]{1,0:T(8,128)(2,1)}, bf16[256,1024]{1,0:T(8,128)(2,1)S(1)}) fusion(bf16[256,1024]{1,0:T(8,128)(2,1)} %unpack.3, f32[1,256,1024]{2,0,1:T(1,128)} %fusion, bf16[256,1024]{1,0:T(8,128)(2,1)} %key_ref.1), kind=kLoop, calls=%fused_computation.14 | loop fusion | flops 1572864 | bytes 3145728 | tf_op jit(solution)/shard_map/convert_element_type | solution.py:326
  113.8 4.1 %collective-permute-done.3 = bf16[128,1024]{1,0:T(8,128)(2,1)S(1)} collective-permute-done((bf16[128,1024]{1,0:T(8,128)(2,1)S(1)}, bf16[128,1024]{1,0:T(8,128)(2,1)S(1)}, u32[]{:S(2)}, u32[]{:S(2)}) %collective-permute-start.3) | collective-permute-done | bytes 262176 | tf_op jit(solution)/shard_map/ppermute | solution.py:287
  118.1 14.0 %fusion.2 = bf16[1,128,1024]{2,0,1:T(2,128)(2,1)S(1)} fusion(bf16[1,383,1024]{2,1,0:T(8,128)(2,1)S(1)} %maximum_bitcast_fusion.1, bf16[256,1,1024]{2,0,1:T(8,128)(2,1)S(1)} %bitcast.27), kind=kOutput, calls=%fused_computation.7 | convolution fusion | flops 67108864 | bytes 1570816 | tf_op jit(solution)/shard_map/conv_general_dilated | solution.py:33
  132.2 2.6 %rev.9 = bf16[128,1024]{1,0:T(8,128)(2,1)} reverse(bf16[128,1024]{1,0:T(8,128)(2,1)S(1)} %bitcast.28), dimensions={0} | reverse | bytes 524288 | tf_op jit(solution)/shard_map/jit(_flip)/rev | solution.py:329
  136.6 11.9 %all-to-all-start.4 = ((bf16[32,4,1024]{2,1,0:T(4,128)(2,1)}), bf16[32,4,1024]{2,1,0:T(4,128)(2,1)S(1)}, u32[]{:S(2)}, u32[]{:S(2)}) async-start(bf16[32,4,1024]{2,1,0:T(4,128)(2,1)} %reshape.50), calls=%async_computation.4 | async-start | bytes 524288 | tf_op jit(solution)/shard_map/all_to_all | solution.py:283
  150.8 7.4 %attn_bwd.1 = (bf16[8,256,128]{2,1,0:T(8,128)(2,1)S(1)}, bf16[4,512,128]{2,1,0:T(8,128)(2,1)S(1)}, f32[4,512,128]{2,1,0:T(8,128)S(1)}, bf16[4,512,128]{2,1,0:T(8,128)(2,1)}) custom-call(s32[8]{0:T(128)S(1)} %fusion.17.width_ref, bf16[8,512,128]{2,1,0:T(8,128)(2,1)S(1)} %all-to-all-done.kv_ref, bf16[4,512,128]{2,1,0:T(8,128)(2,1)S(1)} %collective-permute-done.kvh_ref, ...), custom_call_target="tpu_custom_call" | custom-call | tf_op jit(solution)/shard_map/attn_bwd/pallas_call | solution.py:249
  167.6 8.1 %collective-permute-done.2 = bf16[4,512,128]{2,1,0:T(8,128)(2,1)S(1)} collective-permute-done((bf16[4,512,128]{2,1,0:T(8,128)(2,1)}, bf16[4,512,128]{2,1,0:T(8,128)(2,1)S(1)}, u32[]{:S(2)}, u32[]{:S(2)}) %collective-permute-start.2) | collective-permute-done | bytes 524320 | tf_op jit(solution)/shard_map/ppermute | solution.py:287
  179.7 6.5 %all-to-all-start.2 = ((bf16[8,768,128]{2,1,0:T(8,128)(2,1)}), bf16[8,768,128]{2,1,0:T(8,128)(2,1)S(1)}, u32[]{:S(2)}, u32[]{:S(2)}) async-start(bf16[8,768,128]{2,1,0:T(8,128)(2,1)} %maximum_maximum_fusion), calls=%async_computation.2 | async-start | bytes 3145728 | tf_op jit(solution)/shard_map/all_to_all | solution.py:283
  186.2 2.6 %collective-permute-start.6 = (f32[2,128]{1,0:T(2,128)S(1)}, f32[2,128]{1,0:T(2,128)S(1)}, u32[]{:S(2)}, u32[]{:S(2)}) collective-permute-start(f32[2,128]{1,0:T(2,128)S(1)} %fusion.20), channel_id=1, source_target_pairs={{0,4},{1,5},{2,6},{3,7},{4,0},{5,1},{6,2},{7,3},{8,12},{9,13},{10,... | collective-permute-start | bytes 3080 | tf_op jit(solution)/shard_map/ppermute | solution.py:340
  192.6 2.6 %collective-permute-start.8 = (f32[2,128]{1,0:T(2,128)S(1)}, f32[2,128]{1,0:T(2,128)S(1)}, u32[]{:S(2)}, u32[]{:S(2)}) collective-permute-start(f32[2,128]{1,0:T(2,128)S(1)} %add.62), channel_id=1, source_target_pairs={{0,128},{8,136},{16,144},{24,152},{32,160},{40,168},{48,176},{56,1... | collective-permute-start | bytes 3080 | tf_op jit(solution)/shard_map/ppermute | solution.py:340
  198.7 18.0 %collective-permute-done.9 = f32[2,128]{1,0:T(2,128)S(1)} collective-permute-done((f32[2,128]{1,0:T(2,128)S(1)}, f32[2,128]{1,0:T(2,128)S(1)}, u32[]{:S(2)}, u32[]{:S(2)}) %collective-permute-start.9) | collective-permute-done | bytes 1056 | tf_op jit(solution)/shard_map/ppermute | solution.py:340
  216.7 3.9 %collective-permute-start.10 = (f32[2,128]{1,0:T(2,128)S(1)}, f32[2,128]{1,0:T(2,128)S(1)}, u32[]{:S(2)}, u32[]{:S(2)}) collective-permute-start(f32[2,128]{1,0:T(2,128)S(1)} %add.64), channel_id=1, source_target_pairs={{0,16},{8,24},{16,0},{24,8},{32,48},{40,56},{48,32},{56,40},{64,80... | collective-permute-start | bytes 3080 | tf_op jit(solution)/shard_map/ppermute | solution.py:340
  220.6 14.1 %fusion.4 = f32[1,256,1024]{2,0,1:T(1,128)S(1)} fusion(bf16[1,383,1024]{2,1,0:T(8,128)(2,1)S(1)} %copy-done.15, bf16[128,1,1024]{2,0,1:T(8,128)(2,1)S(1)} %bitcast.30), kind=kOutput, calls=%fused_computation.9 | convolution fusion | flops 67108864 | bytes 2095104 | tf_op jit(solution)/shard_map/conv_general_dilated | solution.py:21
  234.7 3.4 %collective-permute-start.11 = (f32[2,128]{1,0:T(2,128)S(1)}, f32[2,128]{1,0:T(2,128)S(1)}, u32[]{:S(2)}, u32[]{:S(2)}) collective-permute-start(f32[2,128]{1,0:T(2,128)S(1)} %add.65), channel_id=1, source_target_pairs={{0,32},{8,40},{16,48},{24,56},{32,0},{40,8},{48,16},{56,24},{64,96... | collective-permute-start | bytes 3080 | tf_op jit(solution)/shard_map/ppermute | solution.py:340
  244.8 2.4 unpack.2
  (98 shorter events, 44.2 us)
Async XLA Ops:
  2.0 13.5 %copy-start.11 = (bf16[256,1024]{1,0:T(8,128)(2,1)}, bf16[256,1024]{1,0:T(8,128)(2,1)S(1)}, u32[]{:S(2)}) copy-start(bf16[256,1024]{1,0:T(8,128)(2,1)S(1)} %fusion.6) | copy-start | bytes 1572868
  2.1 13.4 %collective-permute-start.1 = (bf16[128,1024]{1,0:T(8,128)(2,1)S(1)}, bf16[128,1024]{1,0:T(8,128)(2,1)S(1)}, u32[]{:S(2)}, u32[]{:S(2)}) collective-permute-start(bf16[128,1024]{1,0:T(8,128)(2,1)S(1)} %slice.73), channel_id=1, source_target_pairs={{8,0},{16,8},{24,16},{32,24},{40,32},{48,40},{56,48},{64,56},{72,6... | collective-permute-start | bytes 786440 | tf_op jit(solution)/shard_map/ppermute | solution.py:287
  5.5 39.2 %all-to-all-start = ((bf16[8,512,128]{2,1,0:T(8,128)(2,1)}), bf16[8,512,128]{2,1,0:T(8,128)(2,1)S(1)}, u32[]{:S(2)}, u32[]{:S(2)}) async-start(bf16[8,512,128]{2,1,0:T(8,128)(2,1)} %pack.1), calls=%async_computation | async-start | bytes 2097152 | tf_op jit(solution)/shard_map/all_to_all | solution.py:283
  35.2 13.1 %copy-start.18 = (s32[8192]{0:T(1024)S(1)}, s32[8192]{0:T(1024)}, u32[]{:S(2)}) copy-start(s32[8192]{0:T(1024)} %param.15) | copy-start | bytes 98308
  44.7 32.7 %all-to-all-start.1 = ((bf16[8,512,128]{2,1,0:T(8,128)(2,1)}), bf16[8,512,128]{2,1,0:T(8,128)(2,1)S(1)}, u32[]{:S(2)}, u32[]{:S(2)}) async-start(bf16[8,512,128]{2,1,0:T(8,128)(2,1)} %pack_grad.1), calls=%async_computation.1 | async-start | bytes 2097152 | tf_op jit(solution)/shard_map/all_to_all | solution.py:283
  48.4 30.0 %collective-permute-start = (bf16[4,512,128]{2,1,0:T(8,128)(2,1)S(1)}, bf16[4,512,128]{2,1,0:T(8,128)(2,1)S(1)}, u32[]{:S(2)}, u32[]{:S(2)}) collective-permute-start(bf16[4,512,128]{2,1,0:T(8,128)(2,1)S(1)} %slice.72), channel_id=1, source_target_pairs={{0,64},{8,72},{16,80},{24,88},{32,96},{40,104},{48,112},{56,120},{... | collective-permute-start | bytes 1572872 | tf_op jit(solution)/shard_map/ppermute | solution.py:287
  112.4 5.6 %collective-permute-start.3 = (bf16[128,1024]{1,0:T(8,128)(2,1)S(1)}, bf16[128,1024]{1,0:T(8,128)(2,1)S(1)}, u32[]{:S(2)}, u32[]{:S(2)}) collective-permute-start(bf16[128,1024]{1,0:T(8,128)(2,1)S(1)} %slice.75), channel_id=1, source_target_pairs={{0,8},{8,16},{16,24},{24,32},{32,40},{40,48},{48,56},{56,64},{64,7... | collective-permute-start | bytes 786440 | tf_op jit(solution)/shard_map/ppermute | solution.py:287
  118.1 14.0 %copy-start.14 = (bf16[1,383,1024]{2,1,0:T(8,128)(2,1)}, bf16[1,383,1024]{2,1,0:T(8,128)(2,1)S(1)}, u32[]{:S(2)}) copy-start(bf16[1,383,1024]{2,1,0:T(8,128)(2,1)S(1)} %maximum_bitcast_fusion.1) | copy-start | bytes 2353156
  136.6 27.0 %all-to-all-start.4 = ((bf16[32,4,1024]{2,1,0:T(4,128)(2,1)}), bf16[32,4,1024]{2,1,0:T(4,128)(2,1)S(1)}, u32[]{:S(2)}, u32[]{:S(2)}) async-start(bf16[32,4,1024]{2,1,0:T(4,128)(2,1)} %reshape.50), calls=%async_computation.4 | async-start | bytes 524288 | tf_op jit(solution)/shard_map/all_to_all | solution.py:283
  160.7 17.6 %copy-start.7 = (bf16[8,256,128]{2,1,0:T(8,128)(2,1)S(1)}, bf16[8,256,128]{2,1,0:T(8,128)(2,1)}, u32[]{:S(2)}) copy-start(bf16[8,256,128]{2,1,0:T(8,128)(2,1)} %copy-done.6) | copy-start | bytes 1572868
  160.7 17.6 %copy-start.9 = (bf16[4,512,128]{2,1,0:T(8,128)(2,1)S(1)}, bf16[4,512,128]{2,1,0:T(8,128)(2,1)}, u32[]{:S(2)}) copy-start(bf16[4,512,128]{2,1,0:T(8,128)(2,1)} %copy-done.8) | copy-start | bytes 1572868
  160.8 14.9 %collective-permute-start.2 = (bf16[4,512,128]{2,1,0:T(8,128)(2,1)}, bf16[4,512,128]{2,1,0:T(8,128)(2,1)S(1)}, u32[]{:S(2)}, u32[]{:S(2)}) collective-permute-start(bf16[4,512,128]{2,1,0:T(8,128)(2,1)} %get-tuple-element.22), channel_id=1, source_target_pairs={{64,0},{72,8},{80,16},{88,24},{96,32},{104,40},{112,48},{120,56},{... | collective-permute-start | bytes 1572872 | tf_op jit(solution)/shard_map/ppermute | solution.py:287
  165.8 11.2 %collective-permute-start.4 = (f32[2,128]{1,0:T(2,128)S(1)}, f32[2,128]{1,0:T(2,128)S(1)}, u32[]{:S(2)}, u32[]{:S(2)}) collective-permute-start(f32[2,128]{1,0:T(2,128)S(1)} %broadcast_in_dim.34), channel_id=1, source_target_pairs={{0,1},{1,0},{2,3},{3,2},{4,5},{5,4},{6,7},{7,6},{8,9},{9,8},{10,11... | collective-permute-start | bytes 3080 | tf_op jit(solution)/shard_map/ppermute | solution.py:340
  177.1 9.1 %collective-permute-start.5 = (f32[2,128]{1,0:T(2,128)S(1)}, f32[2,128]{1,0:T(2,128)S(1)}, u32[]{:S(2)}, u32[]{:S(2)}) collective-permute-start(f32[2,128]{1,0:T(2,128)S(1)} %broadcast_add_fusion), channel_id=1, source_target_pairs={{0,2},{1,3},{2,0},{3,1},{4,6},{5,7},{6,4},{7,5},{8,10},{9,11},{10,... | collective-permute-start | bytes 3080 | tf_op jit(solution)/shard_map/ppermute | solution.py:340
  179.7 18.7 %copy-start.17 = (bf16[128,1024]{1,0:T(8,128)(2,1)S(1)}, bf16[128,1024]{1,0:T(8,128)(2,1)}, u32[]{:S(2)}) copy-start(bf16[128,1024]{1,0:T(8,128)(2,1)} %param.13) | copy-start | bytes 786436
  179.7 40.9 %copy-start.15 = (bf16[1,383,1024]{2,1,0:T(8,128)(2,1)S(1)}, bf16[1,383,1024]{2,1,0:T(8,128)(2,1)}, u32[]{:S(2)}) copy-start(bf16[1,383,1024]{2,1,0:T(8,128)(2,1)} %copy-done.14) | copy-start | bytes 2353156
  179.7 64.0 %all-to-all-start.2 = ((bf16[8,768,128]{2,1,0:T(8,128)(2,1)}), bf16[8,768,128]{2,1,0:T(8,128)(2,1)S(1)}, u32[]{:S(2)}, u32[]{:S(2)}) async-start(bf16[8,768,128]{2,1,0:T(8,128)(2,1)} %maximum_maximum_fusion), calls=%async_computation.2 | async-start | bytes 3145728 | tf_op jit(solution)/shard_map/all_to_all | solution.py:283
  186.2 4.0 %collective-permute-start.6 = (f32[2,128]{1,0:T(2,128)S(1)}, f32[2,128]{1,0:T(2,128)S(1)}, u32[]{:S(2)}, u32[]{:S(2)}) collective-permute-start(f32[2,128]{1,0:T(2,128)S(1)} %fusion.20), channel_id=1, source_target_pairs={{0,4},{1,5},{2,6},{3,7},{4,0},{5,1},{6,2},{7,3},{8,12},{9,13},{10,... | collective-permute-start | bytes 3080 | tf_op jit(solution)/shard_map/ppermute | solution.py:340
  190.2 2.4 collective-permute-start.7
  192.6 4.2 %collective-permute-start.8 = (f32[2,128]{1,0:T(2,128)S(1)}, f32[2,128]{1,0:T(2,128)S(1)}, u32[]{:S(2)}, u32[]{:S(2)}) collective-permute-start(f32[2,128]{1,0:T(2,128)S(1)} %add.62), channel_id=1, source_target_pairs={{0,128},{8,136},{16,144},{24,152},{32,160},{40,168},{48,176},{56,1... | collective-permute-start | bytes 3080 | tf_op jit(solution)/shard_map/ppermute | solution.py:340
  196.9 19.8 %collective-permute-start.9 = (f32[2,128]{1,0:T(2,128)S(1)}, f32[2,128]{1,0:T(2,128)S(1)}, u32[]{:S(2)}, u32[]{:S(2)}) collective-permute-start(f32[2,128]{1,0:T(2,128)S(1)} %add.63), channel_id=1, source_target_pairs={{0,8},{8,0},{16,24},{24,16},{32,40},{40,32},{48,56},{56,48},{64,72... | collective-permute-start | bytes 3080 | tf_op jit(solution)/shard_map/ppermute | solution.py:340
  216.7 18.1 %collective-permute-start.10 = (f32[2,128]{1,0:T(2,128)S(1)}, f32[2,128]{1,0:T(2,128)S(1)}, u32[]{:S(2)}, u32[]{:S(2)}) collective-permute-start(f32[2,128]{1,0:T(2,128)S(1)} %add.64), channel_id=1, source_target_pairs={{0,16},{8,24},{16,0},{24,8},{32,48},{40,56},{48,32},{56,40},{64,80... | collective-permute-start | bytes 3080 | tf_op jit(solution)/shard_map/ppermute | solution.py:340
  220.6 17.6 %copy-start.13 = (bf16[256,1024]{1,0:T(8,128)(2,1)S(1)}, bf16[256,1024]{1,0:T(8,128)(2,1)}, u32[]{:S(2)}) copy-start(bf16[256,1024]{1,0:T(8,128)(2,1)} %param.14) | copy-start | bytes 1572868
  234.7 6.4 %collective-permute-start.11 = (f32[2,128]{1,0:T(2,128)S(1)}, f32[2,128]{1,0:T(2,128)S(1)}, u32[]{:S(2)}, u32[]{:S(2)}) collective-permute-start(f32[2,128]{1,0:T(2,128)S(1)} %add.65), channel_id=1, source_target_pairs={{0,32},{8,40},{16,48},{24,56},{32,0},{40,8},{48,16},{56,24},{64,96... | collective-permute-start | bytes 3080 | tf_op jit(solution)/shard_map/ppermute | solution.py:340
  (11 other events, 24.9 us)

commit v2 on v1

--- a/solution.py
+++ b/solution.py
@@ -11,6 +11,7 @@
 SPAN = 4
 ROW = 8
 TOK = 256
+EXT = TOK + TAPS
 NEG = -1e30
 STEP = 4
 SCALE = HD ** (-0.5)
@@ -61,27 +62,6 @@
     )(*arrays)
 
 
-def pack_grad_kernel(q_ref, mixed_grad_ref, key_ref, out_ref):
-    attn_grad = mixed_grad_ref[...] * key_ref[...].astype(jnp.float32)
-    attn_grad = attn_grad.astype(jnp.bfloat16)
-    for head in range(out_ref.shape[0]):
-        lanes = slice(head * HD, (head + 1) * HD)
-        out_ref[head, :TOK] = q_ref[:, lanes]
-        out_ref[head, TOK:] = attn_grad[:, lanes]
-
-
-def pack_grad(q, mixed_grad, key):
-    heads = key.shape[1] // HD
-    return pl.pallas_call(
-        pack_grad_kernel,
-        grid=(heads // STEP,),
-        in_specs=[pl.BlockSpec((TOK, STEP * HD), lambda h: (0, h))] * 3,
-        out_specs=pl.BlockSpec((STEP, 2 * TOK, HD), lambda h: (h, 0, 0)),
-        out_shape=jax.ShapeDtypeStruct((heads, 2 * TOK, HD), key.dtype),
-        name="pack_grad",
-    )(q, mixed_grad, key)
-
-
 def unpack_kernel(x_ref, *out_refs):
     for head in range(x_ref.shape[0]):
         for n, out_ref in enumerate(out_refs):
@@ -101,6 +81,117 @@
     )(x)
 
 
+def spread(tile_refs, ext_s, sh_s):
+    at = 0
+    for piece in tile_refs:
+        ext_s[at : at + piece.shape[0]] = piece.astype(jnp.float32)
+        at += piece.shape[0]
+    ext_s[at:] = jnp.zeros((8, HD), jnp.float32)
+    for r in range(8):
+        sh_s[r] = ext_s[pl.ds(r, EXT)]
+
+
+def head_anti_kernel(cur_ref, next_ref, edge_ref, w_ref, out_ref, ext_s, sh_s, w_s):
+    last = pl.program_id(0) == ROW - 1
+    after = jnp.where(last, edge_ref[...].astype(jnp.float32), next_ref[0].astype(jnp.float32))
+    spread((cur_ref[0], after), ext_s, sh_s)
+    w_s[...] = w_ref[...].astype(jnp.float32)
+    rows = TOK // 2
+    for half in range(2):
+
+        def group(k, total, half=half):
+            taps = w_s[pl.ds(pl.multiple_of(k * 8, 8), 8)]
+            start = pl.multiple_of(k * 8 + half * rows, 8)
+            for r in range(8):
+                total = total + taps[r : r + 1] * sh_s[r, pl.ds(start, rows)]
+            return total
+
+        out_ref[0, half * rows : (half + 1) * rows] = lax.fori_loop(
+            0, TAPS // 8, group, jnp.zeros((rows, HD), jnp.float32)
+        )
+
+
+def head_anti(packed, edge, weights):
+    return pl.pallas_call(
+        head_anti_kernel,
+        grid=(ROW,),
+        in_specs=[
+            pl.BlockSpec((1, TOK, HD), lambda b: (b, 0, 0)),
+            pl.BlockSpec((1, TAPS, HD), lambda b: (jnp.minimum(b + 1, ROW - 1), 0, 0)),
+            pl.BlockSpec((TAPS, HD), lambda b: (0, 0)),
+            pl.BlockSpec((TAPS, HD), lambda b: (0, 0)),
+        ],
+        out_specs=pl.BlockSpec((1, TOK, HD), lambda b: (b, 0, 0)),
+        out_shape=jax.ShapeDtypeStruct((ROW, TOK, HD), jnp.float32),
+        scratch_shapes=[
+            pltpu.VMEM((EXT + 8, HD), jnp.float32),
+            pltpu.VMEM((8, EXT, HD), jnp.float32),
+            pltpu.VMEM((TAPS, HD), jnp.float32),
+        ],
+        name="head_anti",
+    )(packed, packed, edge, weights)
+
+
+def head_corr_kernel(cur_ref, prev_ref, edge_ref, g_ref, out_ref, ext_s, sh_s, g_s, part_s):
+    block = pl.program_id(0)
+    before = jnp.where(
+        block == 0, edge_ref[...].astype(jnp.float32), prev_ref[0].astype(jnp.float32)
+    )
+    spread((before, cur_ref[0]), ext_s, sh_s)
+    g_s[...] = g_ref[0].astype(jnp.float32)
+
+    @pl.when(block == 0)
+    def _():
+        part_s[...] = jnp.zeros_like(part_s)
+
+    rows = TOK // 2
+
+    def half_of(half, _):
+        base = pl.multiple_of(half * rows, rows)
+        g = [g_s[pl.ds(base + 8 * i, 8)] for i in range(rows // 8)]
+        for r in range(8):
+            for group in range(2):
+                low = (72 if r == 0 else 64) - 64 * group
+                piece = [
+                    sh_s[(8 - r) % 8, pl.ds(base + low + 8 * i, 8)] for i in range(rows // 8 + 7)
+                ]
+                for kk in range(8):
+                    total = g[0] * piece[7 - kk]
+                    for i in range(1, rows // 8):
+                        total = total + g[i] * piece[i + 7 - kk]
+                    part_s[r, 8 * group + kk] += total
+        return 0
+
+    lax.fori_loop(0, 2, half_of, 0)
+
+    @pl.when(block == ROW - 1)
+    def _():
+        for r in range(8):
+            out_ref[pl.ds(r, TAPS // 8, stride=8)] = jnp.sum(part_s[r], 1)
+
+
+def head_corr(mixed, edge, packed):
+    return pl.pallas_call(
+        head_corr_kernel,
+        grid=(ROW,),
+        in_specs=[
+            pl.BlockSpec((1, TOK, HD), lambda b: (b, 0, 0)),
+            pl.BlockSpec((1, TAPS, HD), lambda b: (jnp.maximum(b - 1, 0), 1, 0)),
+            pl.BlockSpec((TAPS, HD), lambda b: (0, 0)),
+            pl.BlockSpec((1, TOK, HD), lambda b: (b, 0, 0)),
+        ],
+        out_specs=pl.BlockSpec((TAPS, HD), lambda b: (0, 0)),
+        out_shape=jax.ShapeDtypeStruct((TAPS, HD), jnp.float32),
+        scratch_shapes=[
+            pltpu.VMEM((EXT + 8, HD), jnp.float32),
+            pltpu.VMEM((8, EXT, HD), jnp.float32),
+            pltpu.VMEM((TOK, HD), jnp.float32),
+            pltpu.VMEM((8, TAPS // 8, 8, HD), jnp.float32),
+        ],
+        name="head_corr",
+    )(mixed, mixed, edge, packed)
+
+
 def dot_nn(a, b):
     return jnp.dot(a, b, preferred_element_type=jnp.float32)
 
@@ -110,11 +201,13 @@
     return first, pl.ds(pl.multiple_of(first * TOK, TOK), width * TOK)
 
 
-def key_blocks(kv_ref, kvh_ref):
+def key_blocks(packed_ref, kvh_ref):
     for b in range(SPAN + ROW):
-        src = kvh_ref if b < SPAN else kv_ref
+        src = kvh_ref if b < SPAN else packed_ref
         at = b if b < SPAN else b - SPAN
-        yield b, slice(b * TOK, (b + 1) * TOK), src[at, :TOK], src[at, TOK:]
+        skip = 0 if b < SPAN else TOK
+        k = src[at, skip : skip + TOK]
+        yield b, slice(b * TOK, (b + 1) * TOK), k, src[at, skip + TOK :]
 
 
 def masked_scores(k, q, kdoc, qdoc, width):
@@ -131,19 +224,20 @@
 
 
 def fwd_kernel(
-    width_ref, kv_ref, kvh_ref, kdoc_ref, qdoc_ref, qg_ref, out_ref, top_ref, inv_ref, k_s, vt_s
+    width_ref, packed_ref, kvh_ref, kdoc_ref, qdoc_ref, qk_ref,
+    out_ref, mixed_ref, top_ref, inv_ref, k_s, vt_s,
 ):
     block = pl.program_id(0)
 
     @pl.when(block == 0)
     def _():
-        for b, rows, k, v in key_blocks(kv_ref, kvh_ref):
+        for b, rows, k, v in key_blocks(packed_ref, kvh_ref):
             k_s[rows] = k
             vt_s[b] = v.T
 
     def attend(width):
         first, rows = window_of(block, width)
-        q = qg_ref[0, :TOK]
+        q = qk_ref[0, :TOK]
         vt = jnp.concatenate([vt_s[first + n] for n in range(width)], 1)
         scores = masked_scores(k_s[rows], q, kdoc_ref[rows], qdoc_ref[0], width)
         top = jnp.max(scores, 0, keepdims=True)
@@ -152,20 +246,24 @@
         top_ref[0] = top
         inv_ref[0] = inv
         probs = (weights * inv).astype(jnp.bfloat16)
-        out_ref[0] = dot_nn(vt, probs).astype(jnp.bfloat16).T
+        out = dot_nn(vt, probs).astype(jnp.bfloat16).T
+        out_ref[0] = out
+        key = qk_ref[0, TOK:].astype(jnp.float32)
+        mixed_ref[0] = (key * out.astype(jnp.float32)).astype(jnp.bfloat16)
 
     by_width(width_ref, block, attend)
 
 
 def bwd_kernel(
-    width_ref, kv_ref, kvh_ref, kdoc_ref, qdoc_ref, qg_ref, out_ref, top_ref, inv_ref,
+    width_ref, packed_ref, kvh_ref, kdoc_ref, qdoc_ref, qk_ref, mixed_grad_ref,
+    out_ref, top_ref, inv_ref,
     dq_ref, dkv_lo_ref, dkv_hi_ref, dkvh_ref, k_s, v_s, kt_s, dk_s, dv_s,
 ):
     block = pl.program_id(0)
 
     @pl.when(block == 0)
     def _():
-        for b, rows, k, v in key_blocks(kv_ref, kvh_ref):
+        for b, rows, k, v in key_blocks(packed_ref, kvh_ref):
             k_s[rows] = k
             v_s[rows] = v
             kt_s[b] = k.T
@@ -174,8 +272,9 @@
 
     def attend(width):
         first, rows = window_of(block, width)
-        q = qg_ref[0, :TOK]
-        grad = qg_ref[0, TOK:]
+        q = qk_ref[0, :TOK]
+        key = qk_ref[0, TOK:].astype(jnp.float32)
+        grad = (mixed_grad_ref[0] * key).astype(jnp.bfloat16)
         grad_t = grad.T
         kt = jnp.concatenate([kt_s[first + n] for n in range(width)], 1)
         scores = masked_scores(k_s[rows], q, kdoc_ref[rows], qdoc_ref[0], width)
@@ -214,7 +313,7 @@
 
 
 SHARED_SPECS = [
-    whole(ROW, 2 * TOK, HD),
+    whole(ROW, 3 * TOK, HD),
     whole(SPAN, 2 * TOK, HD),
     whole(KEYS, HD),
     each(1, TOK),
@@ -229,7 +328,7 @@
             num_scalar_prefetch=1,
             grid=(ROW,),
             in_specs=SHARED_SPECS,
-            out_specs=[each(TOK, HD), each(1, TOK), each(1, TOK)],
+            out_specs=[each(TOK, HD), each(TOK, HD), each(1, TOK), each(1, TOK)],
             scratch_shapes=[
                 pltpu.VMEM((KEYS, HD), jnp.bfloat16),
                 pltpu.VMEM((SPAN + ROW, HD, TOK), jnp.bfloat16),
@@ -237,6 +336,7 @@
         ),
         out_shape=[
             jax.ShapeDtypeStruct((ROW, TOK, HD), jnp.bfloat16),
+            jax.ShapeDtypeStruct((ROW, TOK, HD), jnp.bfloat16),
             jax.ShapeDtypeStruct((ROW, 1, TOK), jnp.float32),
             jax.ShapeDtypeStruct((ROW, 1, TOK), jnp.float32),
         ],
@@ -251,7 +351,7 @@
         grid_spec=pltpu.PrefetchScalarGridSpec(
             num_scalar_prefetch=1,
             grid=(ROW,),
-            in_specs=SHARED_SPECS + [each(TOK, HD), each(1, TOK), each(1, TOK)],
+            in_specs=SHARED_SPECS + [each(TOK, HD), each(TOK, HD), each(1, TOK), each(1, TOK)],
             out_specs=[each(TOK, HD)] + [whole(SPAN, 2 * TOK, HD)] * 3,
             scratch_shapes=[
                 pltpu.VMEM((KEYS, HD), jnp.bfloat16),
@@ -296,23 +396,31 @@
     kdoc = jnp.broadcast_to(docs.reshape(-1, 1), ((SPAN + ROW) * TOK, HD))
     qdoc = docs[SPAN:].reshape(ROW, 1, TOK)
 
-    kv = swap(pack(keys_in, values_in))
-
     conv_grad = (out_grad.astype(jnp.float32) * gate_branch.astype(jnp.float32)).astype(
         jnp.bfloat16
     )
     grad_edge = shift(conv_grad[:TAPS], -1)
+    packed = swap(pack(conv_grad, keys_in, values_in))
     mixed_grad = anti_conv(
         jnp.concatenate([conv_grad, grad_edge[: TAPS - 1]], 0), mr_filter
     )
-    kvh = shift(kv[ROW - SPAN :], ROW)
-    qg = swap(pack_grad(queries_in, mixed_grad, key_branch))
-
-    shared = (widths, kv, kvh, kdoc, qdoc, qg)
-    attn_head, top, inv = attention_fwd(*shared)
+    qk = swap(pack(queries_in, key_branch))
+
+    kvh = shift(packed[ROW - SPAN :, TOK:], ROW)
+    head_edge = shift(packed[0, :TAPS], -ROW)
+    head = position % ROW
+    own_taps = lax.dynamic_slice_in_dim(mr_filter, head * HD, HD, 1)
+    mixed_grad_head = head_anti(packed, head_edge, own_taps)
+
+    shared = (widths, packed, kvh, kdoc, qdoc, qk)
+    attn_head, mixed_head, top, inv = attention_fwd(*shared)
     attn_out = unpack(swap(attn_head))[0]
-    dq_head, dkv_lo, dkv_hi, dkvh = attention_bwd(*shared, attn_head, top, inv)
+    mixed_before = shift(mixed_head[ROW - 1, TOK - TAPS :], ROW)
+    dq_head, dkv_lo, dkv_hi, dkvh = attention_bwd(
+        *shared, mixed_grad_head, attn_head, top, inv
+    )
     back = shift(dkvh, -ROW)
+    filter_part = head_corr(mixed_head, mixed_before, packed)
     dkv_hi = (dkv_hi + back.astype(jnp.float32)).astype(jnp.bfloat16)
     dqkv = jnp.concatenate([dq_head, jnp.concatenate([dkv_lo, dkv_hi], 0)], 1)
     query_grad, key_grad, value_grad = unpack(swap(dqkv))
@@ -320,24 +428,38 @@
     mixed = (key_branch.astype(jnp.float32) * attn_out.astype(jnp.float32)).astype(jnp.bfloat16)
     mixed_edge = shift(mixed[TOK - TAPS :], 1)
     mixed_ext = jnp.concatenate([mixed_edge[1:], mixed], 0)
-    filter_part = anti_conv(mixed_ext, conv_grad)
     conv_out = causal_conv(mixed_ext, mr_filter)
     gate_grad = (out_grad.astype(jnp.float32) * conv_out).astype(jnp.bfloat16)
     branch_grad = (mixed_grad * attn_out.astype(jnp.float32)).astype(jnp.bfloat16)
 
+    def meet(x, axis, hop):
+        pairs = [(i, i ^ hop) for i in range(lax.axis_size(axis))]
+        return x + lax.ppermute(x, axis, pairs)
+
+    rings_n = n_seq // ROW
+    filter_grad = filter_part
+    hop = ROW
+    while hop < n_seq:
+        filter_grad = meet(filter_grad, "seq", hop)
+        hop *= 2
+    tap_share = TAPS // ROW
+    own_filter = lax.dynamic_slice_in_dim(mr_filter, head * tap_share, tap_share, 0)
+    norms = jnp.stack(
+        [jnp.sum(jnp.square(own_filter.astype(jnp.float32))), jnp.sum(filter_grad * filter_grad)]
+    )
+    norms = jnp.broadcast_to(norms[:, None], (2, HD))
+    hop = 1
+    while hop < lax.axis_size("ch"):
+        norms = meet(norms, "ch", hop)
+        hop *= 2
     tap_rows = TAPS // n_seq
-    parts = jnp.flip(filter_part, 0).astype(jnp.bfloat16)
-    parts = swap(parts.reshape(n_seq, tap_rows, -1), None)
-    own_grad = jnp.sum(parts.astype(jnp.float32), 0)
-    own_filter = lax.dynamic_slice_in_dim(mr_filter, position * tap_rows, tap_rows, 0)
-    norms = jnp.stack(
-        [jnp.sum(jnp.square(own_filter.astype(jnp.float32))), jnp.sum(own_grad * own_grad)]
-    )
-    norms = jnp.broadcast_to(norms[:, None], (2, HD))
-    hops = [("ch", 1), ("ch", 2), ("ch", 4)] + [("seq", h) for h in (8, 16, 1, 2, 4)]
-    for axis, hop in hops:
-        pairs = [(i, i ^ hop) for i in range(lax.axis_size(axis))]
-        norms = norms + lax.ppermute(norms, axis, pairs)
+    ring_taps = lax.dynamic_slice_in_dim(
+        filter_grad, (position // ROW) * (TAPS // rings_n), TAPS // rings_n, 0
+    ).reshape(ROW, tap_rows, HD)
+    sent = jnp.concatenate([ring_taps, jnp.broadcast_to(norms[None], (ROW, 2, HD))], 1)
+    got = swap(sent)
+    own_grad = jnp.swapaxes(got[:, :tap_rows], 0, 1).reshape(tap_rows, ROW * HD)
+    norms = jnp.sum(got[:, tap_rows:], 0)
     trust = jnp.sqrt(norms[0, 0]) / jnp.sqrt(norms[1, 0] + 1e-06)
     filter_step = trust * own_grad
     return (query_grad, key_grad, value_grad, gate_grad, branch_grad, filter_step)

time: 251 us -> 276 us (1.100)
  the two profiles are of different devices: /device:TPU:1 before, /device:TPU:6 now
where the time goes in v2:
time: 276 us; the launch traced here: 275 us
  waiting for transfers between devices  105 us (38%)
  starting transfers between devices  52.4 us (19%)
  Pallas kernels  48.8 us (18%)
  matrix products  30 us (11%)
  local copies, waits for them, and re-layouts  23 us (8%)
  other arithmetic  13.2 us (5%)
    all_to_all x5, waiting for transfers between devices, swap(): return lax.all_to_all(x, axis, 0, 0, axis_index_groups=groups, tiled=True)  64.3 us
    ppermute x6, waiting for transfers between devices, shift(): return lax.ppermute(x, 'seq', pairs)  34.1 us
    all_to_all x5, starting transfers between devices, swap(): return lax.all_to_all(x, axis, 0, 0, axis_index_groups=groups, tiled=True)  29.7 us
    unnamed x61, local copies, waits for them, and re-layouts  16.9 us
    conv_general_dilated x1, matrix products, anti_conv(): lax.conv_general_dilated(extended[None], weights_in[:, None, :], (1,), 'V...  15.8 us
    ppermute x6, starting transfers between devices, shift(): return lax.ppermute(x, 'seq', pairs)  15 us
    conv_general_dilated x1, matrix products, causal_conv(): lax.conv_general_dilated(extended[None], kernel, (1,), 'VALID', dimension...  14.2 us
    pallas_call x1, Pallas kernels, head_anti(): pl.pallas_call(head_anti_kernel, grid=(ROW,), in_specs=[pl.BlockSpec((1,...  13.1 us
  transfers between devices with their start and end apart: 16, of which 7 were waited for; matrix products, arithmetic and copies ran while one was open for 17% of the time, Pallas kernels for 9%

profile of v2, /device:TPU:6, one launch (start us, length us, event | category | flops | bytes accessed | tf_op | source)
XLA Modules:
  0.0 274.8 jit_solution(6539453549564492480)
XLA Ops:
  2.8 2.4 pack.2
  5.2 8.5 %all-to-all-start = ((bf16[8,768,128]{2,1,0:T(8,128)(2,1)}), bf16[8,768,128]{2,1,0:T(8,128)(2,1)S(1)}, u32[]{:S(2)}, u32[]{:S(2)}) async-start(bf16[8,768,128]{2,1,0:T(8,128)(2,1)} %pack.2), calls=%async_computation | async-start | bytes 3145728 | tf_op jit(solution)/shard_map/all_to_all | solution.py:383
  15.8 37.9 %all-to-all-done.cur_ref.next_ref.packed_ref.g_ref = bf16[8,768,128]{2,1,0:T(8,128)(2,1)S(1)} async-done(((bf16[8,768,128]{2,1,0:T(8,128)(2,1)}), bf16[8,768,128]{2,1,0:T(8,128)(2,1)S(1)}, u32[]{:S(2)}, u32[]{:S(2)}) %all-to-all-start) | async-done | bytes 1572896 | tf_op jit(solution)/shard_map/all_to_all | solution.py:383
  53.7 3.6 %all-to-all-start.1 = ((bf16[8,512,128]{2,1,0:T(8,128)(2,1)}), bf16[8,512,128]{2,1,0:T(8,128)(2,1)S(1)}, u32[]{:S(2)}, u32[]{:S(2)}) async-start(bf16[8,512,128]{2,1,0:T(8,128)(2,1)} %pack.3), calls=%async_computation.1 | async-start | bytes 2097152 | tf_op jit(solution)/shard_map/all_to_all | solution.py:383
  59.9 26.5 %all-to-all-done.1.qk_ref = bf16[8,512,128]{2,1,0:T(8,128)(2,1)S(1)} async-done(((bf16[8,512,128]{2,1,0:T(8,128)(2,1)}), bf16[8,512,128]{2,1,0:T(8,128)(2,1)S(1)}, u32[]{:S(2)}, u32[]{:S(2)}) %all-to-all-start.1) | async-done | bytes 1048608 | tf_op jit(solution)/shard_map/all_to_all | solution.py:383
  90.4 7.0 %attn_fwd.1 = (bf16[8,256,128]{2,1,0:T(8,128)(2,1)S(1)}, bf16[8,256,128]{2,1,0:T(8,128)(2,1)S(1)}, f32[8,1,256]{2,1,0:T(1,128)S(1)}, f32[8,1,256]{2,1,0:T(1,128)S(1)}) custom-call(s32[8]{0:T(128)S(1)} %fusion.15.width_ref, bf16[8,768,128]{2,1,0:T(8,128)(2,1)S(1)} %all-to-all-done.cur_ref.next_ref.packed_ref.g_ref, bf16[4,512,128]{2,1,0:T(8,128)(2,1)S(1)} %copy-done.8, ...), custom_call_target="tpu_custom_call" | custom-call | tf_op jit(solution)/shard_map/attn_fwd/pallas_call | solution.py:325
  100.5 4.5 %collective-permute-done.5.edge_ref = bf16[128,128]{1,0:T(8,128)(2,1)S(1)} collective-permute-done((bf16[128,128]{1,0:T(8,128)(2,1)S(1)}, bf16[128,128]{1,0:T(8,128)(2,1)S(1)}, u32[]{:S(2)}, u32[]{:S(2)}) %collective-permute-start.5) | collective-permute-done | bytes 32800 | tf_op jit(solution)/shard_map/ppermute | solution.py:387
  105.6 11.9 %head_corr.1 = f32[128,128]{1,0:T(8,128)} custom-call(bf16[8,256,128]{2,1,0:T(8,128)(2,1)} %copy-done.6, bf16[8,256,128]{2,1,0:T(8,128)(2,1)} %copy-done.6, bf16[128,128]{1,0:T(8,128)(2,1)} %copy-done.27, bf16[8,768,128]{2,1,0:T(8,128)(2,1)} %copy-done), custom_call_target="tpu_custom_call" | custom-call | tf_op jit(solution)/shard_map/head_corr/pallas_call | solution.py:174
  118.8 3.2 %collective-permute-done.6 = f32[128,128]{1,0:T(8,128)S(1)} collective-permute-done((f32[128,128]{1,0:T(8,128)}, f32[128,128]{1,0:T(8,128)S(1)}, u32[]{:S(2)}, u32[]{:S(2)}) %collective-permute-start.6) | collective-permute-done | bytes 65568 | tf_op jit(solution)/shard_map/ppermute | solution.py:437
  131.4 2.6 rev.4
  136.4 3.2 %collective-permute-start.1 = (bf16[128,128]{1,0:T(8,128)(2,1)S(1)}, bf16[128,128]{1,0:T(8,128)(2,1)S(1)}, u32[]{:S(2)}, u32[]{:S(2)}) collective-permute-start(bf16[128,128]{1,0:T(8,128)(2,1)S(1)} %slice_bitcast_fusion), channel_id=1, source_target_pairs={{64,0},{72,8},{80,16},{88,24},{96,32},{104,40},{112,48},{120,56},{... | collective-permute-start | bytes 98312 | tf_op jit(solution)/shard_map/ppermute | solution.py:387
  139.7 2.9 %collective-permute-start.10 = (f32[2,128]{1,0:T(2,128)S(1)}, f32[2,128]{1,0:T(2,128)S(1)}, u32[]{:S(2)}, u32[]{:S(2)}) collective-permute-start(f32[2,128]{1,0:T(2,128)S(1)} %fusion.18), channel_id=1, source_target_pairs={{0,4},{1,5},{2,6},{3,7},{4,0},{5,1},{6,2},{7,3},{8,12},{9,13},{10,... | collective-permute-start | bytes 3080 | tf_op jit(solution)/shard_map/ppermute | solution.py:437
  145.4 3.5 %all-to-all-start.4 = ((f32[8,6,128]{2,1,0:T(8,128)}), f32[8,6,128]{2,1,0:T(8,128)S(1)}, u32[]{:S(2)}, u32[]{:S(2)}) async-start(f32[8,6,128]{2,1,0:T(8,128)} %pad_maximum_fusion), calls=%async_computation.4 | async-start | bytes 65536 | tf_op jit(solution)/shard_map/all_to_all | solution.py:383
  150.5 13.1 %head_anti.1.mixed_grad_ref = f32[8,256,128]{2,1,0:T(8,128)} custom-call(bf16[8,768,128]{2,1,0:T(8,128)(2,1)} %copy-done, bf16[8,768,128]{2,1,0:T(8,128)(2,1)} %copy-done, bf16[128,128]{1,0:T(8,128)(2,1)} %copy-done.26, bf16[128,128]{1,0:T(8,128)(2,1)} %constant_dynamic-slice_fusion.1.w_ref), custom_call_target="tpu_custom_call" | custom-call | tf_op jit(solution)/shard_map/head_anti/pallas_call | solution.py:115
  168.1 8.1 %attn_bwd.1 = (bf16[8,256,128]{2,1,0:T(8,128)(2,1)S(1)}, bf16[4,512,128]{2,1,0:T(8,128)(2,1)S(1)}, f32[4,512,128]{2,1,0:T(8,128)S(1)}, bf16[4,512,128]{2,1,0:T(8,128)(2,1)}) custom-call(s32[8]{0:T(128)S(1)} %fusion.15.width_ref, bf16[8,768,128]{2,1,0:T(8,128)(2,1)S(1)} %copy-done.1, bf16[4,512,128]{2,1,0:T(8,128)(2,1)S(1)} %copy-done.9, ...), custom_call_target="tpu_custom_call" | custom-call | tf_op jit(solution)/shard_map/attn_bwd/pallas_call | solution.py:349
  178.8 3.1 %collective-permute-start.2 = (bf16[4,512,128]{2,1,0:T(8,128)(2,1)}, bf16[4,512,128]{2,1,0:T(8,128)(2,1)S(1)}, u32[]{:S(2)}, u32[]{:S(2)}) collective-permute-start(bf16[4,512,128]{2,1,0:T(8,128)(2,1)} %get-tuple-element.23), channel_id=1, source_target_pairs={{64,0},{72,8},{80,16},{88,24},{96,32},{104,40},{112,48},{120,56},{... | collective-permute-start | bytes 1572872 | tf_op jit(solution)/shard_map/ppermute | solution.py:387
  181.9 7.0 %all-to-all-start.3 = ((bf16[8,256,128]{2,1,0:T(8,128)(2,1)}), bf16[8,256,128]{2,1,0:T(8,128)(2,1)S(1)}, u32[]{:S(2)}, u32[]{:S(2)}) async-start(bf16[8,256,128]{2,1,0:T(8,128)(2,1)} %copy-done.10), calls=%async_computation.3 | async-start | bytes 1048576 | tf_op jit(solution)/shard_map/all_to_all | solution.py:383
  188.9 15.8 %fusion = f32[1,256,1024]{2,0,1:T(1,128)} fusion(bf16[1,383,1024]{2,1,0:T(8,128)(2,1)} %maximum_bitcast_fusion.1, bf16[128,1,1024]{2,0,1:T(8,128)(2,1)S(1)} %bitcast.28), kind=kOutput, calls=%fused_computation.1 | convolution fusion | flops 67108864 | bytes 2095104 | tf_op jit(solution)/shard_map/conv_general_dilated | solution.py:34
  208.0 7.2 %all-to-all-start.2 = ((bf16[8,768,128]{2,1,0:T(8,128)(2,1)}), bf16[8,768,128]{2,1,0:T(8,128)(2,1)S(1)}, u32[]{:S(2)}, u32[]{:S(2)}) async-start(bf16[8,768,128]{2,1,0:T(8,128)(2,1)} %maximum_maximum_fusion), calls=%async_computation.2 | async-start | bytes 3145728 | tf_op jit(solution)/shard_map/all_to_all | solution.py:383
  217.0 2.6 fusion.7
  219.6 4.1 %collective-permute-start.3 = (bf16[128,1024]{1,0:T(8,128)(2,1)S(1)}, bf16[128,1024]{1,0:T(8,128)(2,1)S(1)}, u32[]{:S(2)}, u32[]{:S(2)}) collective-permute-start(bf16[128,1024]{1,0:T(8,128)(2,1)S(1)} %slice.90), channel_id=1, source_target_pairs={{0,8},{8,16},{16,24},{24,32},{32,40},{40,48},{48,56},{56,64},{64,7... | collective-permute-start | bytes 786440 | tf_op jit(solution)/shard_map/ppermute | solution.py:387
  226.2 29.6 %collective-permute-done.3 = bf16[128,1024]{1,0:T(8,128)(2,1)S(1)} collective-permute-done((bf16[128,1024]{1,0:T(8,128)(2,1)S(1)}, bf16[128,1024]{1,0:T(8,128)(2,1)S(1)}, u32[]{:S(2)}, u32[]{:S(2)}) %collective-permute-start.3) | collective-permute-done | bytes 262176 | tf_op jit(solution)/shard_map/ppermute | solution.py:387
  256.0 14.2 %fusion.2 = f32[1,256,1024]{2,0,1:T(1,128)S(1)} fusion(bf16[1,383,1024]{2,1,0:T(8,128)(2,1)S(1)} %maximum_bitcast_fusion, bf16[128,1,1024]{2,0,1:T(8,128)(2,1)S(1)} %bitcast.29), kind=kOutput, calls=%fused_computation.3 | convolution fusion | flops 67108864 | bytes 2095104 | tf_op jit(solution)/shard_map/conv_general_dilated | solution.py:22
  272.4 2.4 unpack.2
  (114 shorter events, 47.8 us)
Async XLA Ops:
  5.2 48.4 %all-to-all-start = ((bf16[8,768,128]{2,1,0:T(8,128)(2,1)}), bf16[8,768,128]{2,1,0:T(8,128)(2,1)S(1)}, u32[]{:S(2)}, u32[]{:S(2)}) async-start(bf16[8,768,128]{2,1,0:T(8,128)(2,1)} %pack.2), calls=%async_computation | async-start | bytes 3145728 | tf_op jit(solution)/shard_map/all_to_all | solution.py:383
  15.8 41.5 %copy-start.25 = (s32[8192]{0:T(1024)S(1)}, s32[8192]{0:T(1024)}, u32[]{:S(2)}) copy-start(s32[8192]{0:T(1024)} %param.15) | copy-start | bytes 98308
  53.7 35.0 %copy-start = (bf16[8,768,128]{2,1,0:T(8,128)(2,1)}, bf16[8,768,128]{2,1,0:T(8,128)(2,1)S(1)}, u32[]{:S(2)}) copy-start(bf16[8,768,128]{2,1,0:T(8,128)(2,1)S(1)} %all-to-all-done.cur_ref.next_ref.packed_ref.g_ref) | copy-start | bytes 4718596
  53.7 32.7 %all-to-all-start.1 = ((bf16[8,512,128]{2,1,0:T(8,128)(2,1)}), bf16[8,512,128]{2,1,0:T(8,128)(2,1)S(1)}, u32[]{:S(2)}, u32[]{:S(2)}) async-start(bf16[8,512,128]{2,1,0:T(8,128)(2,1)} %pack.3), calls=%async_computation.1 | async-start | bytes 2097152 | tf_op jit(solution)/shard_map/all_to_all | solution.py:383
  58.1 29.2 %collective-permute-start = (bf16[4,512,128]{2,1,0:T(8,128)(2,1)}, bf16[4,512,128]{2,1,0:T(8,128)(2,1)S(1)}, u32[]{:S(2)}, u32[]{:S(2)}) collective-permute-start(bf16[4,512,128]{2,1,0:T(8,128)(2,1)} %slice.88), channel_id=1, source_target_pairs={{0,64},{8,72},{16,80},{24,88},{32,96},{40,104},{48,112},{56,120},{... | collective-permute-start | bytes 1572872 | tf_op jit(solution)/shard_map/ppermute | solution.py:387
  98.3 26.5 %copy-start.18 = (bf16[256,1024]{1,0:T(8,128)(2,1)S(1)}, bf16[256,1024]{1,0:T(8,128)(2,1)}, u32[]{:S(2)}) copy-start(bf16[256,1024]{1,0:T(8,128)(2,1)} %fusion.4.refs_0_) | copy-start | bytes 1572868
  99.1 27.7 %copy-start.23 = (bf16[128,1024]{1,0:T(8,128)(2,1)S(1)}, bf16[128,1024]{1,0:T(8,128)(2,1)}, u32[]{:S(2)}) copy-start(bf16[128,1024]{1,0:T(8,128)(2,1)} %param.13) | copy-start | bytes 786436
  99.1 5.9 %collective-permute-start.5 = (bf16[128,128]{1,0:T(8,128)(2,1)S(1)}, bf16[128,128]{1,0:T(8,128)(2,1)S(1)}, u32[]{:S(2)}, u32[]{:S(2)}) collective-permute-start(bf16[128,128]{1,0:T(8,128)(2,1)S(1)} %slice_bitcast_fusion.1), channel_id=1, source_target_pairs={{0,64},{8,72},{16,80},{24,88},{32,96},{40,104},{48,112},{56,120},{... | collective-permute-start | bytes 98312 | tf_op jit(solution)/shard_map/ppermute | solution.py:387
  117.5 4.5 %collective-permute-start.6 = (f32[128,128]{1,0:T(8,128)}, f32[128,128]{1,0:T(8,128)S(1)}, u32[]{:S(2)}, u32[]{:S(2)}) collective-permute-start(f32[128,128]{1,0:T(8,128)} %head_corr.1), channel_id=1, source_target_pairs={{0,64},{8,72},{16,80},{24,88},{32,96},{40,104},{48,112},{56,120},{... | collective-permute-start | bytes 196616 | tf_op jit(solution)/shard_map/ppermute | solution.py:437
  122.9 5.9 %collective-permute-start.7 = (f32[128,128]{1,0:T(8,128)S(1)}, f32[128,128]{1,0:T(8,128)S(1)}, u32[]{:S(2)}, u32[]{:S(2)}) collective-permute-start(f32[128,128]{1,0:T(8,128)S(1)} %add.61), channel_id=1, source_target_pairs={{0,128},{8,136},{16,144},{24,152},{32,160},{40,168},{48,176},{56,1... | collective-permute-start | bytes 196616 | tf_op jit(solution)/shard_map/ppermute | solution.py:437
  124.8 24.1 %collective-permute-start.4 = (bf16[128,1024]{1,0:T(8,128)(2,1)S(1)}, bf16[128,1024]{1,0:T(8,128)(2,1)S(1)}, u32[]{:S(2)}, u32[]{:S(2)}) collective-permute-start(bf16[128,1024]{1,0:T(8,128)(2,1)S(1)} %slice.92), channel_id=1, source_target_pairs={{8,0},{16,8},{24,16},{32,24},{40,32},{48,40},{56,48},{64,56},{72,6... | collective-permute-start | bytes 786440 | tf_op jit(solution)/shard_map/ppermute | solution.py:387
  130.8 3.2 %collective-permute-start.8 = (f32[2,128]{1,0:T(2,128)S(1)}, f32[2,128]{1,0:T(2,128)S(1)}, u32[]{:S(2)}, u32[]{:S(2)}) collective-permute-start(f32[2,128]{1,0:T(2,128)S(1)} %broadcast_in_dim.35), channel_id=1, source_target_pairs={{0,1},{1,0},{2,3},{3,2},{4,5},{5,4},{6,7},{7,6},{8,9},{9,8},{10,11... | collective-permute-start | bytes 3080 | tf_op jit(solution)/shard_map/ppermute | solution.py:437
  134.1 5.5 %collective-permute-start.9 = (f32[2,128]{1,0:T(2,128)S(1)}, f32[2,128]{1,0:T(2,128)S(1)}, u32[]{:S(2)}, u32[]{:S(2)}) collective-permute-start(f32[2,128]{1,0:T(2,128)S(1)} %broadcast_add_fusion), channel_id=1, source_target_pairs={{0,2},{1,3},{2,0},{3,1},{4,6},{5,7},{6,4},{7,5},{8,10},{9,11},{10,... | collective-permute-start | bytes 3080 | tf_op jit(solution)/shard_map/ppermute | solution.py:437
  136.4 13.5 %collective-permute-start.1 = (bf16[128,128]{1,0:T(8,128)(2,1)S(1)}, bf16[128,128]{1,0:T(8,128)(2,1)S(1)}, u32[]{:S(2)}, u32[]{:S(2)}) collective-permute-start(bf16[128,128]{1,0:T(8,128)(2,1)S(1)} %slice_bitcast_fusion), channel_id=1, source_target_pairs={{64,0},{72,8},{80,16},{88,24},{96,32},{104,40},{112,48},{120,56},{... | collective-permute-start | bytes 98312 | tf_op jit(solution)/shard_map/ppermute | solution.py:387
  139.7 5.1 %collective-permute-start.10 = (f32[2,128]{1,0:T(2,128)S(1)}, f32[2,128]{1,0:T(2,128)S(1)}, u32[]{:S(2)}, u32[]{:S(2)}) collective-permute-start(f32[2,128]{1,0:T(2,128)S(1)} %fusion.18), channel_id=1, source_target_pairs={{0,4},{1,5},{2,6},{3,7},{4,0},{5,1},{6,2},{7,3},{8,12},{9,13},{10,... | collective-permute-start | bytes 3080 | tf_op jit(solution)/shard_map/ppermute | solution.py:437
  145.4 36.5 %all-to-all-start.4 = ((f32[8,6,128]{2,1,0:T(8,128)}), f32[8,6,128]{2,1,0:T(8,128)S(1)}, u32[]{:S(2)}, u32[]{:S(2)}) async-start(f32[8,6,128]{2,1,0:T(8,128)} %pad_maximum_fusion), calls=%async_computation.4 | async-start | bytes 65536 | tf_op jit(solution)/shard_map/all_to_all | solution.py:383
  149.9 13.7 %copy-start.1 = (bf16[8,768,128]{2,1,0:T(8,128)(2,1)S(1)}, bf16[8,768,128]{2,1,0:T(8,128)(2,1)}, u32[]{:S(2)}) copy-start(bf16[8,768,128]{2,1,0:T(8,128)(2,1)} %copy-done) | copy-start | bytes 4718596
  178.8 25.9 %collective-permute-start.2 = (bf16[4,512,128]{2,1,0:T(8,128)(2,1)}, bf16[4,512,128]{2,1,0:T(8,128)(2,1)S(1)}, u32[]{:S(2)}, u32[]{:S(2)}) collective-permute-start(bf16[4,512,128]{2,1,0:T(8,128)(2,1)} %get-tuple-element.23), channel_id=1, source_target_pairs={{64,0},{72,8},{80,16},{88,24},{96,32},{104,40},{112,48},{120,56},{... | collective-permute-start | bytes 1572872 | tf_op jit(solution)/shard_map/ppermute | solution.py:387
  181.9 25.3 %all-to-all-start.3 = ((bf16[8,256,128]{2,1,0:T(8,128)(2,1)}), bf16[8,256,128]{2,1,0:T(8,128)(2,1)S(1)}, u32[]{:S(2)}, u32[]{:S(2)}) async-start(bf16[8,256,128]{2,1,0:T(8,128)(2,1)} %copy-done.10), calls=%async_computation.3 | async-start | bytes 1048576 | tf_op jit(solution)/shard_map/all_to_all | solution.py:383
  188.9 15.9 %copy-start.13 = (f32[4,512,128]{2,1,0:T(8,128)S(1)}, f32[4,512,128]{2,1,0:T(8,128)}, u32[]{:S(2)}) copy-start(f32[4,512,128]{2,1,0:T(8,128)} %copy-done.12) | copy-start | bytes 3145732
  208.0 63.3 %all-to-all-start.2 = ((bf16[8,768,128]{2,1,0:T(8,128)(2,1)}), bf16[8,768,128]{2,1,0:T(8,128)(2,1)S(1)}, u32[]{:S(2)}, u32[]{:S(2)}) async-start(bf16[8,768,128]{2,1,0:T(8,128)(2,1)} %maximum_maximum_fusion), calls=%async_computation.2 | async-start | bytes 3145728 | tf_op jit(solution)/shard_map/all_to_all | solution.py:383
  219.6 36.4 %copy-start.24 = (bf16[128,1024]{1,0:T(8,128)(2,1)S(1)}, bf16[128,1024]{1,0:T(8,128)(2,1)}, u32[]{:S(2)}) copy-start(bf16[128,1024]{1,0:T(8,128)(2,1)} %rev.4) | copy-start | bytes 786436
  219.6 36.2 %collective-permute-start.3 = (bf16[128,1024]{1,0:T(8,128)(2,1)S(1)}, bf16[128,1024]{1,0:T(8,128)(2,1)S(1)}, u32[]{:S(2)}, u32[]{:S(2)}) collective-permute-start(bf16[128,1024]{1,0:T(8,128)(2,1)S(1)} %slice.90), channel_id=1, source_target_pairs={{0,8},{8,16},{16,24},{24,32},{32,40},{40,48},{48,56},{56,64},{64,7... | collective-permute-start | bytes 786440 | tf_op jit(solution)/shard_map/ppermute | solution.py:387
  256.0 14.2 %copy-start.20 = (bf16[256,1024]{1,0:T(8,128)(2,1)S(1)}, bf16[256,1024]{1,0:T(8,128)(2,1)}, u32[]{:S(2)}) copy-start(bf16[256,1024]{1,0:T(8,128)(2,1)} %param.14) | copy-start | bytes 1572868
  (20 other events, 28.0 us)

commit v3 on v2

--- a/solution.py
+++ b/solution.py
@@ -15,19 +15,7 @@
 NEG = -1e30
 STEP = 4
 SCALE = HD ** (-0.5)
-
-
-def causal_conv(extended, weights_in):
-    kernel = jnp.flip(weights_in, 0)[:, None, :]
-    return lax.conv_general_dilated(
-        extended[None],
-        kernel,
-        (1,),
-        "VALID",
-        dimension_numbers=("NWC", "WIO", "NWC"),
-        feature_group_count=extended.shape[1],
-        preferred_element_type=jnp.float32,
-    )[0]
+PIECES = 4
 
 
 def anti_conv(extended, weights_in):
@@ -42,6 +30,10 @@
     )[0]
 
 
+def hbm(*arrays):
+    return [pltpu.with_memory_space_constraint(x, pltpu.HBM) for x in arrays]
+
+
 def pack_kernel(*refs):
     *in_refs, out_ref = refs
     for head in range(out_ref.shape[0]):
@@ -57,7 +49,7 @@
         grid=(heads // STEP,),
         in_specs=[pl.BlockSpec((TOK, STEP * HD), lambda h: (0, h))] * n,
         out_specs=pl.BlockSpec((STEP, n * TOK, HD), lambda h: (h, 0, 0)),
-        out_shape=jax.ShapeDtypeStruct((heads, n * TOK, HD), arrays[0].dtype),
+        out_shape=pltpu.HBM((heads, n * TOK, HD), arrays[0].dtype),
         name="pack",
     )(*arrays)
 
@@ -78,7 +70,49 @@
         out_specs=[pl.BlockSpec((TOK, STEP * HD), lambda h: (0, h))] * n,
         out_shape=[jax.ShapeDtypeStruct((TOK, heads * HD), x.dtype)] * n,
         name="unpack",
-    )(x)
+    )(*hbm(x))
+
+
+def finish_kernel(x_ref, key_ref, mixed_grad_ref, mixed_ref, branch_ref):
+    for head in range(x_ref.shape[0]):
+        lanes = slice(head * HD, (head + 1) * HD)
+        attn_out = x_ref[head].astype(jnp.float32)
+        mixed_ref[:, lanes] = (key_ref[:, lanes].astype(jnp.float32) * attn_out).astype(
+            jnp.bfloat16
+        )
+        branch_ref[:, lanes] = (mixed_grad_ref[:, lanes] * attn_out).astype(jnp.bfloat16)
+
+
+def finish(attn_out, key, mixed_grad):
+    heads = attn_out.shape[0]
+    column = pl.BlockSpec((TOK, STEP * HD), lambda h: (0, h))
+    shape = jax.ShapeDtypeStruct((TOK, heads * HD), jnp.bfloat16)
+    return pl.pallas_call(
+        finish_kernel,
+        grid=(heads // STEP,),
+        in_specs=[pl.BlockSpec((STEP, TOK, HD), lambda h: (h, 0, 0)), column, column],
+        out_specs=[column] * 2,
+        out_shape=[shape] * 2,
+        name="finish",
+    )(*hbm(attn_out), key, mixed_grad)
+
+
+def join_kernel(joined_ref, own_ref, back_ref, out_ref):
+    out_ref[...] = (own_ref[...] + back_ref[...].astype(jnp.float32)).astype(jnp.bfloat16)
+
+
+def join(joined, own, back):
+    part = pl.BlockSpec((2, 2 * TOK, HD), lambda b: (b, 0, 0))
+    first = (ROW - SPAN) // 2
+    return pl.pallas_call(
+        join_kernel,
+        grid=(SPAN // 2,),
+        in_specs=[pl.BlockSpec(memory_space=pl.ANY), part, part],
+        out_specs=pl.BlockSpec((2, 2 * TOK, HD), lambda b: (b + first, 0, 0)),
+        out_shape=pltpu.HBM(joined.shape, joined.dtype),
+        input_output_aliases={0: 0},
+        name="join",
+    )(*hbm(joined, own, back))
 
 
 def spread(tile_refs, ext_s, sh_s):
@@ -91,24 +125,66 @@
         sh_s[r] = ext_s[pl.ds(r, EXT)]
 
 
+HALF = TOK // 2
+
+
+def ahead(k, r):
+    return r, k * 8
+
+
+def behind(k, r):
+    return ((8 - r) % 8, TAPS - 8 - k * 8) if r else (0, TAPS - k * 8)
+
+
+def filtered(sh_s, w_s, where, half):
+    def group(k, total):
+        taps = w_s[pl.ds(pl.multiple_of(k * 8, 8), 8)]
+        for r in range(8):
+            slot, start = where(k, r)
+            start = pl.multiple_of(start + half * HALF, 8)
+            total = total + taps[r : r + 1] * sh_s[slot, pl.ds(start, HALF)]
+        return total
+
+    return lax.fori_loop(0, TAPS // 8, group, jnp.zeros((HALF, HD), jnp.float32))
+
+
+def causal_kernel(m_ref, edge_ref, w_ref, grad_ref, *refs):
+    out_ref, ext_s, sh_s, w_s = refs[-4:]
+    spread((edge_ref[...], m_ref[...]), ext_s, sh_s)
+    w_s[...] = w_ref[...].astype(jnp.float32)
+    for half in range(2):
+        rows = slice(half * HALF, (half + 1) * HALF)
+        conv_out = filtered(sh_s, w_s, behind, half)
+        out_ref[rows] = (grad_ref[rows].astype(jnp.float32) * conv_out).astype(jnp.bfloat16)
+
+
+def causal_piece(piece, mixed, edge, weights, out_grad, before):
+    tiles = mixed.shape[1] // HD // PIECES
+    column = lambda rows: pl.BlockSpec((rows, HD), lambda c: (0, c + piece * tiles))
+    return pl.pallas_call(
+        causal_kernel,
+        grid=(tiles,),
+        in_specs=[column(TOK), column(TAPS), column(TAPS), column(TOK)]
+        + [pl.BlockSpec(memory_space=pl.ANY)] * len(before),
+        out_specs=column(TOK),
+        out_shape=pltpu.HBM(mixed.shape, jnp.bfloat16),
+        scratch_shapes=[
+            pltpu.VMEM((EXT + 8, HD), jnp.float32),
+            pltpu.VMEM((8, EXT, HD), jnp.float32),
+            pltpu.VMEM((TAPS, HD), jnp.float32),
+        ],
+        input_output_aliases={4: 0} if before else {},
+        name="causal",
+    )(mixed, edge, weights, out_grad, *hbm(*before))
+
+
 def head_anti_kernel(cur_ref, next_ref, edge_ref, w_ref, out_ref, ext_s, sh_s, w_s):
     last = pl.program_id(0) == ROW - 1
     after = jnp.where(last, edge_ref[...].astype(jnp.float32), next_ref[0].astype(jnp.float32))
     spread((cur_ref[0], after), ext_s, sh_s)
     w_s[...] = w_ref[...].astype(jnp.float32)
-    rows = TOK // 2
     for half in range(2):
-
-        def group(k, total, half=half):
-            taps = w_s[pl.ds(pl.multiple_of(k * 8, 8), 8)]
-            start = pl.multiple_of(k * 8 + half * rows, 8)
-            for r in range(8):
-                total = total + taps[r : r + 1] * sh_s[r, pl.ds(start, rows)]
-            return total
-
-        out_ref[0, half * rows : (half + 1) * rows] = lax.fori_loop(
-            0, TAPS // 8, group, jnp.zeros((rows, HD), jnp.float32)
-        )
+        out_ref[0, half * HALF : (half + 1) * HALF] = filtered(sh_s, w_s, ahead, half)
 
 
 def head_anti(packed, edge, weights):
@@ -122,14 +198,14 @@
             pl.BlockSpec((TAPS, HD), lambda b: (0, 0)),
         ],
         out_specs=pl.BlockSpec((1, TOK, HD), lambda b: (b, 0, 0)),
-        out_shape=jax.ShapeDtypeStruct((ROW, TOK, HD), jnp.float32),
+        out_shape=pltpu.HBM((ROW, TOK, HD), jnp.float32),
         scratch_shapes=[
             pltpu.VMEM((EXT + 8, HD), jnp.float32),
             pltpu.VMEM((8, EXT, HD), jnp.float32),
             pltpu.VMEM((TAPS, HD), jnp.float32),
         ],
         name="head_anti",
-    )(packed, packed, edge, weights)
+    )(*hbm(packed, packed), edge, weights)
 
 
 def head_corr_kernel(cur_ref, prev_ref, edge_ref, g_ref, out_ref, ext_s, sh_s, g_s, part_s):
@@ -189,7 +265,7 @@
             pltpu.VMEM((8, TAPS // 8, 8, HD), jnp.float32),
         ],
         name="head_corr",
-    )(mixed, mixed, edge, packed)
+    )(*hbm(mixed, mixed), edge, *hbm(packed))
 
 
 def dot_nn(a, b):
@@ -257,7 +333,7 @@
 def bwd_kernel(
     width_ref, packed_ref, kvh_ref, kdoc_ref, qdoc_ref, qk_ref, mixed_grad_ref,
     out_ref, top_ref, inv_ref,
-    dq_ref, dkv_lo_ref, dkv_hi_ref, dkvh_ref, k_s, v_s, kt_s, dk_s, dv_s,
+    joined_ref, dkv_hi_ref, dkvh_ref, k_s, v_s, kt_s, dk_s, dv_s,
 ):
     block = pl.program_id(0)
 
@@ -285,7 +361,8 @@
         )
         prob_grad = dot_nn(v_s[rows], grad_t)
         score_grad = (weights * (prob_grad - row_dot)).astype(jnp.bfloat16)
-        dq_ref[0] = (dot_nn(kt, score_grad) * SCALE).astype(jnp.bfloat16).T
+        dq = (dot_nn(kt, score_grad) * SCALE).astype(jnp.bfloat16).T
+        joined_ref[block, 2 * TOK :] = dq
         dk_s[rows] += dot_nn(score_grad, q)
         dv_s[rows] += dot_nn(probs, grad)
 
@@ -293,12 +370,12 @@
 
     @pl.when(block == ROW - 1)
     def _():
-        outs = (dkvh_ref, dkv_lo_ref, dkv_hi_ref)
+        outs = (dkvh_ref, joined_ref, dkv_hi_ref)
         for b in range(SPAN + ROW):
             rows = slice(b * TOK, (b + 1) * TOK)
             ref = outs[b // SPAN]
             ref[b % SPAN, :TOK] = (dk_s[rows] * SCALE).astype(ref.dtype)
-            ref[b % SPAN, TOK:] = dv_s[rows].astype(ref.dtype)
+            ref[b % SPAN, TOK : 2 * TOK] = dv_s[rows].astype(ref.dtype)
 
 
 KEYS = (SPAN + ROW) * TOK
@@ -321,7 +398,8 @@
 ]
 
 
-def attention_fwd(widths, *operands):
+def attention_fwd(widths, packed, kvh, kdoc, qdoc, qk):
+    operands = [*hbm(packed, kvh), kdoc, qdoc, *hbm(qk)]
     return pl.pallas_call(
         fwd_kernel,
         grid_spec=pltpu.PrefetchScalarGridSpec(
@@ -335,8 +413,8 @@
             ],
         ),
         out_shape=[
-            jax.ShapeDtypeStruct((ROW, TOK, HD), jnp.bfloat16),
-            jax.ShapeDtypeStruct((ROW, TOK, HD), jnp.bfloat16),
+            pltpu.HBM((ROW, TOK, HD), jnp.bfloat16),
+            pltpu.HBM((ROW, TOK, HD), jnp.bfloat16),
             jax.ShapeDtypeStruct((ROW, 1, TOK), jnp.float32),
             jax.ShapeDtypeStruct((ROW, 1, TOK), jnp.float32),
         ],
@@ -345,14 +423,15 @@
     )(widths, *operands)
 
 
-def attention_bwd(widths, *operands):
+def attention_bwd(widths, packed, kvh, kdoc, qdoc, qk, mixed_grad, out, top, inv):
+    operands = [*hbm(packed, kvh), kdoc, qdoc, *hbm(qk, mixed_grad, out), top, inv]
     return pl.pallas_call(
         bwd_kernel,
         grid_spec=pltpu.PrefetchScalarGridSpec(
             num_scalar_prefetch=1,
             grid=(ROW,),
             in_specs=SHARED_SPECS + [each(TOK, HD), each(TOK, HD), each(1, TOK), each(1, TOK)],
-            out_specs=[each(TOK, HD)] + [whole(SPAN, 2 * TOK, HD)] * 3,
+            out_specs=[whole(ROW, 3 * TOK, HD)] + [whole(SPAN, 2 * TOK, HD)] * 2,
             scratch_shapes=[
                 pltpu.VMEM((KEYS, HD), jnp.bfloat16),
                 pltpu.VMEM((KEYS, HD), jnp.bfloat16),
@@ -362,10 +441,9 @@
             ],
         ),
         out_shape=[
-            jax.ShapeDtypeStruct((ROW, TOK, HD), jnp.bfloat16),
-            jax.ShapeDtypeStruct((SPAN, 2 * TOK, HD), jnp.bfloat16),
-            jax.ShapeDtypeStruct((SPAN, 2 * TOK, HD), jnp.float32),
-            jax.ShapeDtypeStruct((SPAN, 2 * TOK, HD), jnp.bfloat16),
+            pltpu.HBM((ROW, 3 * TOK, HD), jnp.bfloat16),
+            pltpu.HBM((SPAN, 2 * TOK, HD), jnp.float32),
+            pltpu.HBM((SPAN, 2 * TOK, HD), jnp.bfloat16),
         ],
         compiler_params=pltpu.CompilerParams(vmem_limit_bytes=40 << 20),
         name="attn_bwd",
@@ -414,23 +492,22 @@
 
     shared = (widths, packed, kvh, kdoc, qdoc, qk)
     attn_head, mixed_head, top, inv = attention_fwd(*shared)
-    attn_out = unpack(swap(attn_head))[0]
+    attn_out = swap(attn_head)
     mixed_before = shift(mixed_head[ROW - 1, TOK - TAPS :], ROW)
-    dq_head, dkv_lo, dkv_hi, dkvh = attention_bwd(
+    joined, dkv_hi, dkvh = attention_bwd(
         *shared, mixed_grad_head, attn_head, top, inv
     )
     back = shift(dkvh, -ROW)
     filter_part = head_corr(mixed_head, mixed_before, packed)
-    dkv_hi = (dkv_hi + back.astype(jnp.float32)).astype(jnp.bfloat16)
-    dqkv = jnp.concatenate([dq_head, jnp.concatenate([dkv_lo, dkv_hi], 0)], 1)
-    query_grad, key_grad, value_grad = unpack(swap(dqkv))
-
-    mixed = (key_branch.astype(jnp.float32) * attn_out.astype(jnp.float32)).astype(jnp.bfloat16)
+    mixed, branch_grad = finish(attn_out, key_branch, mixed_grad)
     mixed_edge = shift(mixed[TOK - TAPS :], 1)
-    mixed_ext = jnp.concatenate([mixed_edge[1:], mixed], 0)
-    conv_out = causal_conv(mixed_ext, mr_filter)
-    gate_grad = (out_grad.astype(jnp.float32) * conv_out).astype(jnp.bfloat16)
-    branch_grad = (mixed_grad * attn_out.astype(jnp.float32)).astype(jnp.bfloat16)
+    key_grad, value_grad, query_grad = unpack(swap(join(joined, dkv_hi, back)))
+    gate_grad = []
+    for piece in range(PIECES):
+        gate_grad = [
+            causal_piece(piece, mixed, mixed_edge, mr_filter, out_grad, gate_grad)
+        ]
+    gate_grad = gate_grad[0]
 
     def meet(x, axis, hop):
         pairs = [(i, i ^ hop) for i in range(lax.axis_size(axis))]

time: 276 us -> 276 us (level)
  the two profiles are of different devices: /device:TPU:6 before, /device:TPU:10 now
where the time goes in v3:
time: 276 us; the launch traced here: 275 us
  waiting for transfers between devices  104 us (38%)
  Pallas kernels  76.9 us (28%)
  starting transfers between devices  47.4 us (17%)
  matrix products  14.2 us (5%)
  local copies, waits for them, and re-layouts  12.7 us (5%)
  blocking collectives  10.4 us (4%)
  other arithmetic  6.48 us (2%)
    all_to_all x4, waiting for transfers between devices, swap(): return lax.all_to_all(x, axis, 0, 0, axis_index_groups=groups, tiled=True)  62.2 us
    ppermute x6, waiting for transfers between devices, shift(): return lax.ppermute(x, 'seq', pairs)  27 us
    all_to_all x4, starting transfers between devices, swap(): return lax.all_to_all(x, axis, 0, 0, axis_index_groups=groups, tiled=True)  25.3 us
    pallas_call x4, Pallas kernels, causal_piece(): pl.pallas_call(causal_kernel, grid=(tiles,), in_specs=[column(TOK), colum...  18.1 us
    ppermute x6, starting transfers between devices, shift(): return lax.ppermute(x, 'seq', pairs)  17.7 us
    ppermute x5, waiting for transfers between devices, meet(): return x + lax.ppermute(x, axis, pairs)  15 us
    conv_general_dilated x1, matrix products, anti_conv(): lax.conv_general_dilated(extended[None], weights_in[:, None, :], (1,), 'V...  14.2 us
    pallas_call x1, Pallas kernels, head_anti(): pl.pallas_call(head_anti_kernel, grid=(ROW,), in_specs=[pl.BlockSpec((1,...  13.1 us
  transfers between devices with their start and end apart: 15, of which 11 were waited for; matrix products, arithmetic and copies ran while one was open for 8% of the time, Pallas kernels for 18%

profile of v3, /device:TPU:10, one launch (start us, length us, event | category | flops | bytes accessed | tf_op | source)
XLA Modules:
  0.0 274.6 jit_solution(15725482614790626226)
XLA Ops:
  5.3 8.5 %all-to-all-start = ((bf16[8,768,128]{2,1,0:T(8,128)(2,1)}), bf16[8,768,128]{2,1,0:T(8,128)(2,1)S(1)}, u32[]{:S(2)}, u32[]{:S(2)}) async-start(bf16[8,768,128]{2,1,0:T(8,128)(2,1)} %pack.2), calls=%async_computation | async-start | bytes 3145728 | tf_op jit(solution)/shard_map/all_to_all | solution.py:461
  15.8 37.8 %all-to-all-done.cur_ref.next_ref.packed_ref.g_ref = bf16[8,768,128]{2,1,0:T(8,128)(2,1)S(1)} async-done(((bf16[8,768,128]{2,1,0:T(8,128)(2,1)}), bf16[8,768,128]{2,1,0:T(8,128)(2,1)S(1)}, u32[]{:S(2)}, u32[]{:S(2)}) %all-to-all-start) | async-done | bytes 1572896 | tf_op jit(solution)/shard_map/all_to_all | solution.py:461
  53.7 3.6 %all-to-all-start.1 = ((bf16[8,512,128]{2,1,0:T(8,128)(2,1)}), bf16[8,512,128]{2,1,0:T(8,128)(2,1)S(1)}, u32[]{:S(2)}, u32[]{:S(2)}) async-start(bf16[8,512,128]{2,1,0:T(8,128)(2,1)} %pack.3), calls=%async_computation.1 | async-start | bytes 2097152 | tf_op jit(solution)/shard_map/all_to_all | solution.py:461
  58.1 3.4 %collective-permute-start = (bf16[4,512,128]{2,1,0:T(8,128)(2,1)}, bf16[4,512,128]{2,1,0:T(8,128)(2,1)S(1)}, u32[]{:S(2)}, u32[]{:S(2)}) collective-permute-start(bf16[4,512,128]{2,1,0:T(8,128)(2,1)} %slice.84), channel_id=1, source_target_pairs={{0,64},{8,72},{16,80},{24,88},{32,96},{40,104},{48,112},{56,120},{... | collective-permute-start | bytes 1572872 | tf_op jit(solution)/shard_map/ppermute | solution.py:465
  62.0 24.4 %all-to-all-done.1.qk_ref = bf16[8,512,128]{2,1,0:T(8,128)(2,1)S(1)} async-done(((bf16[8,512,128]{2,1,0:T(8,128)(2,1)}), bf16[8,512,128]{2,1,0:T(8,128)(2,1)S(1)}, u32[]{:S(2)}, u32[]{:S(2)}) %all-to-all-start.1) | async-done | bytes 1048608 | tf_op jit(solution)/shard_map/all_to_all | solution.py:461
  88.2 10.3 %attn_fwd.1 = (bf16[8,256,128]{2,1,0:T(8,128)(2,1)}, bf16[8,256,128]{2,1,0:T(8,128)(2,1)}, f32[8,1,256]{2,1,0:T(1,128)S(1)}, f32[8,1,256]{2,1,0:T(1,128)S(1)}) custom-call(s32[8]{0:T(128)S(1)} %fusion.8.width_ref, bf16[8,768,128]{2,1,0:T(8,128)(2,1)} %copy-done, bf16[4,512,128]{2,1,0:T(8,128)(2,1)} %copy-done.6, s32[3072,128]{1,0:T(8,128)S(1)} %broadcast_in_dim.10.kdoc_ref, ...), custom_call_target="tpu_custom_call" | custom-call | tf_op jit(solution)/shard_map/attn_fwd/pallas_call | solution.py:403
  99.2 3.4 %collective-permute-start.5 = (bf16[128,128]{1,0:T(8,128)(2,1)S(1)}, bf16[128,128]{1,0:T(8,128)(2,1)S(1)}, u32[]{:S(2)}, u32[]{:S(2)}) collective-permute-start(bf16[128,128]{1,0:T(8,128)(2,1)S(1)} %slice_bitcast_fusion.1), channel_id=1, source_target_pairs={{0,64},{8,72},{16,80},{24,88},{32,96},{40,104},{48,112},{56,120},{... | collective-permute-start | bytes 98312 | tf_op jit(solution)/shard_map/ppermute | solution.py:465
  105.6 11.9 %head_corr.1 = f32[128,128]{1,0:T(8,128)} custom-call(bf16[8,256,128]{2,1,0:T(8,128)(2,1)} %get-tuple-element.29.cur_ref.prev_ref, bf16[8,256,128]{2,1,0:T(8,128)(2,1)} %get-tuple-element.29.cur_ref.prev_ref, bf16[128,128]{1,0:T(8,128)(2,1)} %copy-done.11, bf16[8,768,128]{2,1,0:T(8,128)(2,1)} %copy-done), custom_call_target="tpu_custom_call" | custom-call | tf_op jit(solution)/shard_map/head_corr/pallas_call | solution.py:250
  117.6 4.5 %collective-permute-done.6 = f32[128,128]{1,0:T(8,128)S(1)} collective-permute-done((f32[128,128]{1,0:T(8,128)}, f32[128,128]{1,0:T(8,128)S(1)}, u32[]{:S(2)}, u32[]{:S(2)}) %collective-permute-start.6) | collective-permute-done | bytes 65568 | tf_op jit(solution)/shard_map/ppermute | solution.py:514
  125.3 3.5 %collective-permute-done.7 = f32[128,128]{1,0:T(8,128)S(1)} collective-permute-done((f32[128,128]{1,0:T(8,128)S(1)}, f32[128,128]{1,0:T(8,128)S(1)}, u32[]{:S(2)}, u32[]{:S(2)}) %collective-permute-start.7) | collective-permute-done | bytes 65568 | tf_op jit(solution)/shard_map/ppermute | solution.py:514
  132.5 3.1 %collective-permute-done.9 = f32[2,128]{1,0:T(2,128)S(1)} collective-permute-done((f32[2,128]{1,0:T(2,128)S(1)}, f32[2,128]{1,0:T(2,128)S(1)}, u32[]{:S(2)}, u32[]{:S(2)}) %collective-permute-start.9) | collective-permute-done | bytes 1056 | tf_op jit(solution)/shard_map/ppermute | solution.py:514
  140.8 10.4 %all_to_all.25 = f32[8,6,128]{2,1,0:T(8,128)S(1)} all-to-all(f32[8,6,128]{2,1,0:T(8,128)S(1)} %pad_maximum_fusion), channel_id=1, replica_groups={{0,8,16,24,32,40,48,56},{64,72,80,88,96,104,112,120},{128,136,144,152,1..., dimensions={0} | all-to-all | bytes 49152 | tf_op jit(solution)/shard_map/all_to_all | solution.py:461
  151.2 3.5 %all-to-all-start.3 = ((bf16[8,256,128]{2,1,0:T(8,128)(2,1)}), bf16[8,256,128]{2,1,0:T(8,128)(2,1)S(1)}, u32[]{:S(2)}, u32[]{:S(2)}) async-start(bf16[8,256,128]{2,1,0:T(8,128)(2,1)} %get-tuple-element.18.out_ref), calls=%async_computation.3 | async-start | bytes 1048576 | tf_op jit(solution)/shard_map/all_to_all | solution.py:461
  161.9 13.1 %head_anti.1.mixed_grad_ref = f32[8,256,128]{2,1,0:T(8,128)} custom-call(bf16[8,768,128]{2,1,0:T(8,128)(2,1)} %copy-done, bf16[8,768,128]{2,1,0:T(8,128)(2,1)} %copy-done, bf16[128,128]{1,0:T(8,128)(2,1)} %copy-done.10, bf16[128,128]{1,0:T(8,128)(2,1)} %constant_dynamic-slice_fusion.1.w_ref), custom_call_target="tpu_custom_call" | custom-call | tf_op jit(solution)/shard_map/head_anti/pallas_call | solution.py:191
  174.9 12.1 %attn_bwd.1 = (bf16[8,768,128]{2,1,0:T(8,128)(2,1)}, f32[4,512,128]{2,1,0:T(8,128)}, bf16[4,512,128]{2,1,0:T(8,128)(2,1)}) custom-call(s32[8]{0:T(128)S(1)} %fusion.8.width_ref, bf16[8,768,128]{2,1,0:T(8,128)(2,1)} %copy-done, bf16[4,512,128]{2,1,0:T(8,128)(2,1)} %copy-done.6, s32[3072,128]{1,0:T(8,128)S(1)} %broadcast_in_dim.10.kdoc_ref, ...), custom_call_target="tpu_custom_call" | custom-call | tf_op jit(solution)/shard_map/attn_bwd/pallas_call | solution.py:428
  191.9 6.6 %collective-permute-done.2.back_ref = bf16[4,512,128]{2,1,0:T(8,128)(2,1)S(1)} collective-permute-done((bf16[4,512,128]{2,1,0:T(8,128)(2,1)}, bf16[4,512,128]{2,1,0:T(8,128)(2,1)S(1)}, u32[]{:S(2)}, u32[]{:S(2)}) %collective-permute-start.2) | collective-permute-done | bytes 524320 | tf_op jit(solution)/shard_map/ppermute | solution.py:465
  202.2 9.8 %all-to-all-start.2 = ((bf16[8,768,128]{2,1,0:T(8,128)(2,1)}), bf16[8,768,128]{2,1,0:T(8,128)(2,1)S(1)}, u32[]{:S(2)}, u32[]{:S(2)}) async-start(bf16[8,768,128]{2,1,0:T(8,128)(2,1)} %join.1), calls=%async_computation.2 | async-start | bytes 3145728 | tf_op jit(solution)/shard_map/all_to_all | solution.py:461
  212.1 14.2 %fusion = f32[1,256,1024]{2,0,1:T(1,128)S(1)} fusion(bf16[1,383,1024]{2,1,0:T(8,128)(2,1)S(1)} %maximum_bitcast_fusion, bf16[128,1,1024]{2,0,1:T(8,128)(2,1)S(1)} %bitcast.24), kind=kOutput, calls=%fused_computation | convolution fusion | flops 67108864 | bytes 2095104 | tf_op jit(solution)/shard_map/conv_general_dilated | solution.py:22
  230.8 3.9 %collective-permute-start.4 = (bf16[128,1024]{1,0:T(8,128)(2,1)S(1)}, bf16[128,1024]{1,0:T(8,128)(2,1)S(1)}, u32[]{:S(2)}, u32[]{:S(2)}) collective-permute-start(bf16[128,1024]{1,0:T(8,128)(2,1)S(1)} %slice.73), channel_id=1, source_target_pairs={{0,8},{8,16},{16,24},{24,32},{32,40},{40,48},{48,56},{56,64},{64,7... | collective-permute-start | bytes 786440 | tf_op jit(solution)/shard_map/ppermute | solution.py:465
  237.3 15.0 %collective-permute-done.4.edge_ref = bf16[128,1024]{1,0:T(8,128)(2,1)S(1)} collective-permute-done((bf16[128,1024]{1,0:T(8,128)(2,1)S(1)}, bf16[128,1024]{1,0:T(8,128)(2,1)S(1)}, u32[]{:S(2)}, u32[]{:S(2)}) %collective-permute-start.4) | collective-permute-done | bytes 262176 | tf_op jit(solution)/shard_map/ppermute | solution.py:465
  253.0 4.5 %causal.4.refs_0_ = bf16[256,1024]{1,0:T(8,128)(2,1)} custom-call(bf16[256,1024]{1,0:T(8,128)(2,1)} %get-tuple-element.27.m_ref, bf16[128,1024]{1,0:T(8,128)(2,1)} %copy-done.5, bf16[128,1024]{1,0:T(8,128)(2,1)} %w_ref.7, bf16[256,1024]{1,0:T(8,128)(2,1)} %grad_ref.7), custom_call_target="tpu_custom_call" | custom-call | tf_op jit(solution)/shard_map/causal/pallas_call | solution.py:164
  257.5 4.5 %causal.5.refs_0_ = bf16[256,1024]{1,0:T(8,128)(2,1)} custom-call(bf16[256,1024]{1,0:T(8,128)(2,1)} %get-tuple-element.27.m_ref, bf16[128,1024]{1,0:T(8,128)(2,1)} %copy-done.5, bf16[128,1024]{1,0:T(8,128)(2,1)} %w_ref.7, bf16[256,1024]{1,0:T(8,128)(2,1)} %grad_ref.7, bf16[256,1024]{1,0:T(8,128)(2,1)} %causal.4.refs_0_), custom_call_target="tpu_custom_call", output_to_operand_aliasing={{}: (4, {})} | custom-call | tf_op jit(solution)/shard_map/causal/pallas_call | solution.py:164
  262.0 4.5 %causal.6.refs_0_ = bf16[256,1024]{1,0:T(8,128)(2,1)} custom-call(bf16[256,1024]{1,0:T(8,128)(2,1)} %get-tuple-element.27.m_ref, bf16[128,1024]{1,0:T(8,128)(2,1)} %copy-done.5, bf16[128,1024]{1,0:T(8,128)(2,1)} %w_ref.7, bf16[256,1024]{1,0:T(8,128)(2,1)} %grad_ref.7, bf16[256,1024]{1,0:T(8,128)(2,1)} %causal.5.refs_0_), custom_call_target="tpu_custom_call", output_to_operand_aliasing={{}: (4, {})} | custom-call | tf_op jit(solution)/shard_map/causal/pallas_call | solution.py:164
  266.5 4.5 %causal.7 = bf16[256,1024]{1,0:T(8,128)(2,1)} custom-call(bf16[256,1024]{1,0:T(8,128)(2,1)} %get-tuple-element.27.m_ref, bf16[128,1024]{1,0:T(8,128)(2,1)} %copy-done.5, bf16[128,1024]{1,0:T(8,128)(2,1)} %w_ref.7, bf16[256,1024]{1,0:T(8,128)(2,1)} %grad_ref.7, bf16[256,1024]{1,0:T(8,128)(2,1)} %causal.6.refs_0_), custom_call_target="tpu_custom_call", output_to_operand_aliasing={{}: (4, {})} | custom-call | tf_op jit(solution)/shard_map/causal/pallas_call | solution.py:164
  (79 shorter events, 51.5 us)
Async XLA Ops:
  5.3 48.4 %all-to-all-start = ((bf16[8,768,128]{2,1,0:T(8,128)(2,1)}), bf16[8,768,128]{2,1,0:T(8,128)(2,1)S(1)}, u32[]{:S(2)}, u32[]{:S(2)}) async-start(bf16[8,768,128]{2,1,0:T(8,128)(2,1)} %pack.2), calls=%async_computation | async-start | bytes 3145728 | tf_op jit(solution)/shard_map/all_to_all | solution.py:461
  15.8 41.4 %copy-start.9 = (s32[8192]{0:T(1024)S(1)}, s32[8192]{0:T(1024)}, u32[]{:S(2)}) copy-start(s32[8192]{0:T(1024)} %param.15) | copy-start | bytes 98308
  53.7 4.5 %copy-start = (bf16[8,768,128]{2,1,0:T(8,128)(2,1)}, bf16[8,768,128]{2,1,0:T(8,128)(2,1)S(1)}, u32[]{:S(2)}) copy-start(bf16[8,768,128]{2,1,0:T(8,128)(2,1)S(1)} %all-to-all-done.cur_ref.next_ref.packed_ref.g_ref) | copy-start | bytes 4718596
  53.7 32.7 %all-to-all-start.1 = ((bf16[8,512,128]{2,1,0:T(8,128)(2,1)}), bf16[8,512,128]{2,1,0:T(8,128)(2,1)S(1)}, u32[]{:S(2)}, u32[]{:S(2)}) async-start(bf16[8,512,128]{2,1,0:T(8,128)(2,1)} %pack.3), calls=%async_computation.1 | async-start | bytes 2097152 | tf_op jit(solution)/shard_map/all_to_all | solution.py:461
  58.1 29.2 %collective-permute-start = (bf16[4,512,128]{2,1,0:T(8,128)(2,1)}, bf16[4,512,128]{2,1,0:T(8,128)(2,1)S(1)}, u32[]{:S(2)}, u32[]{:S(2)}) collective-permute-start(bf16[4,512,128]{2,1,0:T(8,128)(2,1)} %slice.84), channel_id=1, source_target_pairs={{0,64},{8,72},{16,80},{24,88},{32,96},{40,104},{48,112},{56,120},{... | collective-permute-start | bytes 1572872 | tf_op jit(solution)/shard_map/ppermute | solution.py:465
  86.4 1.0 copy-start.1
  87.4 0.8 copy-start.6
  98.4 26.2 %copy-start.4 = (bf16[128,1024]{1,0:T(8,128)(2,1)S(1)}, bf16[128,1024]{1,0:T(8,128)(2,1)}, u32[]{:S(2)}) copy-start(bf16[128,1024]{1,0:T(8,128)(2,1)} %w_ref.7) | copy-start | bytes 786436
  99.2 5.8 %collective-permute-start.5 = (bf16[128,128]{1,0:T(8,128)(2,1)S(1)}, bf16[128,128]{1,0:T(8,128)(2,1)S(1)}, u32[]{:S(2)}, u32[]{:S(2)}) collective-permute-start(bf16[128,128]{1,0:T(8,128)(2,1)S(1)} %slice_bitcast_fusion.1), channel_id=1, source_target_pairs={{0,64},{8,72},{16,80},{24,88},{32,96},{40,104},{48,112},{56,120},{... | collective-permute-start | bytes 98312 | tf_op jit(solution)/shard_map/ppermute | solution.py:465
  117.6 4.5 %collective-permute-start.6 = (f32[128,128]{1,0:T(8,128)}, f32[128,128]{1,0:T(8,128)S(1)}, u32[]{:S(2)}, u32[]{:S(2)}) collective-permute-start(f32[128,128]{1,0:T(8,128)} %head_corr.1), channel_id=1, source_target_pairs={{0,64},{8,72},{16,80},{24,88},{32,96},{40,104},{48,112},{56,120},{... | collective-permute-start | bytes 196616 | tf_op jit(solution)/shard_map/ppermute | solution.py:514
  122.9 5.8 %collective-permute-start.7 = (f32[128,128]{1,0:T(8,128)S(1)}, f32[128,128]{1,0:T(8,128)S(1)}, u32[]{:S(2)}, u32[]{:S(2)}) collective-permute-start(f32[128,128]{1,0:T(8,128)S(1)} %add.57), channel_id=1, source_target_pairs={{0,128},{8,136},{16,144},{24,152},{32,160},{40,168},{48,176},{56,1... | collective-permute-start | bytes 196616 | tf_op jit(solution)/shard_map/ppermute | solution.py:514
  130.8 1.2 collective-permute-start.8
  132.0 3.6 %collective-permute-start.9 = (f32[2,128]{1,0:T(2,128)S(1)}, f32[2,128]{1,0:T(2,128)S(1)}, u32[]{:S(2)}, u32[]{:S(2)}) collective-permute-start(f32[2,128]{1,0:T(2,128)S(1)} %broadcast_add_fusion), channel_id=1, source_target_pairs={{0,2},{1,3},{2,0},{3,1},{4,6},{5,7},{6,4},{7,5},{8,10},{9,11},{10,... | collective-permute-start | bytes 3080 | tf_op jit(solution)/shard_map/ppermute | solution.py:514
  135.7 5.1 %collective-permute-start.10 = (f32[2,128]{1,0:T(2,128)S(1)}, f32[2,128]{1,0:T(2,128)S(1)}, u32[]{:S(2)}, u32[]{:S(2)}) collective-permute-start(f32[2,128]{1,0:T(2,128)S(1)} %fusion.11), channel_id=1, source_target_pairs={{0,4},{1,5},{2,6},{3,7},{4,0},{5,1},{6,2},{7,3},{8,12},{9,13},{10,... | collective-permute-start | bytes 3080 | tf_op jit(solution)/shard_map/ppermute | solution.py:514
  151.2 50.2 %all-to-all-start.3 = ((bf16[8,256,128]{2,1,0:T(8,128)(2,1)}), bf16[8,256,128]{2,1,0:T(8,128)(2,1)S(1)}, u32[]{:S(2)}, u32[]{:S(2)}) async-start(bf16[8,256,128]{2,1,0:T(8,128)(2,1)} %get-tuple-element.18.out_ref), calls=%async_computation.3 | async-start | bytes 1048576 | tf_op jit(solution)/shard_map/all_to_all | solution.py:461
  155.5 5.8 %collective-permute-start.1 = (bf16[128,128]{1,0:T(8,128)(2,1)S(1)}, bf16[128,128]{1,0:T(8,128)(2,1)S(1)}, u32[]{:S(2)}, u32[]{:S(2)}) collective-permute-start(bf16[128,128]{1,0:T(8,128)(2,1)S(1)} %slice_bitcast_fusion), channel_id=1, source_target_pairs={{64,0},{72,8},{80,16},{88,24},{96,32},{104,40},{112,48},{120,56},{... | collective-permute-start | bytes 98312 | tf_op jit(solution)/shard_map/ppermute | solution.py:465
  174.9 14.0 %copy-start.2 = (bf16[256,1024]{1,0:T(8,128)(2,1)S(1)}, bf16[256,1024]{1,0:T(8,128)(2,1)}, u32[]{:S(2)}) copy-start(bf16[256,1024]{1,0:T(8,128)(2,1)} %multiply_convert_fusion.refs_0_) | copy-start | bytes 1572868
  187.0 11.5 %collective-permute-start.2 = (bf16[4,512,128]{2,1,0:T(8,128)(2,1)}, bf16[4,512,128]{2,1,0:T(8,128)(2,1)S(1)}, u32[]{:S(2)}, u32[]{:S(2)}) collective-permute-start(bf16[4,512,128]{2,1,0:T(8,128)(2,1)} %get-tuple-element.23), channel_id=1, source_target_pairs={{64,0},{72,8},{80,16},{88,24},{96,32},{104,40},{112,48},{120,56},{... | collective-permute-start | bytes 1572872 | tf_op jit(solution)/shard_map/ppermute | solution.py:465
  189.0 23.0 %collective-permute-start.3 = (bf16[128,1024]{1,0:T(8,128)(2,1)S(1)}, bf16[128,1024]{1,0:T(8,128)(2,1)S(1)}, u32[]{:S(2)}, u32[]{:S(2)}) collective-permute-start(bf16[128,1024]{1,0:T(8,128)(2,1)S(1)} %slice.86), channel_id=1, source_target_pairs={{8,0},{16,8},{24,16},{32,24},{40,32},{48,40},{56,48},{64,56},{72,6... | collective-permute-start | bytes 786440 | tf_op jit(solution)/shard_map/ppermute | solution.py:465
  198.5 0.8 copy-start.8
  201.4 0.8 copy-start.7
  202.2 68.8 %all-to-all-start.2 = ((bf16[8,768,128]{2,1,0:T(8,128)(2,1)}), bf16[8,768,128]{2,1,0:T(8,128)(2,1)S(1)}, u32[]{:S(2)}, u32[]{:S(2)}) async-start(bf16[8,768,128]{2,1,0:T(8,128)(2,1)} %join.1), calls=%async_computation.2 | async-start | bytes 3145728 | tf_op jit(solution)/shard_map/all_to_all | solution.py:461
  230.8 21.4 %collective-permute-start.4 = (bf16[128,1024]{1,0:T(8,128)(2,1)S(1)}, bf16[128,1024]{1,0:T(8,128)(2,1)S(1)}, u32[]{:S(2)}, u32[]{:S(2)}) collective-permute-start(bf16[128,1024]{1,0:T(8,128)(2,1)S(1)} %slice.73), channel_id=1, source_target_pairs={{0,8},{8,16},{16,24},{24,32},{32,40},{40,48},{48,56},{56,64},{64,7... | collective-permute-start | bytes 786440 | tf_op jit(solution)/shard_map/ppermute | solution.py:465
  271.1 1.2 copy-start.3
  (3 other events, 1.9 us)

commit v4 on v3

--- a/solution.py
+++ b/solution.py
@@ -10,24 +10,13 @@
 TAPS = 128
 SPAN = 4
 ROW = 8
+DOCS = 64
 TOK = 256
 EXT = TOK + TAPS
 NEG = -1e30
 STEP = 4
 SCALE = HD ** (-0.5)
-PIECES = 4
-
-
-def anti_conv(extended, weights_in):
-    return lax.conv_general_dilated(
-        extended[None],
-        weights_in[:, None, :],
-        (1,),
-        "VALID",
-        dimension_numbers=("NWC", "WIO", "NWC"),
-        feature_group_count=extended.shape[1],
-        preferred_element_type=jnp.float32,
-    )[0]
+PIECES = 2
 
 
 def hbm(*arrays):
@@ -94,7 +83,7 @@
         out_specs=[column] * 2,
         out_shape=[shape] * 2,
         name="finish",
-    )(*hbm(attn_out), key, mixed_grad)
+    )(*hbm(attn_out), key, *hbm(mixed_grad))
 
 
 def join_kernel(joined_ref, own_ref, back_ref, out_ref):
@@ -146,6 +135,30 @@
         return total
 
     return lax.fori_loop(0, TAPS // 8, group, jnp.zeros((HALF, HD), jnp.float32))
+
+
+def anti_kernel(g_ref, edge_ref, w_ref, out_ref, ext_s, sh_s, w_s):
+    spread((g_ref[...], edge_ref[...]), ext_s, sh_s)
+    w_s[...] = w_ref[...].astype(jnp.float32)
+    for half in range(2):
+        out_ref[half * HALF : (half + 1) * HALF] = filtered(sh_s, w_s, ahead, half)
+
+
+def anti(conv_grad, edge, weights):
+    column = lambda rows: pl.BlockSpec((rows, HD), lambda c: (0, c))
+    return pl.pallas_call(
+        anti_kernel,
+        grid=(conv_grad.shape[1] // HD,),
+        in_specs=[column(TOK), column(TAPS), column(TAPS)],
+        out_specs=column(TOK),
+        out_shape=pltpu.HBM(conv_grad.shape, jnp.float32),
+        scratch_shapes=[
+            pltpu.VMEM((EXT + 8, HD), jnp.float32),
+            pltpu.VMEM((8, EXT, HD), jnp.float32),
+            pltpu.VMEM((TAPS, HD), jnp.float32),
+        ],
+        name="anti",
+    )(conv_grad, edge, weights)
 
 
 def causal_kernel(m_ref, edge_ref, w_ref, grad_ref, *refs):
@@ -272,6 +285,42 @@
     return jnp.dot(a, b, preferred_element_type=jnp.float32)
 
 
+def norm_kernel(a_ref, b_ref, w_ref, sum_ref, norms_ref):
+    total = a_ref[...] + b_ref[...]
+    sum_ref[...] = total
+    filter_sq = jnp.sum(jnp.square(w_ref[...].astype(jnp.float32)))
+    norms_ref[...] = jnp.zeros_like(norms_ref)
+    norms_ref[0:1] = jnp.full((1, HD), filter_sq, jnp.float32)
+    norms_ref[1:2] = jnp.full((1, HD), jnp.sum(total * total), jnp.float32)
+
+
+def norm_parts(a, b, weights):
+    return pl.pallas_call(
+        norm_kernel,
+        out_shape=[
+            jax.ShapeDtypeStruct(a.shape, jnp.float32),
+            jax.ShapeDtypeStruct((8, HD), jnp.float32),
+        ],
+        name="norm_parts",
+    )(a, b, weights)
+
+
+def step_kernel(got_ref, out_ref):
+    rows = out_ref.shape[0]
+    norms = jnp.sum(got_ref[:, rows : rows + 2], 0)
+    trust = jnp.sqrt(norms[0:1]) / jnp.sqrt(norms[1:2] + 1e-06)
+    for head in range(ROW):
+        out_ref[:, head * HD : (head + 1) * HD] = trust * got_ref[head, :rows]
+
+
+def scaled_step(got, rows):
+    return pl.pallas_call(
+        step_kernel,
+        out_shape=jax.ShapeDtypeStruct((rows, ROW * HD), jnp.float32),
+        name="scaled_step",
+    )(got)
+
+
 def window_of(block, width):
     first = block + (SPAN + 1 - width)
     return first, pl.ds(pl.multiple_of(first * TOK, TOK), width * TOK)
@@ -286,78 +335,79 @@
         yield b, slice(b * TOK, (b + 1) * TOK), k, src[at, skip + TOK :]
 
 
-def masked_scores(k, q, kdoc, qdoc, width):
+def masked_scores(k, q, starts, first, width):
     scores = dot_nn(k, q.T)
-    same = jnp.concatenate([kdoc, kdoc], 1) == qdoc
     key_at = lax.broadcasted_iota(jnp.int32, scores.shape, 0)
-    query_at = lax.broadcasted_iota(jnp.int32, scores.shape, 1) + (width - 1) * TOK
-    return jnp.where(same & (key_at <= query_at), scores, NEG)
-
-
-def by_width(width_ref, block, attend):
-    for width in range(1, SPAN + 2):
-        pl.when(width_ref[block] == width)(lambda width=width: attend(width))
+    allowed = key_at >= starts - first * TOK
+    own = (width - 1) * TOK
+    query_at = lax.broadcasted_iota(jnp.int32, (TOK, TOK), 1)
+    causal = allowed[own:] & (lax.broadcasted_iota(jnp.int32, (TOK, TOK), 0) <= query_at)
+    diagonal = jnp.where(causal, scores[own:], NEG)
+    if width == 1:
+        return diagonal
+    return jnp.concatenate([jnp.where(allowed[:own], scores[:own], NEG), diagonal], 0)
+
+
+def each_block(width_ref, attend):
+    def step(block, carry):
+        for width in range(1, SPAN + 2):
+            pl.when(width_ref[block] == width)(lambda width=width: attend(block, width))
+        return carry
+
+    lax.fori_loop(0, ROW, step, 0)
 
 
 def fwd_kernel(
-    width_ref, packed_ref, kvh_ref, kdoc_ref, qdoc_ref, qk_ref,
+    width_ref, packed_ref, kvh_ref, starts_ref, qk_ref,
     out_ref, mixed_ref, top_ref, inv_ref, k_s, vt_s,
 ):
-    block = pl.program_id(0)
-
-    @pl.when(block == 0)
-    def _():
-        for b, rows, k, v in key_blocks(packed_ref, kvh_ref):
-            k_s[rows] = k
-            vt_s[b] = v.T
-
-    def attend(width):
+    for b, rows, k, v in key_blocks(packed_ref, kvh_ref):
+        k_s[rows] = k
+        vt_s[b] = v.T
+
+    def attend(block, width):
         first, rows = window_of(block, width)
-        q = qk_ref[0, :TOK]
+        q = qk_ref[block, :TOK]
         vt = jnp.concatenate([vt_s[first + n] for n in range(width)], 1)
-        scores = masked_scores(k_s[rows], q, kdoc_ref[rows], qdoc_ref[0], width)
+        scores = masked_scores(k_s[rows], q, starts_ref[block], first, width)
         top = jnp.max(scores, 0, keepdims=True)
         weights = jnp.exp((scores - top) * SCALE)
         inv = 1.0 / jnp.sum(weights, 0, keepdims=True)
-        top_ref[0] = top
-        inv_ref[0] = inv
+        top_ref[block] = top
+        inv_ref[block] = inv
         probs = (weights * inv).astype(jnp.bfloat16)
         out = dot_nn(vt, probs).astype(jnp.bfloat16).T
-        out_ref[0] = out
-        key = qk_ref[0, TOK:].astype(jnp.float32)
-        mixed_ref[0] = (key * out.astype(jnp.float32)).astype(jnp.bfloat16)
-
-    by_width(width_ref, block, attend)
+        out_ref[block] = out
+        key = qk_ref[block, TOK:].astype(jnp.float32)
+        mixed_ref[block] = (key * out.astype(jnp.float32)).astype(jnp.bfloat16)
+
+    each_block(width_ref, attend)
 
 
 def bwd_kernel(
-    width_ref, packed_ref, kvh_ref, kdoc_ref, qdoc_ref, qk_ref, mixed_grad_ref,
+    width_ref, packed_ref, kvh_ref, starts_ref, qk_ref, mixed_grad_ref,
     out_ref, top_ref, inv_ref,
     joined_ref, dkv_hi_ref, dkvh_ref, k_s, v_s, kt_s, dk_s, dv_s,
 ):
-    block = pl.program_id(0)
-
-    @pl.when(block == 0)
-    def _():
-        for b, rows, k, v in key_blocks(packed_ref, kvh_ref):
-            k_s[rows] = k
-            v_s[rows] = v
-            kt_s[b] = k.T
-        dk_s[...] = jnp.zeros_like(dk_s)
-        dv_s[...] = jnp.zeros_like(dv_s)
-
-    def attend(width):
+    for b, rows, k, v in key_blocks(packed_ref, kvh_ref):
+        k_s[rows] = k
+        v_s[rows] = v
+        kt_s[b] = k.T
+    dk_s[...] = jnp.zeros_like(dk_s)
+    dv_s[...] = jnp.zeros_like(dv_s)
+
+    def attend(block, width):
         first, rows = window_of(block, width)
-        q = qk_ref[0, :TOK]
-        key = qk_ref[0, TOK:].astype(jnp.float32)
-        grad = (mixed_grad_ref[0] * key).astype(jnp.bfloat16)
+        q = qk_ref[block, :TOK]
+        key = qk_ref[block, TOK:].astype(jnp.float32)
+        grad = (mixed_grad_ref[block] * key).astype(jnp.bfloat16)
         grad_t = grad.T
         kt = jnp.concatenate([kt_s[first + n] for n in range(width)], 1)
-        scores = masked_scores(k_s[rows], q, kdoc_ref[rows], qdoc_ref[0], width)
-        weights = jnp.exp((scores - top_ref[0]) * SCALE) * inv_ref[0]
+        scores = masked_scores(k_s[rows], q, starts_ref[block], first, width)
+        weights = jnp.exp((scores - top_ref[block]) * SCALE) * inv_ref[block]
         probs = weights.astype(jnp.bfloat16)
         row_dot = jnp.sum(
-            out_ref[0].T.astype(jnp.float32) * grad_t.astype(jnp.float32), 0, keepdims=True
+            out_ref[block].T.astype(jnp.float32) * grad_t.astype(jnp.float32), 0, keepdims=True
         )
         prob_grad = dot_nn(v_s[rows], grad_t)
         score_grad = (weights * (prob_grad - row_dot)).astype(jnp.bfloat16)
@@ -366,16 +416,13 @@
         dk_s[rows] += dot_nn(score_grad, q)
         dv_s[rows] += dot_nn(probs, grad)
 
-    by_width(width_ref, block, attend)
-
-    @pl.when(block == ROW - 1)
-    def _():
-        outs = (dkvh_ref, joined_ref, dkv_hi_ref)
-        for b in range(SPAN + ROW):
-            rows = slice(b * TOK, (b + 1) * TOK)
-            ref = outs[b // SPAN]
-            ref[b % SPAN, :TOK] = (dk_s[rows] * SCALE).astype(ref.dtype)
-            ref[b % SPAN, TOK : 2 * TOK] = dv_s[rows].astype(ref.dtype)
+    each_block(width_ref, attend)
+    outs = (dkvh_ref, joined_ref, dkv_hi_ref)
+    for b in range(SPAN + ROW):
+        rows = slice(b * TOK, (b + 1) * TOK)
+        ref = outs[b // SPAN]
+        ref[b % SPAN, :TOK] = (dk_s[rows] * SCALE).astype(ref.dtype)
+        ref[b % SPAN, TOK : 2 * TOK] = dv_s[rows].astype(ref.dtype)
 
 
 KEYS = (SPAN + ROW) * TOK
@@ -385,28 +432,25 @@
     return pl.BlockSpec(shape, lambda b, w: (0,) * len(shape))
 
 
-def each(*shape):
-    return pl.BlockSpec((1,) + shape, lambda b, w: (b, 0, 0))
-
-
+TOKEN_SPEC = whole(ROW, TOK, HD)
+STAT_SPEC = whole(ROW, 1, TOK)
 SHARED_SPECS = [
     whole(ROW, 3 * TOK, HD),
     whole(SPAN, 2 * TOK, HD),
-    whole(KEYS, HD),
-    each(1, TOK),
-    each(2 * TOK, HD),
+    STAT_SPEC,
+    whole(ROW, 2 * TOK, HD),
 ]
 
 
-def attention_fwd(widths, packed, kvh, kdoc, qdoc, qk):
-    operands = [*hbm(packed, kvh), kdoc, qdoc, *hbm(qk)]
+def attention_fwd(widths, packed, kvh, starts, qk):
+    operands = [*hbm(packed, kvh), starts, *hbm(qk)]
     return pl.pallas_call(
         fwd_kernel,
         grid_spec=pltpu.PrefetchScalarGridSpec(
             num_scalar_prefetch=1,
-            grid=(ROW,),
+            grid=(1,),
             in_specs=SHARED_SPECS,
-            out_specs=[each(TOK, HD), each(TOK, HD), each(1, TOK), each(1, TOK)],
+            out_specs=[TOKEN_SPEC, TOKEN_SPEC, STAT_SPEC, STAT_SPEC],
             scratch_shapes=[
                 pltpu.VMEM((KEYS, HD), jnp.bfloat16),
                 pltpu.VMEM((SPAN + ROW, HD, TOK), jnp.bfloat16),
@@ -423,14 +467,14 @@
     )(widths, *operands)
 
 
-def attention_bwd(widths, packed, kvh, kdoc, qdoc, qk, mixed_grad, out, top, inv):
-    operands = [*hbm(packed, kvh), kdoc, qdoc, *hbm(qk, mixed_grad, out), top, inv]
+def attention_bwd(widths, packed, kvh, starts, qk, mixed_grad, out, top, inv):
+    operands = [*hbm(packed, kvh), starts, *hbm(qk, mixed_grad, out), top, inv]
     return pl.pallas_call(
         bwd_kernel,
         grid_spec=pltpu.PrefetchScalarGridSpec(
             num_scalar_prefetch=1,
-            grid=(ROW,),
-            in_specs=SHARED_SPECS + [each(TOK, HD), each(TOK, HD), each(1, TOK), each(1, TOK)],
+            grid=(1,),
+            in_specs=SHARED_SPECS + [TOKEN_SPEC, TOKEN_SPEC, STAT_SPEC, STAT_SPEC],
             out_specs=[whole(ROW, 3 * TOK, HD)] + [whole(SPAN, 2 * TOK, HD)] * 2,
             scratch_shapes=[
                 pltpu.VMEM((KEYS, HD), jnp.bfloat16),
@@ -471,17 +515,18 @@
     widths = jnp.ones((ROW,), jnp.int32)
     for back in range(1, SPAN + 1):
         widths = widths + (docs[SPAN - back : SPAN + ROW - back, -1] == docs[SPAN:, 0])
-    kdoc = jnp.broadcast_to(docs.reshape(-1, 1), ((SPAN + ROW) * TOK, HD))
-    qdoc = docs[SPAN:].reshape(ROW, 1, TOK)
+    numbers = jnp.arange(DOCS, dtype=jnp.int32)[:, None]
+    first_rows = jnp.sum((doc_ids[None] < numbers).astype(jnp.int32), 1, keepdims=True)
+    first_rows = first_rows - ((position // ROW) * ROW - SPAN) * TOK
+    starts = jnp.sum(jnp.where(docs[SPAN:].reshape(1, -1) == numbers, first_rows, 0), 0)
+    starts = starts.reshape(ROW, 1, TOK)
 
     conv_grad = (out_grad.astype(jnp.float32) * gate_branch.astype(jnp.float32)).astype(
         jnp.bfloat16
     )
     grad_edge = shift(conv_grad[:TAPS], -1)
     packed = swap(pack(conv_grad, keys_in, values_in))
-    mixed_grad = anti_conv(
-        jnp.concatenate([conv_grad, grad_edge[: TAPS - 1]], 0), mr_filter
-    )
+    mixed_grad = anti(conv_grad, grad_edge, mr_filter)
     qk = swap(pack(queries_in, key_branch))
 
     kvh = shift(packed[ROW - SPAN :, TOK:], ROW)
@@ -490,7 +535,7 @@
     own_taps = lax.dynamic_slice_in_dim(mr_filter, head * HD, HD, 1)
     mixed_grad_head = head_anti(packed, head_edge, own_taps)
 
-    shared = (widths, packed, kvh, kdoc, qdoc, qk)
+    shared = (widths, packed, kvh, starts, qk)
     attn_head, mixed_head, top, inv = attention_fwd(*shared)
     attn_out = swap(attn_head)
     mixed_before = shift(mixed_head[ROW - 1, TOK - TAPS :], ROW)
@@ -509,36 +554,27 @@
         ]
     gate_grad = gate_grad[0]
 
-    def meet(x, axis, hop):
+    def partner(x, axis, hop):
         pairs = [(i, i ^ hop) for i in range(lax.axis_size(axis))]
-        return x + lax.ppermute(x, axis, pairs)
+        return lax.ppermute(x, axis, pairs)
 
     rings_n = n_seq // ROW
-    filter_grad = filter_part
-    hop = ROW
-    while hop < n_seq:
-        filter_grad = meet(filter_grad, "seq", hop)
-        hop *= 2
     tap_share = TAPS // ROW
     own_filter = lax.dynamic_slice_in_dim(mr_filter, head * tap_share, tap_share, 0)
-    norms = jnp.stack(
-        [jnp.sum(jnp.square(own_filter.astype(jnp.float32))), jnp.sum(filter_grad * filter_grad)]
-    )
-    norms = jnp.broadcast_to(norms[:, None], (2, HD))
+    filter_grad = filter_part + partner(filter_part, "seq", ROW)
+    other = partner(filter_grad, "seq", 2 * ROW)
+    filter_grad, norms = norm_parts(filter_grad, other, own_filter)
     hop = 1
     while hop < lax.axis_size("ch"):
-        norms = meet(norms, "ch", hop)
+        norms = norms + partner(norms, "ch", hop)
         hop *= 2
     tap_rows = TAPS // n_seq
     ring_taps = lax.dynamic_slice_in_dim(
         filter_grad, (position // ROW) * (TAPS // rings_n), TAPS // rings_n, 0
     ).reshape(ROW, tap_rows, HD)
-    sent = jnp.concatenate([ring_taps, jnp.broadcast_to(norms[None], (ROW, 2, HD))], 1)
-    got = swap(sent)
-    own_grad = jnp.swapaxes(got[:, :tap_rows], 0, 1).reshape(tap_rows, ROW * HD)
-    norms = jnp.sum(got[:, tap_rows:], 0)
-    trust = jnp.sqrt(norms[0, 0]) / jnp.sqrt(norms[1, 0] + 1e-06)
-    filter_step = trust * own_grad
+    spread_norms = jnp.broadcast_to(norms[None, :tap_rows], (ROW, tap_rows, HD))
+    got = swap(jnp.concatenate([ring_taps, spread_norms], 1))
+    filter_step = scaled_step(got, tap_rows)
     return (query_grad, key_grad, value_grad, gate_grad, branch_grad, filter_step)
 
 

time: 276 us -> 294 us (1.065)
  the two profiles are of different devices: /device:TPU:10 before, /device:TPU:18 now
where the time goes in v4:
time: 294 us; the launch traced here: 293 us
  waiting for transfers between devices  128 us (44%)
  Pallas kernels  89.9 us (31%)
  starting transfers between devices  44.8 us (15%)
  local copies, waits for them, and re-layouts  14.5 us (5%)
  blocking collectives  11.1 us (4%)
  other arithmetic  4.23 us (1%)
    all_to_all x4, waiting for transfers between devices, swap(): return lax.all_to_all(x, axis, 0, 0, axis_index_groups=groups, tiled=True)  61.7 us
    ppermute x6, waiting for transfers between devices, shift(): return lax.ppermute(x, 'seq', pairs)  51 us
    all_to_all x4, starting transfers between devices, swap(): return lax.all_to_all(x, axis, 0, 0, axis_index_groups=groups, tiled=True)  22.4 us
    ppermute x6, starting transfers between devices, shift(): return lax.ppermute(x, 'seq', pairs)  19 us
    pallas_call x2, Pallas kernels, causal_piece(): pl.pallas_call(causal_kernel, grid=(tiles,), in_specs=[column(TOK), colum...  15 us
    ppermute x5, waiting for transfers between devices, partner(): return lax.ppermute(x, axis, pairs)  15 us
    pallas_call x1, Pallas kernels, anti(): pl.pallas_call(anti_kernel, grid=(conv_grad.shape[1] // HD,), in_specs=[c...  13.3 us
    pallas_call x1, Pallas kernels, head_anti(): pl.pallas_call(head_anti_kernel, grid=(ROW,), in_specs=[pl.BlockSpec((1,...  13.1 us
  transfers between devices with their start and end apart: 15, of which 12 were waited for; matrix products, arithmetic and copies ran while one was open for 2% of the time, Pallas kernels for 21%

profile of v4, /device:TPU:18, one launch (start us, length us, event | category | flops | bytes accessed | tf_op | source)
XLA Modules:
  0.0 292.9 jit_solution(14578242742420599121)
XLA Ops:
  5.3 8.5 %all-to-all-start = ((bf16[8,768,128]{2,1,0:T(8,128)(2,1)}), bf16[8,768,128]{2,1,0:T(8,128)(2,1)S(1)}, u32[]{:S(2)}, u32[]{:S(2)}) async-start(bf16[8,768,128]{2,1,0:T(8,128)(2,1)} %pack.2), calls=%async_computation | async-start | bytes 3145728 | tf_op jit(solution)/shard_map/all_to_all | solution.py:505
  15.8 37.8 %all-to-all-done.cur_ref.next_ref.packed_ref.g_ref = bf16[8,768,128]{2,1,0:T(8,128)(2,1)S(1)} async-done(((bf16[8,768,128]{2,1,0:T(8,128)(2,1)}), bf16[8,768,128]{2,1,0:T(8,128)(2,1)S(1)}, u32[]{:S(2)}, u32[]{:S(2)}) %all-to-all-start) | async-done | bytes 1572896 | tf_op jit(solution)/shard_map/all_to_all | solution.py:505
  53.7 3.6 %all-to-all-start.1 = ((bf16[8,512,128]{2,1,0:T(8,128)(2,1)}), bf16[8,512,128]{2,1,0:T(8,128)(2,1)S(1)}, u32[]{:S(2)}, u32[]{:S(2)}) async-start(bf16[8,512,128]{2,1,0:T(8,128)(2,1)} %pack.3), calls=%async_computation.1 | async-start | bytes 2097152 | tf_op jit(solution)/shard_map/all_to_all | solution.py:505
  58.9 3.4 %collective-permute-start = (bf16[4,512,128]{2,1,0:T(8,128)(2,1)}, bf16[4,512,128]{2,1,0:T(8,128)(2,1)S(1)}, u32[]{:S(2)}, u32[]{:S(2)}) collective-permute-start(bf16[4,512,128]{2,1,0:T(8,128)(2,1)} %slice.57), channel_id=1, source_target_pairs={{0,64},{8,72},{16,80},{24,88},{32,96},{40,104},{48,112},{56,120},{... | collective-permute-start | bytes 1572872 | tf_op jit(solution)/shard_map/ppermute | solution.py:509
  62.5 23.9 %all-to-all-done.1.qk_ref = bf16[8,512,128]{2,1,0:T(8,128)(2,1)S(1)} async-done(((bf16[8,512,128]{2,1,0:T(8,128)(2,1)}), bf16[8,512,128]{2,1,0:T(8,128)(2,1)S(1)}, u32[]{:S(2)}, u32[]{:S(2)}) %all-to-all-start.1) | async-done | bytes 1048608 | tf_op jit(solution)/shard_map/all_to_all | solution.py:505
  87.5 10.3 %attn_fwd.1 = (bf16[8,256,128]{2,1,0:T(8,128)(2,1)}, bf16[8,256,128]{2,1,0:T(8,128)(2,1)}, f32[8,1,256]{2,1,0:T(1,128)S(1)}, f32[8,1,256]{2,1,0:T(1,128)S(1)}) custom-call(s32[8]{0:T(128)S(1)} %fusion.4.width_ref, bf16[8,768,128]{2,1,0:T(8,128)(2,1)} %copy-done, bf16[4,512,128]{2,1,0:T(8,128)(2,1)} %copy-done.4, s32[8,1,256]{2,1,0:T(1,128)S(1)} %bitcast.8, ...), custom_call_target="tpu_custom_call" | custom-call | tf_op jit(solution)/shard_map/attn_fwd/pallas_call | solution.py:447
  98.6 3.4 %collective-permute-start.5 = (bf16[128,128]{1,0:T(8,128)(2,1)S(1)}, bf16[128,128]{1,0:T(8,128)(2,1)S(1)}, u32[]{:S(2)}, u32[]{:S(2)}) collective-permute-start(bf16[128,128]{1,0:T(8,128)(2,1)S(1)} %slice_bitcast_fusion.1), channel_id=1, source_target_pairs={{0,64},{8,72},{16,80},{24,88},{32,96},{40,104},{48,112},{56,120},{... | collective-permute-start | bytes 98312 | tf_op jit(solution)/shard_map/ppermute | solution.py:509
  105.0 11.9 %head_corr.1 = f32[128,128]{1,0:T(8,128)} custom-call(bf16[8,256,128]{2,1,0:T(8,128)(2,1)} %get-tuple-element.31.cur_ref.prev_ref, bf16[8,256,128]{2,1,0:T(8,128)(2,1)} %get-tuple-element.31.cur_ref.prev_ref, bf16[128,128]{1,0:T(8,128)(2,1)} %copy-done.13, bf16[8,768,128]{2,1,0:T(8,128)(2,1)} %copy-done), custom_call_target="tpu_custom_call" | custom-call | tf_op jit(solution)/shard_map/head_corr/pallas_call | solution.py:263
  116.9 4.5 %collective-permute-done.6 = f32[128,128]{1,0:T(8,128)S(1)} collective-permute-done((f32[128,128]{1,0:T(8,128)}, f32[128,128]{1,0:T(8,128)S(1)}, u32[]{:S(2)}, u32[]{:S(2)}) %collective-permute-start.6) | collective-permute-done | bytes 65568 | tf_op jit(solution)/shard_map/ppermute | solution.py:559
  125.4 2.7 collective-permute-done.7.b_ref
  137.1 4.1 %collective-permute-done.10 = f32[8,128]{1,0:T(8,128)S(1)} collective-permute-done((f32[8,128]{1,0:T(8,128)S(1)}, f32[8,128]{1,0:T(8,128)S(1)}, u32[]{:S(2)}, u32[]{:S(2)}) %collective-permute-start.10) | collective-permute-done | bytes 4128 | tf_op jit(solution)/shard_map/ppermute | solution.py:559
  141.2 11.1 %all_to_all.25.got_ref = f32[8,8,128]{2,1,0:T(8,128)} all-to-all(f32[8,8,128]{2,1,0:T(8,128)S(1)} %pad_maximum_fusion), channel_id=1, replica_groups={{0,8,16,24,32,40,48,56},{64,72,80,88,96,104,112,120},{128,136,144,152,1..., dimensions={0} | all-to-all | bytes 65536 | tf_op jit(solution)/shard_map/all_to_all | solution.py:505
  152.3 3.5 %all-to-all-start.3 = ((bf16[8,256,128]{2,1,0:T(8,128)(2,1)}), bf16[8,256,128]{2,1,0:T(8,128)(2,1)S(1)}, u32[]{:S(2)}, u32[]{:S(2)}) async-start(bf16[8,256,128]{2,1,0:T(8,128)(2,1)} %get-tuple-element.20.out_ref), calls=%async_computation.3 | async-start | bytes 1048576 | tf_op jit(solution)/shard_map/all_to_all | solution.py:505
  163.0 13.1 %head_anti.1.mixed_grad_ref = f32[8,256,128]{2,1,0:T(8,128)} custom-call(bf16[8,768,128]{2,1,0:T(8,128)(2,1)} %copy-done, bf16[8,768,128]{2,1,0:T(8,128)(2,1)} %copy-done, bf16[128,128]{1,0:T(8,128)(2,1)} %copy-done.12, bf16[128,128]{1,0:T(8,128)(2,1)} %constant_dynamic-slice_fusion.1.w_ref), custom_call_target="tpu_custom_call" | custom-call | tf_op jit(solution)/shard_map/head_anti/pallas_call | solution.py:204
  176.0 11.8 %attn_bwd.1 = (bf16[8,768,128]{2,1,0:T(8,128)(2,1)}, f32[4,512,128]{2,1,0:T(8,128)}, bf16[4,512,128]{2,1,0:T(8,128)(2,1)}) custom-call(s32[8]{0:T(128)S(1)} %fusion.4.width_ref, bf16[8,768,128]{2,1,0:T(8,128)(2,1)} %copy-done, bf16[4,512,128]{2,1,0:T(8,128)(2,1)} %copy-done.4, s32[8,1,256]{2,1,0:T(1,128)S(1)} %bitcast.9, bf16[8,512,128]{2,1,0:T(8,128)(2,1)} %copy-done.1, ...), custom_call_target="tpu_custom_call" | custom-call | tf_op jit(solution)/shard_map/attn_bwd/pallas_call | solution.py:472
  189.7 9.6 %collective-permute-done.2.back_ref = bf16[4,512,128]{2,1,0:T(8,128)(2,1)S(1)} collective-permute-done((bf16[4,512,128]{2,1,0:T(8,128)(2,1)}, bf16[4,512,128]{2,1,0:T(8,128)(2,1)S(1)}, u32[]{:S(2)}, u32[]{:S(2)}) %collective-permute-start.2) | collective-permute-done | bytes 524320 | tf_op jit(solution)/shard_map/ppermute | solution.py:509
  203.0 6.9 %all-to-all-start.2 = ((bf16[8,768,128]{2,1,0:T(8,128)(2,1)}), bf16[8,768,128]{2,1,0:T(8,128)(2,1)S(1)}, u32[]{:S(2)}, u32[]{:S(2)}) async-start(bf16[8,768,128]{2,1,0:T(8,128)(2,1)} %join.1), calls=%async_computation.2 | async-start | bytes 3145728 | tf_op jit(solution)/shard_map/all_to_all | solution.py:505
  209.9 4.8 %collective-permute-start.3 = (bf16[128,1024]{1,0:T(8,128)(2,1)S(1)}, bf16[128,1024]{1,0:T(8,128)(2,1)S(1)}, u32[]{:S(2)}, u32[]{:S(2)}) collective-permute-start(bf16[128,1024]{1,0:T(8,128)(2,1)S(1)} %slice.59), channel_id=1, source_target_pairs={{8,0},{16,8},{24,16},{32,24},{40,32},{48,40},{56,48},{64,56},{72,6... | collective-permute-start | bytes 786440 | tf_op jit(solution)/shard_map/ppermute | solution.py:509
  214.7 31.1 %collective-permute-done.3.edge_ref = bf16[128,1024]{1,0:T(8,128)(2,1)S(1)} collective-permute-done((bf16[128,1024]{1,0:T(8,128)(2,1)S(1)}, bf16[128,1024]{1,0:T(8,128)(2,1)S(1)}, u32[]{:S(2)}, u32[]{:S(2)}) %collective-permute-start.3) | collective-permute-done | bytes 262176 | tf_op jit(solution)/shard_map/ppermute | solution.py:509
  246.6 13.3 %anti.1.mixed_grad_ref = f32[256,1024]{1,0:T(8,128)} custom-call(bf16[256,1024]{1,0:T(8,128)(2,1)} %multiply_convert_fusion.refs_0_.g_ref, bf16[128,1024]{1,0:T(8,128)(2,1)} %copy-done.10, bf16[128,1024]{1,0:T(8,128)(2,1)} %w_ref.5), custom_call_target="tpu_custom_call" | custom-call | tf_op jit(solution)/shard_map/anti/pallas_call | solution.py:149
  263.2 3.4 %collective-permute-start.4 = (bf16[128,1024]{1,0:T(8,128)(2,1)S(1)}, bf16[128,1024]{1,0:T(8,128)(2,1)S(1)}, u32[]{:S(2)}, u32[]{:S(2)}) collective-permute-start(bf16[128,1024]{1,0:T(8,128)(2,1)S(1)} %slice.49), channel_id=1, source_target_pairs={{0,8},{8,16},{16,24},{24,32},{32,40},{40,48},{48,56},{56,64},{64,7... | collective-permute-start | bytes 786440 | tf_op jit(solution)/shard_map/ppermute | solution.py:509
  268.0 5.6 %collective-permute-done.4.edge_ref = bf16[128,1024]{1,0:T(8,128)(2,1)S(1)} collective-permute-done((bf16[128,1024]{1,0:T(8,128)(2,1)S(1)}, bf16[128,1024]{1,0:T(8,128)(2,1)S(1)}, u32[]{:S(2)}, u32[]{:S(2)}) %collective-permute-start.4) | collective-permute-done | bytes 262176 | tf_op jit(solution)/shard_map/ppermute | solution.py:509
  274.3 7.5 %causal.2.refs_0_ = bf16[256,1024]{1,0:T(8,128)(2,1)} custom-call(bf16[256,1024]{1,0:T(8,128)(2,1)} %get-tuple-element.29.m_ref, bf16[128,1024]{1,0:T(8,128)(2,1)} %copy-done.6, bf16[128,1024]{1,0:T(8,128)(2,1)} %w_ref.5, bf16[256,1024]{1,0:T(8,128)(2,1)} %grad_ref.3), custom_call_target="tpu_custom_call" | custom-call | tf_op jit(solution)/shard_map/causal/pallas_call | solution.py:177
  281.8 7.5 %causal.3 = bf16[256,1024]{1,0:T(8,128)(2,1)} custom-call(bf16[256,1024]{1,0:T(8,128)(2,1)} %get-tuple-element.29.m_ref, bf16[128,1024]{1,0:T(8,128)(2,1)} %copy-done.6, bf16[128,1024]{1,0:T(8,128)(2,1)} %w_ref.5, bf16[256,1024]{1,0:T(8,128)(2,1)} %grad_ref.3, bf16[256,1024]{1,0:T(8,128)(2,1)} %causal.2.refs_0_), custom_call_target="tpu_custom_call", output_to_operand_aliasing={{}: (4, {})} | custom-call | tf_op jit(solution)/shard_map/causal/pallas_call | solution.py:177
  (78 shorter events, 48.9 us)
Async XLA Ops:
  5.3 48.4 %all-to-all-start = ((bf16[8,768,128]{2,1,0:T(8,128)(2,1)}), bf16[8,768,128]{2,1,0:T(8,128)(2,1)S(1)}, u32[]{:S(2)}, u32[]{:S(2)}) async-start(bf16[8,768,128]{2,1,0:T(8,128)(2,1)} %pack.2), calls=%async_computation | async-start | bytes 3145728 | tf_op jit(solution)/shard_map/all_to_all | solution.py:505
  15.8 41.4 %copy-start.8 = (s32[8192]{0:T(1024)S(1)}, s32[8192]{0:T(1024)}, u32[]{:S(2)}) copy-start(s32[8192]{0:T(1024)} %param.15) | copy-start | bytes 98308
  53.7 5.3 %copy-start = (bf16[8,768,128]{2,1,0:T(8,128)(2,1)}, bf16[8,768,128]{2,1,0:T(8,128)(2,1)S(1)}, u32[]{:S(2)}) copy-start(bf16[8,768,128]{2,1,0:T(8,128)(2,1)S(1)} %all-to-all-done.cur_ref.next_ref.packed_ref.g_ref) | copy-start | bytes 4718596
  53.7 32.7 %all-to-all-start.1 = ((bf16[8,512,128]{2,1,0:T(8,128)(2,1)}), bf16[8,512,128]{2,1,0:T(8,128)(2,1)S(1)}, u32[]{:S(2)}, u32[]{:S(2)}) async-start(bf16[8,512,128]{2,1,0:T(8,128)(2,1)} %pack.3), calls=%async_computation.1 | async-start | bytes 2097152 | tf_op jit(solution)/shard_map/all_to_all | solution.py:505
  58.9 27.5 %collective-permute-start = (bf16[4,512,128]{2,1,0:T(8,128)(2,1)}, bf16[4,512,128]{2,1,0:T(8,128)(2,1)S(1)}, u32[]{:S(2)}, u32[]{:S(2)}) collective-permute-start(bf16[4,512,128]{2,1,0:T(8,128)(2,1)} %slice.57), channel_id=1, source_target_pairs={{0,64},{8,72},{16,80},{24,88},{32,96},{40,104},{48,112},{56,120},{... | collective-permute-start | bytes 1572872 | tf_op jit(solution)/shard_map/ppermute | solution.py:509
  86.4 1.0 copy-start.1
  86.4 1.1 copy-start.4
  98.6 5.8 %collective-permute-start.5 = (bf16[128,128]{1,0:T(8,128)(2,1)S(1)}, bf16[128,128]{1,0:T(8,128)(2,1)S(1)}, u32[]{:S(2)}, u32[]{:S(2)}) collective-permute-start(bf16[128,128]{1,0:T(8,128)(2,1)S(1)} %slice_bitcast_fusion.1), channel_id=1, source_target_pairs={{0,64},{8,72},{16,80},{24,88},{32,96},{40,104},{48,112},{56,120},{... | collective-permute-start | bytes 98312 | tf_op jit(solution)/shard_map/ppermute | solution.py:509
  116.9 4.5 %collective-permute-start.6 = (f32[128,128]{1,0:T(8,128)}, f32[128,128]{1,0:T(8,128)S(1)}, u32[]{:S(2)}, u32[]{:S(2)}) collective-permute-start(f32[128,128]{1,0:T(8,128)} %head_corr.1), channel_id=1, source_target_pairs={{0,64},{8,72},{16,80},{24,88},{32,96},{40,104},{48,112},{56,120},{... | collective-permute-start | bytes 196616 | tf_op jit(solution)/shard_map/ppermute | solution.py:559
  122.3 5.9 %copy-start.9 = (f32[128,128]{1,0:T(8,128)}, f32[128,128]{1,0:T(8,128)S(1)}, u32[]{:S(2)}) copy-start(f32[128,128]{1,0:T(8,128)S(1)} %add.51.a_ref) | copy-start | bytes 196612
  122.3 5.9 %collective-permute-start.7 = (f32[128,128]{1,0:T(8,128)S(1)}, f32[128,128]{1,0:T(8,128)S(1)}, u32[]{:S(2)}, u32[]{:S(2)}) collective-permute-start(f32[128,128]{1,0:T(8,128)S(1)} %add.51.a_ref), channel_id=1, source_target_pairs={{0,128},{8,136},{16,144},{24,152},{32,160},{40,168},{48,176},{56,1... | collective-permute-start | bytes 196616 | tf_op jit(solution)/shard_map/ppermute | solution.py:559
  130.4 1.4 collective-permute-start.8
  132.4 3.6 %collective-permute-start.9 = (f32[8,128]{1,0:T(8,128)S(1)}, f32[8,128]{1,0:T(8,128)S(1)}, u32[]{:S(2)}, u32[]{:S(2)}) collective-permute-start(f32[8,128]{1,0:T(8,128)S(1)} %add.54), channel_id=1, source_target_pairs={{0,2},{1,3},{2,0},{3,1},{4,6},{5,7},{6,4},{7,5},{8,10},{9,11},{10,... | collective-permute-start | bytes 12296 | tf_op jit(solution)/shard_map/ppermute | solution.py:559
  136.1 5.1 %collective-permute-start.10 = (f32[8,128]{1,0:T(8,128)S(1)}, f32[8,128]{1,0:T(8,128)S(1)}, u32[]{:S(2)}, u32[]{:S(2)}) collective-permute-start(f32[8,128]{1,0:T(8,128)S(1)} %add.55), channel_id=1, source_target_pairs={{0,4},{1,5},{2,6},{3,7},{4,0},{5,1},{6,2},{7,3},{8,12},{9,13},{10,... | collective-permute-start | bytes 12296 | tf_op jit(solution)/shard_map/ppermute | solution.py:559
  152.3 49.9 %all-to-all-start.3 = ((bf16[8,256,128]{2,1,0:T(8,128)(2,1)}), bf16[8,256,128]{2,1,0:T(8,128)(2,1)S(1)}, u32[]{:S(2)}, u32[]{:S(2)}) async-start(bf16[8,256,128]{2,1,0:T(8,128)(2,1)} %get-tuple-element.20.out_ref), calls=%async_computation.3 | async-start | bytes 1048576 | tf_op jit(solution)/shard_map/all_to_all | solution.py:505
  156.5 5.8 %collective-permute-start.1 = (bf16[128,128]{1,0:T(8,128)(2,1)S(1)}, bf16[128,128]{1,0:T(8,128)(2,1)S(1)}, u32[]{:S(2)}, u32[]{:S(2)}) collective-permute-start(bf16[128,128]{1,0:T(8,128)(2,1)S(1)} %slice_bitcast_fusion), channel_id=1, source_target_pairs={{64,0},{72,8},{80,16},{88,24},{96,32},{104,40},{112,48},{120,56},{... | collective-permute-start | bytes 98312 | tf_op jit(solution)/shard_map/ppermute | solution.py:509
  187.8 11.5 %collective-permute-start.2 = (bf16[4,512,128]{2,1,0:T(8,128)(2,1)}, bf16[4,512,128]{2,1,0:T(8,128)(2,1)S(1)}, u32[]{:S(2)}, u32[]{:S(2)}) collective-permute-start(bf16[4,512,128]{2,1,0:T(8,128)(2,1)} %get-tuple-element.25), channel_id=1, source_target_pairs={{64,0},{72,8},{80,16},{88,24},{96,32},{104,40},{112,48},{120,56},{... | collective-permute-start | bytes 1572872 | tf_op jit(solution)/shard_map/ppermute | solution.py:509
  199.3 0.8 copy-start.7
  202.2 7.7 %copy-start.2 = (bf16[256,1024]{1,0:T(8,128)(2,1)S(1)}, bf16[256,1024]{1,0:T(8,128)(2,1)}, u32[]{:S(2)}) copy-start(bf16[256,1024]{1,0:T(8,128)(2,1)} %multiply_convert_fusion.refs_0_.g_ref) | copy-start | bytes 1572868
  202.2 0.8 copy-start.5
  203.0 86.4 %all-to-all-start.2 = ((bf16[8,768,128]{2,1,0:T(8,128)(2,1)}), bf16[8,768,128]{2,1,0:T(8,128)(2,1)S(1)}, u32[]{:S(2)}, u32[]{:S(2)}) async-start(bf16[8,768,128]{2,1,0:T(8,128)(2,1)} %join.1), calls=%async_computation.2 | async-start | bytes 3145728 | tf_op jit(solution)/shard_map/all_to_all | solution.py:505
  209.9 35.9 %collective-permute-start.3 = (bf16[128,1024]{1,0:T(8,128)(2,1)S(1)}, bf16[128,1024]{1,0:T(8,128)(2,1)S(1)}, u32[]{:S(2)}, u32[]{:S(2)}) collective-permute-start(bf16[128,1024]{1,0:T(8,128)(2,1)S(1)} %slice.59), channel_id=1, source_target_pairs={{8,0},{16,8},{24,16},{32,24},{40,32},{48,40},{56,48},{64,56},{72,6... | collective-permute-start | bytes 786440 | tf_op jit(solution)/shard_map/ppermute | solution.py:509
  263.2 10.4 %collective-permute-start.4 = (bf16[128,1024]{1,0:T(8,128)(2,1)S(1)}, bf16[128,1024]{1,0:T(8,128)(2,1)S(1)}, u32[]{:S(2)}, u32[]{:S(2)}) collective-permute-start(bf16[128,1024]{1,0:T(8,128)(2,1)S(1)} %slice.49), channel_id=1, source_target_pairs={{0,8},{8,16},{16,24},{24,32},{32,40},{40,48},{48,56},{56,64},{64,7... | collective-permute-start | bytes 786440 | tf_op jit(solution)/shard_map/ppermute | solution.py:509
  289.3 1.2 copy-start.3
  (5 other events, 3.3 us)

commit v5 on v4

--- a/solution.py
+++ b/solution.py
@@ -14,6 +14,7 @@
 TOK = 256
 EXT = TOK + TAPS
 NEG = -1e30
+GRANT = pltpu.CompilerParams(vmem_limit_bytes=8 << 20)
 STEP = 4
 SCALE = HD ** (-0.5)
 PIECES = 2
@@ -39,6 +40,7 @@
         in_specs=[pl.BlockSpec((TOK, STEP * HD), lambda h: (0, h))] * n,
         out_specs=pl.BlockSpec((STEP, n * TOK, HD), lambda h: (h, 0, 0)),
         out_shape=pltpu.HBM((heads, n * TOK, HD), arrays[0].dtype),
+        compiler_params=GRANT,
         name="pack",
     )(*arrays)
 
@@ -58,8 +60,9 @@
         in_specs=[pl.BlockSpec((STEP, rows, HD), lambda h: (h, 0, 0))],
         out_specs=[pl.BlockSpec((TOK, STEP * HD), lambda h: (0, h))] * n,
         out_shape=[jax.ShapeDtypeStruct((TOK, heads * HD), x.dtype)] * n,
+        compiler_params=GRANT,
         name="unpack",
-    )(*hbm(x))
+    )(x)
 
 
 def finish_kernel(x_ref, key_ref, mixed_grad_ref, mixed_ref, branch_ref):
@@ -82,8 +85,9 @@
         in_specs=[pl.BlockSpec((STEP, TOK, HD), lambda h: (h, 0, 0)), column, column],
         out_specs=[column] * 2,
         out_shape=[shape] * 2,
+        compiler_params=GRANT,
         name="finish",
-    )(*hbm(attn_out), key, *hbm(mixed_grad))
+    )(attn_out, key, mixed_grad)
 
 
 def join_kernel(joined_ref, own_ref, back_ref, out_ref):
@@ -100,8 +104,9 @@
         out_specs=pl.BlockSpec((2, 2 * TOK, HD), lambda b: (b + first, 0, 0)),
         out_shape=pltpu.HBM(joined.shape, joined.dtype),
         input_output_aliases={0: 0},
+        compiler_params=GRANT,
         name="join",
-    )(*hbm(joined, own, back))
+    )(*hbm(joined), own, back)
 
 
 def spread(tile_refs, ext_s, sh_s):
@@ -151,12 +156,13 @@
         grid=(conv_grad.shape[1] // HD,),
         in_specs=[column(TOK), column(TAPS), column(TAPS)],
         out_specs=column(TOK),
-        out_shape=pltpu.HBM(conv_grad.shape, jnp.float32),
+        out_shape=jax.ShapeDtypeStruct(conv_grad.shape, jnp.float32),
         scratch_shapes=[
             pltpu.VMEM((EXT + 8, HD), jnp.float32),
             pltpu.VMEM((8, EXT, HD), jnp.float32),
             pltpu.VMEM((TAPS, HD), jnp.float32),
         ],
+        compiler_params=GRANT,
         name="anti",
     )(conv_grad, edge, weights)
 
@@ -187,6 +193,7 @@
             pltpu.VMEM((TAPS, HD), jnp.float32),
         ],
         input_output_aliases={4: 0} if before else {},
+        compiler_params=GRANT,
         name="causal",
     )(mixed, edge, weights, out_grad, *hbm(*before))
 
@@ -211,14 +218,15 @@
             pl.BlockSpec((TAPS, HD), lambda b: (0, 0)),
         ],
         out_specs=pl.BlockSpec((1, TOK, HD), lambda b: (b, 0, 0)),
-        out_shape=pltpu.HBM((ROW, TOK, HD), jnp.float32),
+        out_shape=jax.ShapeDtypeStruct((ROW, TOK, HD), jnp.float32),
         scratch_shapes=[
             pltpu.VMEM((EXT + 8, HD), jnp.float32),
             pltpu.VMEM((8, EXT, HD), jnp.float32),
             pltpu.VMEM((TAPS, HD), jnp.float32),
         ],
+        compiler_params=GRANT,
         name="head_anti",
-    )(*hbm(packed, packed), edge, weights)
+    )(packed, packed, edge, weights)
 
 
 def head_corr_kernel(cur_ref, prev_ref, edge_ref, g_ref, out_ref, ext_s, sh_s, g_s, part_s):
@@ -277,8 +285,9 @@
             pltpu.VMEM((TOK, HD), jnp.float32),
             pltpu.VMEM((8, TAPS // 8, 8, HD), jnp.float32),
         ],
+        compiler_params=GRANT,
         name="head_corr",
-    )(*hbm(mixed, mixed), edge, *hbm(packed))
+    )(mixed, mixed, edge, packed)
 
 
 def dot_nn(a, b):
@@ -301,6 +310,7 @@
             jax.ShapeDtypeStruct(a.shape, jnp.float32),
             jax.ShapeDtypeStruct((8, HD), jnp.float32),
         ],
+        compiler_params=GRANT,
         name="norm_parts",
     )(a, b, weights)
 
@@ -317,6 +327,7 @@
     return pl.pallas_call(
         step_kernel,
         out_shape=jax.ShapeDtypeStruct((rows, ROW * HD), jnp.float32),
+        compiler_params=GRANT,
         name="scaled_step",
     )(got)
 
@@ -432,25 +443,18 @@
     return pl.BlockSpec(shape, lambda b, w: (0,) * len(shape))
 
 
-TOKEN_SPEC = whole(ROW, TOK, HD)
-STAT_SPEC = whole(ROW, 1, TOK)
-SHARED_SPECS = [
-    whole(ROW, 3 * TOK, HD),
-    whole(SPAN, 2 * TOK, HD),
-    STAT_SPEC,
-    whole(ROW, 2 * TOK, HD),
-]
+VMEM = pl.BlockSpec(memory_space=pltpu.VMEM)
 
 
 def attention_fwd(widths, packed, kvh, starts, qk):
-    operands = [*hbm(packed, kvh), starts, *hbm(qk)]
+    operands = [packed, kvh, starts, qk]
     return pl.pallas_call(
         fwd_kernel,
         grid_spec=pltpu.PrefetchScalarGridSpec(
             num_scalar_prefetch=1,
             grid=(1,),
-            in_specs=SHARED_SPECS,
-            out_specs=[TOKEN_SPEC, TOKEN_SPEC, STAT_SPEC, STAT_SPEC],
+            in_specs=[VMEM] * 4,
+            out_specs=[whole(ROW, TOK, HD), VMEM, VMEM, VMEM],
             scratch_shapes=[
                 pltpu.VMEM((KEYS, HD), jnp.bfloat16),
                 pltpu.VMEM((SPAN + ROW, HD, TOK), jnp.bfloat16),
@@ -458,24 +462,24 @@
         ),
         out_shape=[
             pltpu.HBM((ROW, TOK, HD), jnp.bfloat16),
-            pltpu.HBM((ROW, TOK, HD), jnp.bfloat16),
+            jax.ShapeDtypeStruct((ROW, TOK, HD), jnp.bfloat16),
             jax.ShapeDtypeStruct((ROW, 1, TOK), jnp.float32),
             jax.ShapeDtypeStruct((ROW, 1, TOK), jnp.float32),
         ],
-        compiler_params=pltpu.CompilerParams(vmem_limit_bytes=40 << 20),
+        compiler_params=pltpu.CompilerParams(vmem_limit_bytes=20 << 20),
         name="attn_fwd",
     )(widths, *operands)
 
 
 def attention_bwd(widths, packed, kvh, starts, qk, mixed_grad, out, top, inv):
-    operands = [*hbm(packed, kvh), starts, *hbm(qk, mixed_grad, out), top, inv]
+    operands = [packed, kvh, starts, qk, mixed_grad, out, top, inv]
     return pl.pallas_call(
         bwd_kernel,
         grid_spec=pltpu.PrefetchScalarGridSpec(
             num_scalar_prefetch=1,
             grid=(1,),
-            in_specs=SHARED_SPECS + [TOKEN_SPEC, TOKEN_SPEC, STAT_SPEC, STAT_SPEC],
-            out_specs=[whole(ROW, 3 * TOK, HD)] + [whole(SPAN, 2 * TOK, HD)] * 2,
+            in_specs=[VMEM] * 8,
+            out_specs=[whole(ROW, 3 * TOK, HD), VMEM, VMEM],
             scratch_shapes=[
                 pltpu.VMEM((KEYS, HD), jnp.bfloat16),
                 pltpu.VMEM((KEYS, HD), jnp.bfloat16),
@@ -486,10 +490,10 @@
         ),
         out_shape=[
             pltpu.HBM((ROW, 3 * TOK, HD), jnp.bfloat16),
-            pltpu.HBM((SPAN, 2 * TOK, HD), jnp.float32),
-            pltpu.HBM((SPAN, 2 * TOK, HD), jnp.bfloat16),
-        ],
-        compiler_params=pltpu.CompilerParams(vmem_limit_bytes=40 << 20),
+            jax.ShapeDtypeStruct((SPAN, 2 * TOK, HD), jnp.float32),
+            jax.ShapeDtypeStruct((SPAN, 2 * TOK, HD), jnp.bfloat16),
+        ],
+        compiler_params=pltpu.CompilerParams(vmem_limit_bytes=28 << 20),
         name="attn_bwd",
     )(widths, *operands)
 

time: 294 us -> 269 us (0.915)
  the two profiles are of different devices: /device:TPU:18 before, /device:TPU:10 now
where the time goes in v5:
time: 269 us; the launch traced here: 268 us
  waiting for transfers between devices  130 us (48%)
  Pallas kernels  74 us (28%)
  starting transfers between devices  47 us (17%)
  blocking collectives  10.4 us (4%)
  other arithmetic  2.83 us (1%)
  local copies, waits for them, and re-layouts  2.8 us (1%)
    all_to_all x4, waiting for transfers between devices, swap(): return lax.all_to_all(x, axis, 0, 0, axis_index_groups=groups, tiled=True)  62.6 us
    ppermute x6, waiting for transfers between devices, shift(): return lax.ppermute(x, 'seq', pairs)  52.7 us
    all_to_all x4, starting transfers between devices, swap(): return lax.all_to_all(x, axis, 0, 0, axis_index_groups=groups, tiled=True)  23.1 us
    ppermute x6, starting transfers between devices, shift(): return lax.ppermute(x, 'seq', pairs)  19.3 us
    ppermute x5, waiting for transfers between devices, partner(): return lax.ppermute(x, axis, pairs)  14.8 us
    pallas_call x2, Pallas kernels, causal_piece(): pl.pallas_call(causal_kernel, grid=(tiles,), in_specs=[column(TOK), colum...  13.6 us
    pallas_call x1, Pallas kernels, anti(): pl.pallas_call(anti_kernel, grid=(conv_grad.shape[1] // HD,), in_specs=[c...  12 us
    pallas_call x1, Pallas kernels, head_anti(): pl.pallas_call(head_anti_kernel, grid=(ROW,), in_specs=[pl.BlockSpec((1,...  11.3 us
  transfers between devices with their start and end apart: 15, of which 12 were waited for; matrix products, arithmetic and copies ran while one was open for 1% of the time, Pallas kernels for 19%

profile of v5, /device:TPU:10, one launch (start us, length us, event | category | flops | bytes accessed | tf_op | source)
XLA Modules:
  0.0 268.3 jit_solution(591834234447790975)
XLA Ops:
  3.6 8.6 %all-to-all-start = ((bf16[8,768,128]{2,1,0:T(8,128)(2,1)}), bf16[8,768,128]{2,1,0:T(8,128)(2,1)S(1)}, u32[]{:S(2)}, u32[]{:S(2)}) async-start(bf16[8,768,128]{2,1,0:T(8,128)(2,1)} %pack.2), calls=%async_computation | async-start | bytes 3145728 | tf_op jit(solution)/shard_map/all_to_all | solution.py:509
  13.4 38.8 %all-to-all-done.cur_ref.next_ref.packed_ref.g_ref = bf16[8,768,128]{2,1,0:T(8,128)(2,1)S(1)} async-done(((bf16[8,768,128]{2,1,0:T(8,128)(2,1)}), bf16[8,768,128]{2,1,0:T(8,128)(2,1)S(1)}, u32[]{:S(2)}, u32[]{:S(2)}) %all-to-all-start) | async-done | bytes 1572896 | tf_op jit(solution)/shard_map/all_to_all | solution.py:509
  52.2 3.6 %all-to-all-start.1 = ((bf16[8,512,128]{2,1,0:T(8,128)(2,1)}), bf16[8,512,128]{2,1,0:T(8,128)(2,1)S(1)}, u32[]{:S(2)}, u32[]{:S(2)}) async-start(bf16[8,512,128]{2,1,0:T(8,128)(2,1)} %pack.3), calls=%async_computation.1 | async-start | bytes 2097152 | tf_op jit(solution)/shard_map/all_to_all | solution.py:509
  57.4 3.4 %collective-permute-start = (bf16[4,512,128]{2,1,0:T(8,128)(2,1)}, bf16[4,512,128]{2,1,0:T(8,128)(2,1)}, u32[]{:S(2)}, u32[]{:S(2)}) collective-permute-start(bf16[4,512,128]{2,1,0:T(8,128)(2,1)} %slice.57), channel_id=1, source_target_pairs={{0,64},{8,72},{16,80},{24,88},{32,96},{40,104},{48,112},{56,120},{... | collective-permute-start | bytes 1572872 | tf_op jit(solution)/shard_map/ppermute | solution.py:513
  61.0 23.9 %all-to-all-done.1.qk_ref = bf16[8,512,128]{2,1,0:T(8,128)(2,1)S(1)} async-done(((bf16[8,512,128]{2,1,0:T(8,128)(2,1)}), bf16[8,512,128]{2,1,0:T(8,128)(2,1)S(1)}, u32[]{:S(2)}, u32[]{:S(2)}) %all-to-all-start.1) | async-done | bytes 1048608 | tf_op jit(solution)/shard_map/all_to_all | solution.py:509
  84.9 9.3 %attn_fwd.1 = (bf16[8,256,128]{2,1,0:T(8,128)(2,1)}, bf16[8,256,128]{2,1,0:T(8,128)(2,1)S(1)}, f32[8,1,256]{2,1,0:T(1,128)S(1)}, f32[8,1,256]{2,1,0:T(1,128)S(1)}) custom-call(s32[8]{0:T(128)S(1)} %fusion.4.width_ref, bf16[8,768,128]{2,1,0:T(8,128)(2,1)S(1)} %all-to-all-done.cur_ref.next_ref.packed_ref.g_ref, ...), custom_call_target="tpu_custom_call" | custom-call | tf_op jit(solution)/shard_map/attn_fwd/pallas_call | solution.py:451
  94.2 3.5 %collective-permute-start.5 = (bf16[128,128]{1,0:T(8,128)(2,1)S(1)}, bf16[128,128]{1,0:T(8,128)(2,1)S(1)}, u32[]{:S(2)}, u32[]{:S(2)}) collective-permute-start(bf16[128,128]{1,0:T(8,128)(2,1)S(1)} %slice_bitcast_fusion.1), channel_id=1, source_target_pairs={{0,64},{8,72},{16,80},{24,88},{32,96},{40,104},{48,112},{56,120},{... | collective-permute-start | bytes 98312 | tf_op jit(solution)/shard_map/ppermute | solution.py:513
  100.2 10.2 %head_corr.1 = f32[128,128]{1,0:T(8,128)S(1)} custom-call(bf16[8,256,128]{2,1,0:T(8,128)(2,1)S(1)} %get-tuple-element.31.cur_ref.prev_ref, bf16[8,256,128]{2,1,0:T(8,128)(2,1)S(1)} %get-tuple-element.31.cur_ref.prev_ref, bf16[128,128]{1,0:T(8,128)(2,1)S(1)} %collective-permute-done.5.edge_ref, ...), custom_call_target="tpu_custom_call" | custom-call | tf_op jit(solution)/shard_map/head_corr/pallas_call | solution.py:271
  110.5 4.3 %collective-permute-done.6 = f32[128,128]{1,0:T(8,128)} collective-permute-done((f32[128,128]{1,0:T(8,128)S(1)}, f32[128,128]{1,0:T(8,128)}, u32[]{:S(2)}, u32[]{:S(2)}) %collective-permute-start.6) | collective-permute-done | bytes 65568 | tf_op jit(solution)/shard_map/ppermute | solution.py:563
  117.5 4.1 %collective-permute-done.7.b_ref = f32[128,128]{1,0:T(8,128)S(1)} collective-permute-done((f32[128,128]{1,0:T(8,128)S(1)}, f32[128,128]{1,0:T(8,128)S(1)}, u32[]{:S(2)}, u32[]{:S(2)}) %collective-permute-start.7) | collective-permute-done | bytes 65568 | tf_op jit(solution)/shard_map/ppermute | solution.py:563
  132.2 10.4 %all_to_all.25.got_ref = f32[8,8,128]{2,1,0:T(8,128)S(1)} all-to-all(f32[8,8,128]{2,1,0:T(8,128)S(1)} %pad_maximum_fusion), channel_id=1, replica_groups={{0,8,16,24,32,40,48,56},{64,72,80,88,96,104,112,120},{128,136,144,152,1..., dimensions={0} | all-to-all | bytes 65536 | tf_op jit(solution)/shard_map/all_to_all | solution.py:509
  142.6 4.1 %all-to-all-start.3 = ((bf16[8,256,128]{2,1,0:T(8,128)(2,1)}), bf16[8,256,128]{2,1,0:T(8,128)(2,1)}, u32[]{:S(2)}, u32[]{:S(2)}) async-start(bf16[8,256,128]{2,1,0:T(8,128)(2,1)} %get-tuple-element.20.out_ref), calls=%async_computation.3 | async-start | bytes 1048576 | tf_op jit(solution)/shard_map/all_to_all | solution.py:509
  149.0 3.6 %collective-permute-done.1.edge_ref = bf16[128,128]{1,0:T(8,128)(2,1)S(1)} collective-permute-done((bf16[128,128]{1,0:T(8,128)(2,1)S(1)}, bf16[128,128]{1,0:T(8,128)(2,1)S(1)}, u32[]{:S(2)}, u32[]{:S(2)}) %collective-permute-start.1) | collective-permute-done | bytes 32800 | tf_op jit(solution)/shard_map/ppermute | solution.py:513
  152.6 11.3 %head_anti.1.mixed_grad_ref = f32[8,256,128]{2,1,0:T(8,128)S(1)} custom-call(bf16[8,768,128]{2,1,0:T(8,128)(2,1)S(1)} %all-to-all-done.cur_ref.next_ref.packed_ref.g_ref, bf16[8,768,128]{2,1,0:T(8,128)(2,1)S(1)} %all-to-all-done.cur_ref.next_ref.packed_ref.g_ref, bf16[128,128]{1,0:T(8,128)(2,1)S(1)} %collective-permute-done.1.edge_ref, ...), custom_call_target="tpu_custom_call" | custom-call | tf_op jit(solution)/shard_map/head_anti/pallas_call | solution.py:211
  164.0 10.0 %attn_bwd.1 = (bf16[8,768,128]{2,1,0:T(8,128)(2,1)}, f32[4,512,128]{2,1,0:T(8,128)S(1)}, bf16[4,512,128]{2,1,0:T(8,128)(2,1)S(1)}) custom-call(s32[8]{0:T(128)S(1)} %fusion.4.width_ref, bf16[8,768,128]{2,1,0:T(8,128)(2,1)S(1)} %all-to-all-done.cur_ref.next_ref.packed_ref.g_ref, bf16[4,512,128]{2,1,0:T(8,128)(2,1)} %collective-permute-done.kvh_ref, ...), custom_call_target="tpu_custom_call" | custom-call | tf_op jit(solution)/shard_map/attn_bwd/pallas_call | solution.py:476
  175.9 9.4 %collective-permute-done.2.back_ref = bf16[4,512,128]{2,1,0:T(8,128)(2,1)S(1)} collective-permute-done((bf16[4,512,128]{2,1,0:T(8,128)(2,1)S(1)}, bf16[4,512,128]{2,1,0:T(8,128)(2,1)S(1)}, u32[]{:S(2)}, u32[]{:S(2)}) %collective-permute-start.2) | collective-permute-done | bytes 524320 | tf_op jit(solution)/shard_map/ppermute | solution.py:513
  186.1 6.9 %all-to-all-start.2 = ((bf16[8,768,128]{2,1,0:T(8,128)(2,1)}), bf16[8,768,128]{2,1,0:T(8,128)(2,1)S(1)}, u32[]{:S(2)}, u32[]{:S(2)}) async-start(bf16[8,768,128]{2,1,0:T(8,128)(2,1)} %join.1), calls=%async_computation.2 | async-start | bytes 3145728 | tf_op jit(solution)/shard_map/all_to_all | solution.py:509
  193.0 4.9 %collective-permute-start.3 = (bf16[128,1024]{1,0:T(8,128)(2,1)S(1)}, bf16[128,1024]{1,0:T(8,128)(2,1)S(1)}, u32[]{:S(2)}, u32[]{:S(2)}) collective-permute-start(bf16[128,1024]{1,0:T(8,128)(2,1)S(1)} %slice.59), channel_id=1, source_target_pairs={{8,0},{16,8},{24,16},{32,24},{40,32},{48,40},{56,48},{64,56},{72,6... | collective-permute-start | bytes 786440 | tf_op jit(solution)/shard_map/ppermute | solution.py:513
  198.0 31.0 %collective-permute-done.3.edge_ref = bf16[128,1024]{1,0:T(8,128)(2,1)S(1)} collective-permute-done((bf16[128,1024]{1,0:T(8,128)(2,1)S(1)}, bf16[128,1024]{1,0:T(8,128)(2,1)S(1)}, u32[]{:S(2)}, u32[]{:S(2)}) %collective-permute-start.3) | collective-permute-done | bytes 262176 | tf_op jit(solution)/shard_map/ppermute | solution.py:513
  229.0 12.0 %anti.1.mixed_grad_ref = f32[256,1024]{1,0:T(8,128)S(1)} custom-call(bf16[256,1024]{1,0:T(8,128)(2,1)S(1)} %multiply_convert_fusion.refs_0_.g_ref, bf16[128,1024]{1,0:T(8,128)(2,1)S(1)} %collective-permute-done.3.edge_ref, bf16[128,1024]{1,0:T(8,128)(2,1)S(1)} %copy-done.1), custom_call_target="tpu_custom_call" | custom-call | tf_op jit(solution)/shard_map/anti/pallas_call | solution.py:154
  243.0 3.4 %collective-permute-start.4 = (bf16[128,1024]{1,0:T(8,128)(2,1)S(1)}, bf16[128,1024]{1,0:T(8,128)(2,1)S(1)}, u32[]{:S(2)}, u32[]{:S(2)}) collective-permute-start(bf16[128,1024]{1,0:T(8,128)(2,1)S(1)} %slice.49), channel_id=1, source_target_pairs={{0,8},{8,16},{16,24},{24,32},{32,40},{40,48},{48,56},{56,64},{64,7... | collective-permute-start | bytes 786440 | tf_op jit(solution)/shard_map/ppermute | solution.py:513
  247.0 6.4 %collective-permute-done.4.edge_ref = bf16[128,1024]{1,0:T(8,128)(2,1)S(1)} collective-permute-done((bf16[128,1024]{1,0:T(8,128)(2,1)S(1)}, bf16[128,1024]{1,0:T(8,128)(2,1)S(1)}, u32[]{:S(2)}, u32[]{:S(2)}) %collective-permute-start.4) | collective-permute-done | bytes 262176 | tf_op jit(solution)/shard_map/ppermute | solution.py:513
  253.4 6.8 %causal.2.refs_0_ = bf16[256,1024]{1,0:T(8,128)(2,1)} custom-call(bf16[256,1024]{1,0:T(8,128)(2,1)S(1)} %get-tuple-element.29.m_ref, bf16[128,1024]{1,0:T(8,128)(2,1)S(1)} %collective-permute-done.4.edge_ref, bf16[128,1024]{1,0:T(8,128)(2,1)S(1)} %copy-done.1, bf16[256,1024]{1,0:T(8,128)(2,1)S(1)} %copy-done), custom_call_target="tpu_custom_call" | custom-call | tf_op jit(solution)/shard_map/causal/pallas_call | solution.py:183
  260.2 6.8 %causal.3 = bf16[256,1024]{1,0:T(8,128)(2,1)} custom-call(bf16[256,1024]{1,0:T(8,128)(2,1)S(1)} %get-tuple-element.29.m_ref, bf16[128,1024]{1,0:T(8,128)(2,1)S(1)} %collective-permute-done.4.edge_ref, bf16[128,1024]{1,0:T(8,128)(2,1)S(1)} %copy-done.1, bf16[256,1024]{1,0:T(8,128)(2,1)S(1)} %copy-done, ...), custom_call_target="tpu_custom_call", output_to_operand_aliasing={{}: (4, {})} | custom-call | tf_op jit(solution)/shard_map/causal/pallas_call | solution.py:183
  (70 shorter events, 30.6 us)
Async XLA Ops:
  0.6 1.5 copy-start.5
  0.6 1.5 copy-start.6
  3.6 8.6 %copy-start.3 = (bf16[256,1024]{1,0:T(8,128)(2,1)S(1)}, bf16[256,1024]{1,0:T(8,128)(2,1)}, u32[]{:S(2)}) copy-start(bf16[256,1024]{1,0:T(8,128)(2,1)} %key_ref.1) | copy-start | bytes 1572868
  3.6 8.6 %copy-start.7 = (bf16[256,1024]{1,0:T(8,128)(2,1)S(1)}, bf16[256,1024]{1,0:T(8,128)(2,1)}, u32[]{:S(2)}) copy-start(bf16[256,1024]{1,0:T(8,128)(2,1)} %refs_0_.1) | copy-start | bytes 1572868
  3.6 48.6 %all-to-all-start = ((bf16[8,768,128]{2,1,0:T(8,128)(2,1)}), bf16[8,768,128]{2,1,0:T(8,128)(2,1)S(1)}, u32[]{:S(2)}, u32[]{:S(2)}) async-start(bf16[8,768,128]{2,1,0:T(8,128)(2,1)} %pack.2), calls=%async_computation | async-start | bytes 3145728 | tf_op jit(solution)/shard_map/all_to_all | solution.py:509
  13.4 42.4 %copy-start.9 = (s32[8192]{0:T(1024)S(1)}, s32[8192]{0:T(1024)}, u32[]{:S(2)}) copy-start(s32[8192]{0:T(1024)} %param.15) | copy-start | bytes 98308
  52.2 32.7 %all-to-all-start.1 = ((bf16[8,512,128]{2,1,0:T(8,128)(2,1)}), bf16[8,512,128]{2,1,0:T(8,128)(2,1)S(1)}, u32[]{:S(2)}, u32[]{:S(2)}) async-start(bf16[8,512,128]{2,1,0:T(8,128)(2,1)} %pack.3), calls=%async_computation.1 | async-start | bytes 2097152 | tf_op jit(solution)/shard_map/all_to_all | solution.py:509
  57.4 27.5 %collective-permute-start = (bf16[4,512,128]{2,1,0:T(8,128)(2,1)}, bf16[4,512,128]{2,1,0:T(8,128)(2,1)}, u32[]{:S(2)}, u32[]{:S(2)}) collective-permute-start(bf16[4,512,128]{2,1,0:T(8,128)(2,1)} %slice.57), channel_id=1, source_target_pairs={{0,64},{8,72},{16,80},{24,88},{32,96},{40,104},{48,112},{56,120},{... | collective-permute-start | bytes 1572872 | tf_op jit(solution)/shard_map/ppermute | solution.py:513
  94.2 23.2 %copy-start.1 = (bf16[128,1024]{1,0:T(8,128)(2,1)S(1)}, bf16[128,1024]{1,0:T(8,128)(2,1)}, u32[]{:S(2)}) copy-start(bf16[128,1024]{1,0:T(8,128)(2,1)} %w_ref.5) | copy-start | bytes 786436
  94.2 5.9 %collective-permute-start.5 = (bf16[128,128]{1,0:T(8,128)(2,1)S(1)}, bf16[128,128]{1,0:T(8,128)(2,1)S(1)}, u32[]{:S(2)}, u32[]{:S(2)}) collective-permute-start(bf16[128,128]{1,0:T(8,128)(2,1)S(1)} %slice_bitcast_fusion.1), channel_id=1, source_target_pairs={{0,64},{8,72},{16,80},{24,88},{32,96},{40,104},{48,112},{56,120},{... | collective-permute-start | bytes 98312 | tf_op jit(solution)/shard_map/ppermute | solution.py:513
  110.4 4.5 %collective-permute-start.6 = (f32[128,128]{1,0:T(8,128)S(1)}, f32[128,128]{1,0:T(8,128)}, u32[]{:S(2)}, u32[]{:S(2)}) collective-permute-start(f32[128,128]{1,0:T(8,128)S(1)} %head_corr.1), channel_id=1, source_target_pairs={{0,64},{8,72},{16,80},{24,88},{32,96},{40,104},{48,112},{56,120},{... | collective-permute-start | bytes 196616 | tf_op jit(solution)/shard_map/ppermute | solution.py:563
  115.7 5.8 %collective-permute-start.7 = (f32[128,128]{1,0:T(8,128)S(1)}, f32[128,128]{1,0:T(8,128)S(1)}, u32[]{:S(2)}, u32[]{:S(2)}) collective-permute-start(f32[128,128]{1,0:T(8,128)S(1)} %add.51.a_ref), channel_id=1, source_target_pairs={{0,128},{8,136},{16,144},{24,152},{32,160},{40,168},{48,176},{56,1... | collective-permute-start | bytes 196616 | tf_op jit(solution)/shard_map/ppermute | solution.py:563
  122.3 1.2 collective-permute-start.8
  123.5 3.6 %collective-permute-start.9 = (f32[8,128]{1,0:T(8,128)S(1)}, f32[8,128]{1,0:T(8,128)S(1)}, u32[]{:S(2)}, u32[]{:S(2)}) collective-permute-start(f32[8,128]{1,0:T(8,128)S(1)} %add.54), channel_id=1, source_target_pairs={{0,2},{1,3},{2,0},{3,1},{4,6},{5,7},{6,4},{7,5},{8,10},{9,11},{10,... | collective-permute-start | bytes 12296 | tf_op jit(solution)/shard_map/ppermute | solution.py:563
  127.1 5.1 %collective-permute-start.10 = (f32[8,128]{1,0:T(8,128)S(1)}, f32[8,128]{1,0:T(8,128)S(1)}, u32[]{:S(2)}, u32[]{:S(2)}) collective-permute-start(f32[8,128]{1,0:T(8,128)S(1)} %add.55), channel_id=1, source_target_pairs={{0,4},{1,5},{2,6},{3,7},{4,0},{5,1},{6,2},{7,3},{8,12},{9,13},{10,... | collective-permute-start | bytes 12296 | tf_op jit(solution)/shard_map/ppermute | solution.py:563
  142.6 43.5 %all-to-all-start.3 = ((bf16[8,256,128]{2,1,0:T(8,128)(2,1)}), bf16[8,256,128]{2,1,0:T(8,128)(2,1)}, u32[]{:S(2)}, u32[]{:S(2)}) async-start(bf16[8,256,128]{2,1,0:T(8,128)(2,1)} %get-tuple-element.20.out_ref), calls=%async_computation.3 | async-start | bytes 1048576 | tf_op jit(solution)/shard_map/all_to_all | solution.py:509
  146.8 5.8 %collective-permute-start.1 = (bf16[128,128]{1,0:T(8,128)(2,1)S(1)}, bf16[128,128]{1,0:T(8,128)(2,1)S(1)}, u32[]{:S(2)}, u32[]{:S(2)}) collective-permute-start(bf16[128,128]{1,0:T(8,128)(2,1)S(1)} %slice_bitcast_fusion), channel_id=1, source_target_pairs={{64,0},{72,8},{80,16},{88,24},{96,32},{104,40},{112,48},{120,56},{... | collective-permute-start | bytes 98312 | tf_op jit(solution)/shard_map/ppermute | solution.py:513
  149.0 15.0 %copy-start.2 = (bf16[8,256,128]{2,1,0:T(8,128)(2,1)S(1)}, bf16[8,256,128]{2,1,0:T(8,128)(2,1)}, u32[]{:S(2)}) copy-start(bf16[8,256,128]{2,1,0:T(8,128)(2,1)} %get-tuple-element.20.out_ref) | copy-start | bytes 1572868
  174.0 11.3 %collective-permute-start.2 = (bf16[4,512,128]{2,1,0:T(8,128)(2,1)S(1)}, bf16[4,512,128]{2,1,0:T(8,128)(2,1)S(1)}, u32[]{:S(2)}, u32[]{:S(2)}) collective-permute-start(bf16[4,512,128]{2,1,0:T(8,128)(2,1)S(1)} %get-tuple-element.25), channel_id=1, source_target_pairs={{64,0},{72,8},{80,16},{88,24},{96,32},{104,40},{112,48},{120,56},{... | collective-permute-start | bytes 1572872 | tf_op jit(solution)/shard_map/ppermute | solution.py:513
  186.1 80.8 %all-to-all-start.2 = ((bf16[8,768,128]{2,1,0:T(8,128)(2,1)}), bf16[8,768,128]{2,1,0:T(8,128)(2,1)S(1)}, u32[]{:S(2)}, u32[]{:S(2)}) async-start(bf16[8,768,128]{2,1,0:T(8,128)(2,1)} %join.1), calls=%async_computation.2 | async-start | bytes 3145728 | tf_op jit(solution)/shard_map/all_to_all | solution.py:509
  193.0 48.0 %copy-start.4 = (bf16[256,1024]{1,0:T(8,128)(2,1)S(1)}, bf16[256,1024]{1,0:T(8,128)(2,1)}, u32[]{:S(2)}) copy-start(bf16[256,1024]{1,0:T(8,128)(2,1)} %key_ref.1) | copy-start | bytes 1572868
  193.0 35.9 %collective-permute-start.3 = (bf16[128,1024]{1,0:T(8,128)(2,1)S(1)}, bf16[128,1024]{1,0:T(8,128)(2,1)S(1)}, u32[]{:S(2)}, u32[]{:S(2)}) collective-permute-start(bf16[128,1024]{1,0:T(8,128)(2,1)S(1)} %slice.59), channel_id=1, source_target_pairs={{8,0},{16,8},{24,16},{32,24},{40,32},{48,40},{56,48},{64,56},{72,6... | collective-permute-start | bytes 786440 | tf_op jit(solution)/shard_map/ppermute | solution.py:513
  241.0 12.4 %copy-start = (bf16[256,1024]{1,0:T(8,128)(2,1)S(1)}, bf16[256,1024]{1,0:T(8,128)(2,1)}, u32[]{:S(2)}) copy-start(bf16[256,1024]{1,0:T(8,128)(2,1)} %grad_ref.3) | copy-start | bytes 1572868
  243.0 10.4 %collective-permute-start.4 = (bf16[128,1024]{1,0:T(8,128)(2,1)S(1)}, bf16[128,1024]{1,0:T(8,128)(2,1)S(1)}, u32[]{:S(2)}, u32[]{:S(2)}) collective-permute-start(bf16[128,1024]{1,0:T(8,128)(2,1)S(1)} %slice.49), channel_id=1, source_target_pairs={{0,8},{8,16},{16,24},{24,32},{32,40},{40,48},{48,56},{56,64},{64,7... | collective-permute-start | bytes 786440 | tf_op jit(solution)/shard_map/ppermute | solution.py:513
  (1 other events, 0.6 us)

commit v6 on v5

--- a/solution.py
+++ b/solution.py
@@ -78,7 +78,7 @@
 def finish(attn_out, key, mixed_grad):
     heads = attn_out.shape[0]
     column = pl.BlockSpec((TOK, STEP * HD), lambda h: (0, h))
-    shape = jax.ShapeDtypeStruct((TOK, heads * HD), jnp.bfloat16)
+    shape = pltpu.HBM((TOK, heads * HD), jnp.bfloat16)
     return pl.pallas_call(
         finish_kernel,
         grid=(heads // STEP,),
@@ -87,7 +87,7 @@
         out_shape=[shape] * 2,
         compiler_params=GRANT,
         name="finish",
-    )(attn_out, key, mixed_grad)
+    )(attn_out, *hbm(key, mixed_grad))
 
 
 def join_kernel(joined_ref, own_ref, back_ref, out_ref):
@@ -156,7 +156,7 @@
         grid=(conv_grad.shape[1] // HD,),
         in_specs=[column(TOK), column(TAPS), column(TAPS)],
         out_specs=column(TOK),
-        out_shape=jax.ShapeDtypeStruct(conv_grad.shape, jnp.float32),
+        out_shape=pltpu.HBM(conv_grad.shape, jnp.float32),
         scratch_shapes=[
             pltpu.VMEM((EXT + 8, HD), jnp.float32),
             pltpu.VMEM((8, EXT, HD), jnp.float32),
@@ -195,7 +195,7 @@
         input_output_aliases={4: 0} if before else {},
         compiler_params=GRANT,
         name="causal",
-    )(mixed, edge, weights, out_grad, *hbm(*before))
+    )(*hbm(mixed, edge, weights, out_grad, *before))
 
 
 def head_anti_kernel(cur_ref, next_ref, edge_ref, w_ref, out_ref, ext_s, sh_s, w_s):
@@ -218,7 +218,7 @@
             pl.BlockSpec((TAPS, HD), lambda b: (0, 0)),
         ],
         out_specs=pl.BlockSpec((1, TOK, HD), lambda b: (b, 0, 0)),
-        out_shape=jax.ShapeDtypeStruct((ROW, TOK, HD), jnp.float32),
+        out_shape=pltpu.HBM((ROW, TOK, HD), jnp.float32),
         scratch_shapes=[
             pltpu.VMEM((EXT + 8, HD), jnp.float32),
             pltpu.VMEM((8, EXT, HD), jnp.float32),
@@ -447,13 +447,13 @@
 
 
 def attention_fwd(widths, packed, kvh, starts, qk):
-    operands = [packed, kvh, starts, qk]
+    operands = [packed, *hbm(kvh), starts, qk]
     return pl.pallas_call(
         fwd_kernel,
         grid_spec=pltpu.PrefetchScalarGridSpec(
             num_scalar_prefetch=1,
             grid=(1,),
-            in_specs=[VMEM] * 4,
+            in_specs=[VMEM, whole(SPAN, 2 * TOK, HD), VMEM, VMEM],
             out_specs=[whole(ROW, TOK, HD), VMEM, VMEM, VMEM],
             scratch_shapes=[
                 pltpu.VMEM((KEYS, HD), jnp.bfloat16),
@@ -472,13 +472,15 @@
 
 
 def attention_bwd(widths, packed, kvh, starts, qk, mixed_grad, out, top, inv):
-    operands = [packed, kvh, starts, qk, mixed_grad, out, top, inv]
+    operands = [packed, *hbm(kvh), starts, qk, *hbm(mixed_grad, out), top, inv]
     return pl.pallas_call(
         bwd_kernel,
         grid_spec=pltpu.PrefetchScalarGridSpec(
             num_scalar_prefetch=1,
             grid=(1,),
-            in_specs=[VMEM] * 8,
+            in_specs=[VMEM, whole(SPAN, 2 * TOK, HD), VMEM, VMEM]
+            + [whole(ROW, TOK, HD)] * 2
+            + [VMEM] * 2,
             out_specs=[whole(ROW, 3 * TOK, HD), VMEM, VMEM],
             scratch_shapes=[
                 pltpu.VMEM((KEYS, HD), jnp.bfloat16),

time: 269 us -> 275 us (1.022)
  Pallas kernels: 74 us -> 77.8 us
  transfers between devices with their start and end apart: 15 -> 15, of which waited for: 12 -> 12; matrix products, arithmetic and copies ran while one was open for 1% -> 1% of each run, Pallas kernels for 19% -> 20%
where the time goes in v6:
time: 275 us; the launch traced here: 274 us
  waiting for transfers between devices  130 us (47%)
  Pallas kernels  77.8 us (28%)
  starting transfers between devices  46.9 us (17%)
  blocking collectives  10.4 us (4%)
  local copies, waits for them, and re-layouts  4.43 us (2%)
  other arithmetic  2.83 us (1%)
    all_to_all x4, waiting for transfers between devices, swap(): return lax.all_to_all(x, axis, 0, 0, axis_index_groups=groups, tiled=True)  62.6 us
    ppermute x6, waiting for transfers between devices, shift(): return lax.ppermute(x, 'seq', pairs)  52.9 us
    all_to_all x4, starting transfers between devices, swap(): return lax.all_to_all(x, axis, 0, 0, axis_index_groups=groups, tiled=True)  23.2 us
    ppermute x6, starting transfers between devices, shift(): return lax.ppermute(x, 'seq', pairs)  19.2 us
    pallas_call x2, Pallas kernels, causal_piece(): pl.pallas_call(causal_kernel, grid=(tiles,), in_specs=[column(TOK), colum...  15 us
    ppermute x5, waiting for transfers between devices, partner(): return lax.ppermute(x, axis, pairs)  14.8 us
    pallas_call x1, Pallas kernels, anti(): pl.pallas_call(anti_kernel, grid=(conv_grad.shape[1] // HD,), in_specs=[c...  12.7 us
    pallas_call x1, Pallas kernels, head_anti(): pl.pallas_call(head_anti_kernel, grid=(ROW,), in_specs=[pl.BlockSpec((1,...  12 us
  transfers between devices with their start and end apart: 15, of which 12 were waited for; matrix products, arithmetic and copies ran while one was open for 1% of the time, Pallas kernels for 20%

profile of v6, /device:TPU:10, one launch (start us, length us, event | category | flops | bytes accessed | tf_op | source)
XLA Modules:
  0.0 273.6 jit_solution(18037243932446360380)
XLA Ops:
  3.6 8.6 %all-to-all-start = ((bf16[8,768,128]{2,1,0:T(8,128)(2,1)}), bf16[8,768,128]{2,1,0:T(8,128)(2,1)S(1)}, u32[]{:S(2)}, u32[]{:S(2)}) async-start(bf16[8,768,128]{2,1,0:T(8,128)(2,1)} %pack.2), calls=%async_computation | async-start | bytes 3145728 | tf_op jit(solution)/shard_map/all_to_all | solution.py:511
  13.4 38.8 %all-to-all-done.cur_ref.next_ref.packed_ref.g_ref = bf16[8,768,128]{2,1,0:T(8,128)(2,1)S(1)} async-done(((bf16[8,768,128]{2,1,0:T(8,128)(2,1)}), bf16[8,768,128]{2,1,0:T(8,128)(2,1)S(1)}, u32[]{:S(2)}, u32[]{:S(2)}) %all-to-all-start) | async-done | bytes 1572896 | tf_op jit(solution)/shard_map/all_to_all | solution.py:511
  52.2 3.6 %all-to-all-start.1 = ((bf16[8,512,128]{2,1,0:T(8,128)(2,1)}), bf16[8,512,128]{2,1,0:T(8,128)(2,1)S(1)}, u32[]{:S(2)}, u32[]{:S(2)}) async-start(bf16[8,512,128]{2,1,0:T(8,128)(2,1)} %pack.3), calls=%async_computation.1 | async-start | bytes 2097152 | tf_op jit(solution)/shard_map/all_to_all | solution.py:511
  57.4 3.4 %collective-permute-start = (bf16[4,512,128]{2,1,0:T(8,128)(2,1)}, bf16[4,512,128]{2,1,0:T(8,128)(2,1)}, u32[]{:S(2)}, u32[]{:S(2)}) collective-permute-start(bf16[4,512,128]{2,1,0:T(8,128)(2,1)} %slice.57), channel_id=1, source_target_pairs={{0,64},{8,72},{16,80},{24,88},{32,96},{40,104},{48,112},{56,120},{... | collective-permute-start | bytes 1572872 | tf_op jit(solution)/shard_map/ppermute | solution.py:515
  61.0 23.9 %all-to-all-done.1.qk_ref = bf16[8,512,128]{2,1,0:T(8,128)(2,1)S(1)} async-done(((bf16[8,512,128]{2,1,0:T(8,128)(2,1)}), bf16[8,512,128]{2,1,0:T(8,128)(2,1)S(1)}, u32[]{:S(2)}, u32[]{:S(2)}) %all-to-all-start.1) | async-done | bytes 1048608 | tf_op jit(solution)/shard_map/all_to_all | solution.py:511
  84.9 9.3 %attn_fwd.1 = (bf16[8,256,128]{2,1,0:T(8,128)(2,1)}, bf16[8,256,128]{2,1,0:T(8,128)(2,1)S(1)}, f32[8,1,256]{2,1,0:T(1,128)S(1)}, f32[8,1,256]{2,1,0:T(1,128)S(1)}) custom-call(s32[8]{0:T(128)S(1)} %fusion.4.width_ref, bf16[8,768,128]{2,1,0:T(8,128)(2,1)S(1)} %all-to-all-done.cur_ref.next_ref.packed_ref.g_ref, ...), custom_call_target="tpu_custom_call" | custom-call | tf_op jit(solution)/shard_map/attn_fwd/pallas_call | solution.py:451
  94.2 3.5 %collective-permute-start.5 = (bf16[128,128]{1,0:T(8,128)(2,1)S(1)}, bf16[128,128]{1,0:T(8,128)(2,1)S(1)}, u32[]{:S(2)}, u32[]{:S(2)}) collective-permute-start(bf16[128,128]{1,0:T(8,128)(2,1)S(1)} %slice_bitcast_fusion.1), channel_id=1, source_target_pairs={{0,64},{8,72},{16,80},{24,88},{32,96},{40,104},{48,112},{56,120},{... | collective-permute-start | bytes 98312 | tf_op jit(solution)/shard_map/ppermute | solution.py:515
  100.2 10.2 %head_corr.1 = f32[128,128]{1,0:T(8,128)S(1)} custom-call(bf16[8,256,128]{2,1,0:T(8,128)(2,1)S(1)} %get-tuple-element.31.cur_ref.prev_ref, bf16[8,256,128]{2,1,0:T(8,128)(2,1)S(1)} %get-tuple-element.31.cur_ref.prev_ref, bf16[128,128]{1,0:T(8,128)(2,1)S(1)} %collective-permute-done.5.edge_ref, ...), custom_call_target="tpu_custom_call" | custom-call | tf_op jit(solution)/shard_map/head_corr/pallas_call | solution.py:271
  110.5 4.3 %collective-permute-done.6 = f32[128,128]{1,0:T(8,128)} collective-permute-done((f32[128,128]{1,0:T(8,128)S(1)}, f32[128,128]{1,0:T(8,128)}, u32[]{:S(2)}, u32[]{:S(2)}) %collective-permute-start.6) | collective-permute-done | bytes 65568 | tf_op jit(solution)/shard_map/ppermute | solution.py:565
  117.5 4.1 %collective-permute-done.7.b_ref = f32[128,128]{1,0:T(8,128)S(1)} collective-permute-done((f32[128,128]{1,0:T(8,128)S(1)}, f32[128,128]{1,0:T(8,128)S(1)}, u32[]{:S(2)}, u32[]{:S(2)}) %collective-permute-start.7) | collective-permute-done | bytes 65568 | tf_op jit(solution)/shard_map/ppermute | solution.py:565
  132.2 10.4 %all_to_all.25.got_ref = f32[8,8,128]{2,1,0:T(8,128)S(1)} all-to-all(f32[8,8,128]{2,1,0:T(8,128)S(1)} %pad_maximum_fusion), channel_id=1, replica_groups={{0,8,16,24,32,40,48,56},{64,72,80,88,96,104,112,120},{128,136,144,152,1..., dimensions={0} | all-to-all | bytes 65536 | tf_op jit(solution)/shard_map/all_to_all | solution.py:511
  142.6 4.1 %all-to-all-start.3 = ((bf16[8,256,128]{2,1,0:T(8,128)(2,1)}), bf16[8,256,128]{2,1,0:T(8,128)(2,1)}, u32[]{:S(2)}, u32[]{:S(2)}) async-start(bf16[8,256,128]{2,1,0:T(8,128)(2,1)} %get-tuple-element.20.out_ref), calls=%async_computation.3 | async-start | bytes 1048576 | tf_op jit(solution)/shard_map/all_to_all | solution.py:511
  149.0 3.6 %collective-permute-done.1.edge_ref = bf16[128,128]{1,0:T(8,128)(2,1)S(1)} collective-permute-done((bf16[128,128]{1,0:T(8,128)(2,1)S(1)}, bf16[128,128]{1,0:T(8,128)(2,1)S(1)}, u32[]{:S(2)}, u32[]{:S(2)}) %collective-permute-start.1) | collective-permute-done | bytes 32800 | tf_op jit(solution)/shard_map/ppermute | solution.py:515
  152.6 12.0 %head_anti.1.mixed_grad_ref = f32[8,256,128]{2,1,0:T(8,128)} custom-call(bf16[8,768,128]{2,1,0:T(8,128)(2,1)S(1)} %all-to-all-done.cur_ref.next_ref.packed_ref.g_ref, bf16[8,768,128]{2,1,0:T(8,128)(2,1)S(1)} %all-to-all-done.cur_ref.next_ref.packed_ref.g_ref, bf16[128,128]{1,0:T(8,128)(2,1)S(1)} %collective-permute-done.1.edge_ref, ...), custom_call_target="tpu_custom_call" | custom-call | tf_op jit(solution)/shard_map/head_anti/pallas_call | solution.py:211
  164.7 10.5 %attn_bwd.1 = (bf16[8,768,128]{2,1,0:T(8,128)(2,1)}, f32[4,512,128]{2,1,0:T(8,128)S(1)}, bf16[4,512,128]{2,1,0:T(8,128)(2,1)S(1)}) custom-call(s32[8]{0:T(128)S(1)} %fusion.4.width_ref, bf16[8,768,128]{2,1,0:T(8,128)(2,1)S(1)} %all-to-all-done.cur_ref.next_ref.packed_ref.g_ref, bf16[4,512,128]{2,1,0:T(8,128)(2,1)} %collective-permute-done.kvh_ref, ...), custom_call_target="tpu_custom_call" | custom-call | tf_op jit(solution)/shard_map/attn_bwd/pallas_call | solution.py:476
  177.1 9.4 %collective-permute-done.2.back_ref = bf16[4,512,128]{2,1,0:T(8,128)(2,1)S(1)} collective-permute-done((bf16[4,512,128]{2,1,0:T(8,128)(2,1)S(1)}, bf16[4,512,128]{2,1,0:T(8,128)(2,1)S(1)}, u32[]{:S(2)}, u32[]{:S(2)}) %collective-permute-start.2) | collective-permute-done | bytes 524320 | tf_op jit(solution)/shard_map/ppermute | solution.py:515
  187.3 6.9 %all-to-all-start.2 = ((bf16[8,768,128]{2,1,0:T(8,128)(2,1)}), bf16[8,768,128]{2,1,0:T(8,128)(2,1)S(1)}, u32[]{:S(2)}, u32[]{:S(2)}) async-start(bf16[8,768,128]{2,1,0:T(8,128)(2,1)} %join.1), calls=%async_computation.2 | async-start | bytes 3145728 | tf_op jit(solution)/shard_map/all_to_all | solution.py:511
  194.2 4.8 %collective-permute-start.3 = (bf16[128,1024]{1,0:T(8,128)(2,1)S(1)}, bf16[128,1024]{1,0:T(8,128)(2,1)S(1)}, u32[]{:S(2)}, u32[]{:S(2)}) collective-permute-start(bf16[128,1024]{1,0:T(8,128)(2,1)S(1)} %slice.59), channel_id=1, source_target_pairs={{8,0},{16,8},{24,16},{32,24},{40,32},{48,40},{56,48},{64,56},{72,6... | collective-permute-start | bytes 786440 | tf_op jit(solution)/shard_map/ppermute | solution.py:515
  199.0 31.1 %collective-permute-done.3.edge_ref = bf16[128,1024]{1,0:T(8,128)(2,1)S(1)} collective-permute-done((bf16[128,1024]{1,0:T(8,128)(2,1)S(1)}, bf16[128,1024]{1,0:T(8,128)(2,1)S(1)}, u32[]{:S(2)}, u32[]{:S(2)}) %collective-permute-start.3) | collective-permute-done | bytes 262176 | tf_op jit(solution)/shard_map/ppermute | solution.py:515
  230.1 12.7 %anti.1.mixed_grad_ref = f32[256,1024]{1,0:T(8,128)} custom-call(bf16[256,1024]{1,0:T(8,128)(2,1)S(1)} %multiply_convert_fusion.refs_0_.g_ref, bf16[128,1024]{1,0:T(8,128)(2,1)S(1)} %collective-permute-done.3.edge_ref, bf16[128,1024]{1,0:T(8,128)(2,1)S(1)} %copy-done), custom_call_target="tpu_custom_call" | custom-call | tf_op jit(solution)/shard_map/anti/pallas_call | solution.py:154
  246.2 3.4 %collective-permute-start.4 = (bf16[128,1024]{1,0:T(8,128)(2,1)S(1)}, bf16[128,1024]{1,0:T(8,128)(2,1)S(1)}, u32[]{:S(2)}, u32[]{:S(2)}) collective-permute-start(bf16[128,1024]{1,0:T(8,128)(2,1)S(1)} %slice.49), channel_id=1, source_target_pairs={{0,8},{8,16},{16,24},{24,32},{32,40},{40,48},{48,56},{56,64},{64,7... | collective-permute-start | bytes 786440 | tf_op jit(solution)/shard_map/ppermute | solution.py:515
  250.2 6.4 %collective-permute-done.4.edge_ref = bf16[128,1024]{1,0:T(8,128)(2,1)S(1)} collective-permute-done((bf16[128,1024]{1,0:T(8,128)(2,1)S(1)}, bf16[128,1024]{1,0:T(8,128)(2,1)S(1)}, u32[]{:S(2)}, u32[]{:S(2)}) %collective-permute-start.4) | collective-permute-done | bytes 262176 | tf_op jit(solution)/shard_map/ppermute | solution.py:515
  257.3 7.5 %causal.2.refs_0_ = bf16[256,1024]{1,0:T(8,128)(2,1)} custom-call(bf16[256,1024]{1,0:T(8,128)(2,1)} %get-tuple-element.29.m_ref, bf16[128,1024]{1,0:T(8,128)(2,1)} %copy-done.6, bf16[128,1024]{1,0:T(8,128)(2,1)} %w_ref.5, bf16[256,1024]{1,0:T(8,128)(2,1)} %grad_ref.3), custom_call_target="tpu_custom_call" | custom-call | tf_op jit(solution)/shard_map/causal/pallas_call | solution.py:183
  264.8 7.5 %causal.3 = bf16[256,1024]{1,0:T(8,128)(2,1)} custom-call(bf16[256,1024]{1,0:T(8,128)(2,1)} %get-tuple-element.29.m_ref, bf16[128,1024]{1,0:T(8,128)(2,1)} %copy-done.6, bf16[128,1024]{1,0:T(8,128)(2,1)} %w_ref.5, bf16[256,1024]{1,0:T(8,128)(2,1)} %grad_ref.3, bf16[256,1024]{1,0:T(8,128)(2,1)} %causal.2.refs_0_), custom_call_target="tpu_custom_call", output_to_operand_aliasing={{}: (4, {})} | custom-call | tf_op jit(solution)/shard_map/causal/pallas_call | solution.py:183
  (66 shorter events, 32.7 us)
Async XLA Ops:
  0.6 1.5 copy-start.2
  0.6 1.5 copy-start.3
  3.6 8.6 %copy-start.1 = (bf16[256,1024]{1,0:T(8,128)(2,1)S(1)}, bf16[256,1024]{1,0:T(8,128)(2,1)}, u32[]{:S(2)}) copy-start(bf16[256,1024]{1,0:T(8,128)(2,1)} %key_ref.1) | copy-start | bytes 1572868
  3.6 8.6 %copy-start.4 = (bf16[256,1024]{1,0:T(8,128)(2,1)S(1)}, bf16[256,1024]{1,0:T(8,128)(2,1)}, u32[]{:S(2)}) copy-start(bf16[256,1024]{1,0:T(8,128)(2,1)} %refs_0_.1) | copy-start | bytes 1572868
  3.6 48.6 %all-to-all-start = ((bf16[8,768,128]{2,1,0:T(8,128)(2,1)}), bf16[8,768,128]{2,1,0:T(8,128)(2,1)S(1)}, u32[]{:S(2)}, u32[]{:S(2)}) async-start(bf16[8,768,128]{2,1,0:T(8,128)(2,1)} %pack.2), calls=%async_computation | async-start | bytes 3145728 | tf_op jit(solution)/shard_map/all_to_all | solution.py:511
  13.4 42.4 %copy-start.7 = (s32[8192]{0:T(1024)S(1)}, s32[8192]{0:T(1024)}, u32[]{:S(2)}) copy-start(s32[8192]{0:T(1024)} %param.15) | copy-start | bytes 98308
  52.2 32.7 %all-to-all-start.1 = ((bf16[8,512,128]{2,1,0:T(8,128)(2,1)}), bf16[8,512,128]{2,1,0:T(8,128)(2,1)S(1)}, u32[]{:S(2)}, u32[]{:S(2)}) async-start(bf16[8,512,128]{2,1,0:T(8,128)(2,1)} %pack.3), calls=%async_computation.1 | async-start | bytes 2097152 | tf_op jit(solution)/shard_map/all_to_all | solution.py:511
  57.4 27.5 %collective-permute-start = (bf16[4,512,128]{2,1,0:T(8,128)(2,1)}, bf16[4,512,128]{2,1,0:T(8,128)(2,1)}, u32[]{:S(2)}, u32[]{:S(2)}) collective-permute-start(bf16[4,512,128]{2,1,0:T(8,128)(2,1)} %slice.57), channel_id=1, source_target_pairs={{0,64},{8,72},{16,80},{24,88},{32,96},{40,104},{48,112},{56,120},{... | collective-permute-start | bytes 1572872 | tf_op jit(solution)/shard_map/ppermute | solution.py:515
  94.2 23.2 %copy-start = (bf16[128,1024]{1,0:T(8,128)(2,1)S(1)}, bf16[128,1024]{1,0:T(8,128)(2,1)}, u32[]{:S(2)}) copy-start(bf16[128,1024]{1,0:T(8,128)(2,1)} %w_ref.5) | copy-start | bytes 786436
  94.2 5.9 %collective-permute-start.5 = (bf16[128,128]{1,0:T(8,128)(2,1)S(1)}, bf16[128,128]{1,0:T(8,128)(2,1)S(1)}, u32[]{:S(2)}, u32[]{:S(2)}) collective-permute-start(bf16[128,128]{1,0:T(8,128)(2,1)S(1)} %slice_bitcast_fusion.1), channel_id=1, source_target_pairs={{0,64},{8,72},{16,80},{24,88},{32,96},{40,104},{48,112},{56,120},{... | collective-permute-start | bytes 98312 | tf_op jit(solution)/shard_map/ppermute | solution.py:515
  110.4 4.5 %collective-permute-start.6 = (f32[128,128]{1,0:T(8,128)S(1)}, f32[128,128]{1,0:T(8,128)}, u32[]{:S(2)}, u32[]{:S(2)}) collective-permute-start(f32[128,128]{1,0:T(8,128)S(1)} %head_corr.1), channel_id=1, source_target_pairs={{0,64},{8,72},{16,80},{24,88},{32,96},{40,104},{48,112},{56,120},{... | collective-permute-start | bytes 196616 | tf_op jit(solution)/shard_map/ppermute | solution.py:565
  115.7 5.8 %collective-permute-start.7 = (f32[128,128]{1,0:T(8,128)S(1)}, f32[128,128]{1,0:T(8,128)S(1)}, u32[]{:S(2)}, u32[]{:S(2)}) collective-permute-start(f32[128,128]{1,0:T(8,128)S(1)} %add.51.a_ref), channel_id=1, source_target_pairs={{0,128},{8,136},{16,144},{24,152},{32,160},{40,168},{48,176},{56,1... | collective-permute-start | bytes 196616 | tf_op jit(solution)/shard_map/ppermute | solution.py:565
  121.7 0.6 copy-start.5
  122.3 1.2 collective-permute-start.8
  123.5 3.6 %collective-permute-start.9 = (f32[8,128]{1,0:T(8,128)S(1)}, f32[8,128]{1,0:T(8,128)S(1)}, u32[]{:S(2)}, u32[]{:S(2)}) collective-permute-start(f32[8,128]{1,0:T(8,128)S(1)} %add.54), channel_id=1, source_target_pairs={{0,2},{1,3},{2,0},{3,1},{4,6},{5,7},{6,4},{7,5},{8,10},{9,11},{10,... | collective-permute-start | bytes 12296 | tf_op jit(solution)/shard_map/ppermute | solution.py:565
  127.1 5.1 %collective-permute-start.10 = (f32[8,128]{1,0:T(8,128)S(1)}, f32[8,128]{1,0:T(8,128)S(1)}, u32[]{:S(2)}, u32[]{:S(2)}) collective-permute-start(f32[8,128]{1,0:T(8,128)S(1)} %add.55), channel_id=1, source_target_pairs={{0,4},{1,5},{2,6},{3,7},{4,0},{5,1},{6,2},{7,3},{8,12},{9,13},{10,... | collective-permute-start | bytes 12296 | tf_op jit(solution)/shard_map/ppermute | solution.py:565
  142.6 44.7 %all-to-all-start.3 = ((bf16[8,256,128]{2,1,0:T(8,128)(2,1)}), bf16[8,256,128]{2,1,0:T(8,128)(2,1)}, u32[]{:S(2)}, u32[]{:S(2)}) async-start(bf16[8,256,128]{2,1,0:T(8,128)(2,1)} %get-tuple-element.20.out_ref), calls=%async_computation.3 | async-start | bytes 1048576 | tf_op jit(solution)/shard_map/all_to_all | solution.py:511
  146.8 5.8 %collective-permute-start.1 = (bf16[128,128]{1,0:T(8,128)(2,1)S(1)}, bf16[128,128]{1,0:T(8,128)(2,1)S(1)}, u32[]{:S(2)}, u32[]{:S(2)}) collective-permute-start(bf16[128,128]{1,0:T(8,128)(2,1)S(1)} %slice_bitcast_fusion), channel_id=1, source_target_pairs={{64,0},{72,8},{80,16},{88,24},{96,32},{104,40},{112,48},{120,56},{... | collective-permute-start | bytes 98312 | tf_op jit(solution)/shard_map/ppermute | solution.py:515
  175.2 11.3 %collective-permute-start.2 = (bf16[4,512,128]{2,1,0:T(8,128)(2,1)S(1)}, bf16[4,512,128]{2,1,0:T(8,128)(2,1)S(1)}, u32[]{:S(2)}, u32[]{:S(2)}) collective-permute-start(bf16[4,512,128]{2,1,0:T(8,128)(2,1)S(1)} %get-tuple-element.25), channel_id=1, source_target_pairs={{64,0},{72,8},{80,16},{88,24},{96,32},{104,40},{112,48},{120,56},{... | collective-permute-start | bytes 1572872 | tf_op jit(solution)/shard_map/ppermute | solution.py:515
  187.3 85.0 %all-to-all-start.2 = ((bf16[8,768,128]{2,1,0:T(8,128)(2,1)}), bf16[8,768,128]{2,1,0:T(8,128)(2,1)S(1)}, u32[]{:S(2)}, u32[]{:S(2)}) async-start(bf16[8,768,128]{2,1,0:T(8,128)(2,1)} %join.1), calls=%async_computation.2 | async-start | bytes 3145728 | tf_op jit(solution)/shard_map/all_to_all | solution.py:511
  194.2 36.0 %collective-permute-start.3 = (bf16[128,1024]{1,0:T(8,128)(2,1)S(1)}, bf16[128,1024]{1,0:T(8,128)(2,1)S(1)}, u32[]{:S(2)}, u32[]{:S(2)}) collective-permute-start(bf16[128,1024]{1,0:T(8,128)(2,1)S(1)} %slice.59), channel_id=1, source_target_pairs={{8,0},{16,8},{24,16},{32,24},{40,32},{48,40},{56,48},{64,56},{72,6... | collective-permute-start | bytes 786440 | tf_op jit(solution)/shard_map/ppermute | solution.py:515
  246.2 10.4 %collective-permute-start.4 = (bf16[128,1024]{1,0:T(8,128)(2,1)S(1)}, bf16[128,1024]{1,0:T(8,128)(2,1)S(1)}, u32[]{:S(2)}, u32[]{:S(2)}) collective-permute-start(bf16[128,1024]{1,0:T(8,128)(2,1)S(1)} %slice.49), channel_id=1, source_target_pairs={{0,8},{8,16},{16,24},{24,32},{32,40},{40,48},{48,56},{56,64},{64,7... | collective-permute-start | bytes 786440 | tf_op jit(solution)/shard_map/ppermute | solution.py:515
  256.6 0.7 copy-start.6

commit v7 on v6

--- a/solution.py
+++ b/solution.py
@@ -17,7 +17,7 @@
 GRANT = pltpu.CompilerParams(vmem_limit_bytes=8 << 20)
 STEP = 4
 SCALE = HD ** (-0.5)
-PIECES = 2
+PIECES = 4
 
 
 def hbm(*arrays):
@@ -65,7 +65,7 @@
     )(x)
 
 
-def finish_kernel(x_ref, key_ref, mixed_grad_ref, mixed_ref, branch_ref):
+def finish_kernel(x_ref, key_ref, mixed_grad_ref, mixed_ref, branch_ref, edge_ref):
     for head in range(x_ref.shape[0]):
         lanes = slice(head * HD, (head + 1) * HD)
         attn_out = x_ref[head].astype(jnp.float32)
@@ -73,6 +73,7 @@
             jnp.bfloat16
         )
         branch_ref[:, lanes] = (mixed_grad_ref[:, lanes] * attn_out).astype(jnp.bfloat16)
+    edge_ref[...] = mixed_ref[TOK - TAPS :]
 
 
 def finish(attn_out, key, mixed_grad):
@@ -83,8 +84,8 @@
         finish_kernel,
         grid=(heads // STEP,),
         in_specs=[pl.BlockSpec((STEP, TOK, HD), lambda h: (h, 0, 0)), column, column],
-        out_specs=[column] * 2,
-        out_shape=[shape] * 2,
+        out_specs=[column] * 2 + [pl.BlockSpec((TAPS, STEP * HD), lambda h: (0, h))],
+        out_shape=[shape] * 2 + [jax.ShapeDtypeStruct((TAPS, heads * HD), jnp.bfloat16)],
         compiler_params=GRANT,
         name="finish",
     )(attn_out, *hbm(key, mixed_grad))
@@ -287,7 +288,7 @@
         ],
         compiler_params=GRANT,
         name="head_corr",
-    )(mixed, mixed, edge, packed)
+    )(*hbm(mixed, mixed), edge, packed)
 
 
 def dot_nn(a, b):
@@ -454,7 +455,7 @@
             num_scalar_prefetch=1,
             grid=(1,),
             in_specs=[VMEM, whole(SPAN, 2 * TOK, HD), VMEM, VMEM],
-            out_specs=[whole(ROW, TOK, HD), VMEM, VMEM, VMEM],
+            out_specs=[whole(ROW, TOK, HD), whole(ROW, TOK, HD), VMEM, VMEM],
             scratch_shapes=[
                 pltpu.VMEM((KEYS, HD), jnp.bfloat16),
                 pltpu.VMEM((SPAN + ROW, HD, TOK), jnp.bfloat16),
@@ -462,7 +463,7 @@
         ),
         out_shape=[
             pltpu.HBM((ROW, TOK, HD), jnp.bfloat16),
-            jax.ShapeDtypeStruct((ROW, TOK, HD), jnp.bfloat16),
+            pltpu.HBM((ROW, TOK, HD), jnp.bfloat16),
             jax.ShapeDtypeStruct((ROW, 1, TOK), jnp.float32),
             jax.ShapeDtypeStruct((ROW, 1, TOK), jnp.float32),
         ],
@@ -550,8 +551,8 @@
     )
     back = shift(dkvh, -ROW)
     filter_part = head_corr(mixed_head, mixed_before, packed)
-    mixed, branch_grad = finish(attn_out, key_branch, mixed_grad)
-    mixed_edge = shift(mixed[TOK - TAPS :], 1)
+    mixed, branch_grad, last_rows = finish(attn_out, key_branch, mixed_grad)
+    mixed_edge = shift(last_rows, 1)
     key_grad, value_grad, query_grad = unpack(swap(join(joined, dkv_hi, back)))
     gate_grad = []
     for piece in range(PIECES):

time: 275 us -> 279 us (1.015)
  the two profiles are of different devices: /device:TPU:10 before, /device:TPU:18 now
where the time goes in v7:
time: 279 us; the launch traced here: 277 us
  waiting for transfers between devices  131 us (47%)
  Pallas kernels  82 us (29%)
  starting transfers between devices  45.6 us (16%)
  blocking collectives  10.4 us (4%)
  local copies, waits for them, and re-layouts  4.27 us (2%)
  other arithmetic  2.83 us (1%)
    all_to_all x4, waiting for transfers between devices, swap(): return lax.all_to_all(x, axis, 0, 0, axis_index_groups=groups, tiled=True)  62.6 us
    ppermute x6, waiting for transfers between devices, shift(): return lax.ppermute(x, 'seq', pairs)  52.9 us
    all_to_all x4, starting transfers between devices, swap(): return lax.all_to_all(x, axis, 0, 0, axis_index_groups=groups, tiled=True)  23.1 us
    ppermute x6, starting transfers between devices, shift(): return lax.ppermute(x, 'seq', pairs)  19 us
    pallas_call x4, Pallas kernels, causal_piece(): pl.pallas_call(causal_kernel, grid=(tiles,), in_specs=[column(TOK), colum...  18.1 us
    ppermute x5, waiting for transfers between devices, partner(): return lax.ppermute(x, axis, pairs)  16 us
    pallas_call x1, Pallas kernels, anti(): pl.pallas_call(anti_kernel, grid=(conv_grad.shape[1] // HD,), in_specs=[c...  12.7 us
    pallas_call x1, Pallas kernels, head_anti(): pl.pallas_call(head_anti_kernel, grid=(ROW,), in_specs=[pl.BlockSpec((1,...  12 us
  transfers between devices with their start and end apart: 15, of which 12 were waited for; matrix products, arithmetic and copies ran while one was open for 1% of the time, Pallas kernels for 21%

profile of v7, /device:TPU:18, one launch (start us, length us, event | category | flops | bytes accessed | tf_op | source)
XLA Modules:
  0.0 277.5 jit_solution(3688937794386584712)
XLA Ops:
  3.6 8.6 %all-to-all-start = ((bf16[8,768,128]{2,1,0:T(8,128)(2,1)}), bf16[8,768,128]{2,1,0:T(8,128)(2,1)S(1)}, u32[]{:S(2)}, u32[]{:S(2)}) async-start(bf16[8,768,128]{2,1,0:T(8,128)(2,1)} %pack.2), calls=%async_computation | async-start | bytes 3145728 | tf_op jit(solution)/shard_map/all_to_all | solution.py:512
  13.4 38.8 %all-to-all-done.cur_ref.next_ref.packed_ref.g_ref = bf16[8,768,128]{2,1,0:T(8,128)(2,1)S(1)} async-done(((bf16[8,768,128]{2,1,0:T(8,128)(2,1)}), bf16[8,768,128]{2,1,0:T(8,128)(2,1)S(1)}, u32[]{:S(2)}, u32[]{:S(2)}) %all-to-all-start) | async-done | bytes 1572896 | tf_op jit(solution)/shard_map/all_to_all | solution.py:512
  52.2 3.6 %all-to-all-start.1 = ((bf16[8,512,128]{2,1,0:T(8,128)(2,1)}), bf16[8,512,128]{2,1,0:T(8,128)(2,1)S(1)}, u32[]{:S(2)}, u32[]{:S(2)}) async-start(bf16[8,512,128]{2,1,0:T(8,128)(2,1)} %pack.3), calls=%async_computation.1 | async-start | bytes 2097152 | tf_op jit(solution)/shard_map/all_to_all | solution.py:512
  61.0 23.9 %all-to-all-done.1.qk_ref = bf16[8,512,128]{2,1,0:T(8,128)(2,1)S(1)} async-done(((bf16[8,512,128]{2,1,0:T(8,128)(2,1)}), bf16[8,512,128]{2,1,0:T(8,128)(2,1)S(1)}, u32[]{:S(2)}, u32[]{:S(2)}) %all-to-all-start.1) | async-done | bytes 1048608 | tf_op jit(solution)/shard_map/all_to_all | solution.py:512
  84.9 9.5 %attn_fwd.1 = (bf16[8,256,128]{2,1,0:T(8,128)(2,1)}, bf16[8,256,128]{2,1,0:T(8,128)(2,1)}, f32[8,1,256]{2,1,0:T(1,128)S(1)}, f32[8,1,256]{2,1,0:T(1,128)S(1)}) custom-call(s32[8]{0:T(128)S(1)} %fusion.4.width_ref, bf16[8,768,128]{2,1,0:T(8,128)(2,1)S(1)} %all-to-all-done.cur_ref.next_ref.packed_ref.g_ref, bf16[4,512,128]{2,1,0:T(8,128)(2,1)} %collective-permute-done.kvh_ref, ...), custom_call_target="tpu_custom_call" | custom-call | tf_op jit(solution)/shard_map/attn_fwd/pallas_call | solution.py:452
  101.0 11.2 %head_corr.1 = f32[128,128]{1,0:T(8,128)S(1)} custom-call(bf16[8,256,128]{2,1,0:T(8,128)(2,1)} %get-tuple-element.33.cur_ref.prev_ref, bf16[8,256,128]{2,1,0:T(8,128)(2,1)} %get-tuple-element.33.cur_ref.prev_ref, bf16[128,128]{1,0:T(8,128)(2,1)S(1)} %collective-permute-done.5.edge_ref, bf16[8,768,128]{2,1,0:T(8,128)(2,1)S(1)} %all-to-all-done.cur_ref.next_ref.packed_ref.g_ref), custom_call_target="tpu_custom_call" | custom-call | tf_op jit(solution)/shard_map/head_corr/pallas_call | solution.py:272
  112.3 4.3 %collective-permute-done.6 = f32[128,128]{1,0:T(8,128)} collective-permute-done((f32[128,128]{1,0:T(8,128)S(1)}, f32[128,128]{1,0:T(8,128)}, u32[]{:S(2)}, u32[]{:S(2)}) %collective-permute-start.6) | collective-permute-done | bytes 65568 | tf_op jit(solution)/shard_map/ppermute | solution.py:566
  119.3 4.1 %collective-permute-done.7.b_ref = f32[128,128]{1,0:T(8,128)S(1)} collective-permute-done((f32[128,128]{1,0:T(8,128)S(1)}, f32[128,128]{1,0:T(8,128)S(1)}, u32[]{:S(2)}, u32[]{:S(2)}) %collective-permute-start.7) | collective-permute-done | bytes 65568 | tf_op jit(solution)/shard_map/ppermute | solution.py:566
  130.0 4.1 %collective-permute-done.10 = f32[8,128]{1,0:T(8,128)S(1)} collective-permute-done((f32[8,128]{1,0:T(8,128)S(1)}, f32[8,128]{1,0:T(8,128)S(1)}, u32[]{:S(2)}, u32[]{:S(2)}) %collective-permute-start.10) | collective-permute-done | bytes 4128 | tf_op jit(solution)/shard_map/ppermute | solution.py:566
  134.1 10.4 %all_to_all.25.got_ref = f32[8,8,128]{2,1,0:T(8,128)S(1)} all-to-all(f32[8,8,128]{2,1,0:T(8,128)S(1)} %pad_maximum_fusion), channel_id=1, replica_groups={{0,8,16,24,32,40,48,56},{64,72,80,88,96,104,112,120},{128,136,144,152,1..., dimensions={0} | all-to-all | bytes 65536 | tf_op jit(solution)/shard_map/all_to_all | solution.py:512
  144.4 4.1 %all-to-all-start.3 = ((bf16[8,256,128]{2,1,0:T(8,128)(2,1)}), bf16[8,256,128]{2,1,0:T(8,128)(2,1)}, u32[]{:S(2)}, u32[]{:S(2)}) async-start(bf16[8,256,128]{2,1,0:T(8,128)(2,1)} %get-tuple-element.21.out_ref), calls=%async_computation.3 | async-start | bytes 1048576 | tf_op jit(solution)/shard_map/all_to_all | solution.py:512
  150.8 3.6 %collective-permute-done.1.edge_ref = bf16[128,128]{1,0:T(8,128)(2,1)S(1)} collective-permute-done((bf16[128,128]{1,0:T(8,128)(2,1)S(1)}, bf16[128,128]{1,0:T(8,128)(2,1)S(1)}, u32[]{:S(2)}, u32[]{:S(2)}) %collective-permute-start.1) | collective-permute-done | bytes 32800 | tf_op jit(solution)/shard_map/ppermute | solution.py:516
  154.4 12.0 %head_anti.1.mixed_grad_ref = f32[8,256,128]{2,1,0:T(8,128)} custom-call(bf16[8,768,128]{2,1,0:T(8,128)(2,1)S(1)} %all-to-all-done.cur_ref.next_ref.packed_ref.g_ref, bf16[8,768,128]{2,1,0:T(8,128)(2,1)S(1)} %all-to-all-done.cur_ref.next_ref.packed_ref.g_ref, bf16[128,128]{1,0:T(8,128)(2,1)S(1)} %collective-permute-done.1.edge_ref, ...), custom_call_target="tpu_custom_call" | custom-call | tf_op jit(solution)/shard_map/head_anti/pallas_call | solution.py:212
  166.5 10.5 %attn_bwd.1 = (bf16[8,768,128]{2,1,0:T(8,128)(2,1)}, f32[4,512,128]{2,1,0:T(8,128)S(1)}, bf16[4,512,128]{2,1,0:T(8,128)(2,1)S(1)}) custom-call(s32[8]{0:T(128)S(1)} %fusion.4.width_ref, bf16[8,768,128]{2,1,0:T(8,128)(2,1)S(1)} %all-to-all-done.cur_ref.next_ref.packed_ref.g_ref, bf16[4,512,128]{2,1,0:T(8,128)(2,1)} %collective-permute-done.kvh_ref, ...), custom_call_target="tpu_custom_call" | custom-call | tf_op jit(solution)/shard_map/attn_bwd/pallas_call | solution.py:477
  178.9 9.4 %collective-permute-done.2.back_ref = bf16[4,512,128]{2,1,0:T(8,128)(2,1)S(1)} collective-permute-done((bf16[4,512,128]{2,1,0:T(8,128)(2,1)S(1)}, bf16[4,512,128]{2,1,0:T(8,128)(2,1)S(1)}, u32[]{:S(2)}, u32[]{:S(2)}) %collective-permute-start.2) | collective-permute-done | bytes 524320 | tf_op jit(solution)/shard_map/ppermute | solution.py:516
  189.1 6.9 %all-to-all-start.2 = ((bf16[8,768,128]{2,1,0:T(8,128)(2,1)}), bf16[8,768,128]{2,1,0:T(8,128)(2,1)S(1)}, u32[]{:S(2)}, u32[]{:S(2)}) async-start(bf16[8,768,128]{2,1,0:T(8,128)(2,1)} %join.1), calls=%async_computation.2 | async-start | bytes 3145728 | tf_op jit(solution)/shard_map/all_to_all | solution.py:512
  196.0 4.8 %collective-permute-start.3 = (bf16[128,1024]{1,0:T(8,128)(2,1)S(1)}, bf16[128,1024]{1,0:T(8,128)(2,1)S(1)}, u32[]{:S(2)}, u32[]{:S(2)}) collective-permute-start(bf16[128,1024]{1,0:T(8,128)(2,1)S(1)} %slice.55), channel_id=1, source_target_pairs={{8,0},{16,8},{24,16},{32,24},{40,32},{48,40},{56,48},{64,56},{72,6... | collective-permute-start | bytes 786440 | tf_op jit(solution)/shard_map/ppermute | solution.py:516
  200.8 31.1 %collective-permute-done.3.edge_ref = bf16[128,1024]{1,0:T(8,128)(2,1)S(1)} collective-permute-done((bf16[128,1024]{1,0:T(8,128)(2,1)S(1)}, bf16[128,1024]{1,0:T(8,128)(2,1)S(1)}, u32[]{:S(2)}, u32[]{:S(2)}) %collective-permute-start.3) | collective-permute-done | bytes 262176 | tf_op jit(solution)/shard_map/ppermute | solution.py:516
  231.9 12.7 %anti.1.mixed_grad_ref = f32[256,1024]{1,0:T(8,128)} custom-call(bf16[256,1024]{1,0:T(8,128)(2,1)S(1)} %multiply_convert_fusion.refs_0_.g_ref, bf16[128,1024]{1,0:T(8,128)(2,1)S(1)} %collective-permute-done.3.edge_ref, bf16[128,1024]{1,0:T(8,128)(2,1)S(1)} %copy-done), custom_call_target="tpu_custom_call" | custom-call | tf_op jit(solution)/shard_map/anti/pallas_call | solution.py:155
  251.1 6.4 %collective-permute-done.4.edge_ref = bf16[128,1024]{1,0:T(8,128)(2,1)S(1)} collective-permute-done((bf16[128,1024]{1,0:T(8,128)(2,1)S(1)}, bf16[128,1024]{1,0:T(8,128)(2,1)S(1)}, u32[]{:S(2)}, u32[]{:S(2)}) %collective-permute-start.4) | collective-permute-done | bytes 262176 | tf_op jit(solution)/shard_map/ppermute | solution.py:516
  258.1 4.5 %causal.4.refs_0_ = bf16[256,1024]{1,0:T(8,128)(2,1)} custom-call(bf16[256,1024]{1,0:T(8,128)(2,1)} %get-tuple-element.30.m_ref, bf16[128,1024]{1,0:T(8,128)(2,1)} %copy-done.6, bf16[128,1024]{1,0:T(8,128)(2,1)} %w_ref.9, bf16[256,1024]{1,0:T(8,128)(2,1)} %grad_ref.7), custom_call_target="tpu_custom_call" | custom-call | tf_op jit(solution)/shard_map/causal/pallas_call | solution.py:184
  262.6 4.5 %causal.5.refs_0_ = bf16[256,1024]{1,0:T(8,128)(2,1)} custom-call(bf16[256,1024]{1,0:T(8,128)(2,1)} %get-tuple-element.30.m_ref, bf16[128,1024]{1,0:T(8,128)(2,1)} %copy-done.6, bf16[128,1024]{1,0:T(8,128)(2,1)} %w_ref.9, bf16[256,1024]{1,0:T(8,128)(2,1)} %grad_ref.7, bf16[256,1024]{1,0:T(8,128)(2,1)} %causal.4.refs_0_), custom_call_target="tpu_custom_call", output_to_operand_aliasing={{}: (4, {})} | custom-call | tf_op jit(solution)/shard_map/causal/pallas_call | solution.py:184
  267.2 4.5 %causal.6.refs_0_ = bf16[256,1024]{1,0:T(8,128)(2,1)} custom-call(bf16[256,1024]{1,0:T(8,128)(2,1)} %get-tuple-element.30.m_ref, bf16[128,1024]{1,0:T(8,128)(2,1)} %copy-done.6, bf16[128,1024]{1,0:T(8,128)(2,1)} %w_ref.9, bf16[256,1024]{1,0:T(8,128)(2,1)} %grad_ref.7, bf16[256,1024]{1,0:T(8,128)(2,1)} %causal.5.refs_0_), custom_call_target="tpu_custom_call", output_to_operand_aliasing={{}: (4, {})} | custom-call | tf_op jit(solution)/shard_map/causal/pallas_call | solution.py:184
  271.7 4.5 %causal.7 = bf16[256,1024]{1,0:T(8,128)(2,1)} custom-call(bf16[256,1024]{1,0:T(8,128)(2,1)} %get-tuple-element.30.m_ref, bf16[128,1024]{1,0:T(8,128)(2,1)} %copy-done.6, bf16[128,1024]{1,0:T(8,128)(2,1)} %w_ref.9, bf16[256,1024]{1,0:T(8,128)(2,1)} %grad_ref.7, bf16[256,1024]{1,0:T(8,128)(2,1)} %causal.6.refs_0_), custom_call_target="tpu_custom_call", output_to_operand_aliasing={{}: (4, {})} | custom-call | tf_op jit(solution)/shard_map/causal/pallas_call | solution.py:184
  (67 shorter events, 38.6 us)
Async XLA Ops:
  0.6 1.5 copy-start.2
  0.6 1.5 copy-start.3
  3.6 8.6 %copy-start.1 = (bf16[256,1024]{1,0:T(8,128)(2,1)S(1)}, bf16[256,1024]{1,0:T(8,128)(2,1)}, u32[]{:S(2)}) copy-start(bf16[256,1024]{1,0:T(8,128)(2,1)} %key_ref.1) | copy-start | bytes 1572868
  3.6 8.6 %copy-start.4 = (bf16[256,1024]{1,0:T(8,128)(2,1)S(1)}, bf16[256,1024]{1,0:T(8,128)(2,1)}, u32[]{:S(2)}) copy-start(bf16[256,1024]{1,0:T(8,128)(2,1)} %refs_0_.1) | copy-start | bytes 1572868
  3.6 48.6 %all-to-all-start = ((bf16[8,768,128]{2,1,0:T(8,128)(2,1)}), bf16[8,768,128]{2,1,0:T(8,128)(2,1)S(1)}, u32[]{:S(2)}, u32[]{:S(2)}) async-start(bf16[8,768,128]{2,1,0:T(8,128)(2,1)} %pack.2), calls=%async_computation | async-start | bytes 3145728 | tf_op jit(solution)/shard_map/all_to_all | solution.py:512
  13.4 42.4 %copy-start.7 = (s32[8192]{0:T(1024)S(1)}, s32[8192]{0:T(1024)}, u32[]{:S(2)}) copy-start(s32[8192]{0:T(1024)} %param.15) | copy-start | bytes 98308
  52.2 32.7 %all-to-all-start.1 = ((bf16[8,512,128]{2,1,0:T(8,128)(2,1)}), bf16[8,512,128]{2,1,0:T(8,128)(2,1)S(1)}, u32[]{:S(2)}, u32[]{:S(2)}) async-start(bf16[8,512,128]{2,1,0:T(8,128)(2,1)} %pack.3), calls=%async_computation.1 | async-start | bytes 2097152 | tf_op jit(solution)/shard_map/all_to_all | solution.py:512
  57.4 27.5 %collective-permute-start = (bf16[4,512,128]{2,1,0:T(8,128)(2,1)}, bf16[4,512,128]{2,1,0:T(8,128)(2,1)}, u32[]{:S(2)}, u32[]{:S(2)}) collective-permute-start(bf16[4,512,128]{2,1,0:T(8,128)(2,1)} %slice.53), channel_id=1, source_target_pairs={{0,64},{8,72},{16,80},{24,88},{32,96},{40,104},{48,112},{56,120},{... | collective-permute-start | bytes 1572872 | tf_op jit(solution)/shard_map/ppermute | solution.py:516
  94.4 24.9 %copy-start = (bf16[128,1024]{1,0:T(8,128)(2,1)S(1)}, bf16[128,1024]{1,0:T(8,128)(2,1)}, u32[]{:S(2)}) copy-start(bf16[128,1024]{1,0:T(8,128)(2,1)} %w_ref.9) | copy-start | bytes 786436
  95.2 5.8 %collective-permute-start.5 = (bf16[128,128]{1,0:T(8,128)(2,1)S(1)}, bf16[128,128]{1,0:T(8,128)(2,1)S(1)}, u32[]{:S(2)}, u32[]{:S(2)}) collective-permute-start(bf16[128,128]{1,0:T(8,128)(2,1)S(1)} %slice_bitcast_fusion.1), channel_id=1, source_target_pairs={{0,64},{8,72},{16,80},{24,88},{32,96},{40,104},{48,112},{56,120},{... | collective-permute-start | bytes 98312 | tf_op jit(solution)/shard_map/ppermute | solution.py:516
  112.2 4.5 %collective-permute-start.6 = (f32[128,128]{1,0:T(8,128)S(1)}, f32[128,128]{1,0:T(8,128)}, u32[]{:S(2)}, u32[]{:S(2)}) collective-permute-start(f32[128,128]{1,0:T(8,128)S(1)} %head_corr.1), channel_id=1, source_target_pairs={{0,64},{8,72},{16,80},{24,88},{32,96},{40,104},{48,112},{56,120},{... | collective-permute-start | bytes 196616 | tf_op jit(solution)/shard_map/ppermute | solution.py:566
  117.5 5.8 %collective-permute-start.7 = (f32[128,128]{1,0:T(8,128)S(1)}, f32[128,128]{1,0:T(8,128)S(1)}, u32[]{:S(2)}, u32[]{:S(2)}) collective-permute-start(f32[128,128]{1,0:T(8,128)S(1)} %add.51.a_ref), channel_id=1, source_target_pairs={{0,128},{8,136},{16,144},{24,152},{32,160},{40,168},{48,176},{56,1... | collective-permute-start | bytes 196616 | tf_op jit(solution)/shard_map/ppermute | solution.py:566
  123.5 0.6 copy-start.5
  124.1 1.2 collective-permute-start.8
  125.3 3.6 %collective-permute-start.9 = (f32[8,128]{1,0:T(8,128)S(1)}, f32[8,128]{1,0:T(8,128)S(1)}, u32[]{:S(2)}, u32[]{:S(2)}) collective-permute-start(f32[8,128]{1,0:T(8,128)S(1)} %add.54), channel_id=1, source_target_pairs={{0,2},{1,3},{2,0},{3,1},{4,6},{5,7},{6,4},{7,5},{8,10},{9,11},{10,... | collective-permute-start | bytes 12296 | tf_op jit(solution)/shard_map/ppermute | solution.py:566
  128.9 5.1 %collective-permute-start.10 = (f32[8,128]{1,0:T(8,128)S(1)}, f32[8,128]{1,0:T(8,128)S(1)}, u32[]{:S(2)}, u32[]{:S(2)}) collective-permute-start(f32[8,128]{1,0:T(8,128)S(1)} %add.55), channel_id=1, source_target_pairs={{0,4},{1,5},{2,6},{3,7},{4,0},{5,1},{6,2},{7,3},{8,12},{9,13},{10,... | collective-permute-start | bytes 12296 | tf_op jit(solution)/shard_map/ppermute | solution.py:566
  144.4 44.7 %all-to-all-start.3 = ((bf16[8,256,128]{2,1,0:T(8,128)(2,1)}), bf16[8,256,128]{2,1,0:T(8,128)(2,1)}, u32[]{:S(2)}, u32[]{:S(2)}) async-start(bf16[8,256,128]{2,1,0:T(8,128)(2,1)} %get-tuple-element.21.out_ref), calls=%async_computation.3 | async-start | bytes 1048576 | tf_op jit(solution)/shard_map/all_to_all | solution.py:512
  148.6 5.8 %collective-permute-start.1 = (bf16[128,128]{1,0:T(8,128)(2,1)S(1)}, bf16[128,128]{1,0:T(8,128)(2,1)S(1)}, u32[]{:S(2)}, u32[]{:S(2)}) collective-permute-start(bf16[128,128]{1,0:T(8,128)(2,1)S(1)} %slice_bitcast_fusion), channel_id=1, source_target_pairs={{64,0},{72,8},{80,16},{88,24},{96,32},{104,40},{112,48},{120,56},{... | collective-permute-start | bytes 98312 | tf_op jit(solution)/shard_map/ppermute | solution.py:516
  177.0 11.3 %collective-permute-start.2 = (bf16[4,512,128]{2,1,0:T(8,128)(2,1)S(1)}, bf16[4,512,128]{2,1,0:T(8,128)(2,1)S(1)}, u32[]{:S(2)}, u32[]{:S(2)}) collective-permute-start(bf16[4,512,128]{2,1,0:T(8,128)(2,1)S(1)} %get-tuple-element.26), channel_id=1, source_target_pairs={{64,0},{72,8},{80,16},{88,24},{96,32},{104,40},{112,48},{120,56},{... | collective-permute-start | bytes 1572872 | tf_op jit(solution)/shard_map/ppermute | solution.py:516
  189.1 87.1 %all-to-all-start.2 = ((bf16[8,768,128]{2,1,0:T(8,128)(2,1)}), bf16[8,768,128]{2,1,0:T(8,128)(2,1)S(1)}, u32[]{:S(2)}, u32[]{:S(2)}) async-start(bf16[8,768,128]{2,1,0:T(8,128)(2,1)} %join.1), calls=%async_computation.2 | async-start | bytes 3145728 | tf_op jit(solution)/shard_map/all_to_all | solution.py:512
  196.0 36.0 %collective-permute-start.3 = (bf16[128,1024]{1,0:T(8,128)(2,1)S(1)}, bf16[128,1024]{1,0:T(8,128)(2,1)S(1)}, u32[]{:S(2)}, u32[]{:S(2)}) collective-permute-start(bf16[128,1024]{1,0:T(8,128)(2,1)S(1)} %slice.55), channel_id=1, source_target_pairs={{8,0},{16,8},{24,16},{32,24},{40,32},{48,40},{56,48},{64,56},{72,6... | collective-permute-start | bytes 786440 | tf_op jit(solution)/shard_map/ppermute | solution.py:516
  247.1 10.4 %collective-permute-start.4 = (bf16[128,1024]{1,0:T(8,128)(2,1)S(1)}, bf16[128,1024]{1,0:T(8,128)(2,1)S(1)}, u32[]{:S(2)}, u32[]{:S(2)}) collective-permute-start(bf16[128,1024]{1,0:T(8,128)(2,1)S(1)} %get-tuple-element.31), channel_id=1, source_target_pairs={{0,8},{8,16},{16,24},{24,32},{32,40},{40,48},{48,56},{56,64},{64,7... | collective-permute-start | bytes 786440 | tf_op jit(solution)/shard_map/ppermute | solution.py:516
  257.4 0.7 copy-start.6
